TPU v7x, 512 devices: a whole 4x4x16 slice. The times are simulated.
512 devices in a mesh: region: 64 (over z, y_hi, core), tracer: 8 (over x, y_lo).
Axes of the slice: x: 4, y: 4 (y_hi: 2, y_lo: 2; y = y_hi * 2 + y_lo), z: 16, core: 2. Of those that a mesh axis runs over, the one named last changes fastest.
Arguments:
- cotangent: float32 [32, 32768], P('tracer', 'region'), may hold values from -6 to 6
- states: float32 [6, 32, 32768], P(None, 'tracer', 'region'), may hold values from -6 to 6
- implicit_inverse: float32 [1024, 32, 32], P('region'), may hold values from -3 to 3
- wet_levels: int32 [1024], P('region'), may hold values from 1 to 32
- explicit_tiles: bfloat16 [64, 5, 512, 512], P('region'), may hold values from -0.125 to 0.125
- tile_offset: int32 [64, 5], P('region'), may hold values from -2 to 2, as said below
- tile_count: int32 [64], P('region'), may hold values from 1 to 5
- uptake_weight: float32 [32, 32], replicated, may hold values from -1 to 1
- release_weight: float32 [32, 32], replicated, may hold values from -1 to 1
Outputs:
- initial_adjoint: float32 [32, 32768], P('tracer', 'region')
Inputs may be any that keep to these rules, and one draw needn't show every extreme that they name: `tile_offset`: the offsets of one region are distinct; only the first tile_count slots of a region are used.
All inputs are finite; a program needn't handle non-finite values.
Results may differ from a plain program's by a relative error of at most 0.0032.
Values sent between devices are 32-bit elements; how exact they have to be, the bound alone decides.
No kernel may reach another device: no remote copies, remote signals or barrier semaphores. Data moves between devices by JAX's collectives and lax.ppermute only.
A program may use at most 64 MiB of HBM per device.

v0:
```python
import jax
import jax.numpy as jnp
from jax import lax
from jax.sharding import PartitionSpec as P

REACH = 2


def from_behind(block, axis, distance):
    devices = range(lax.axis_size(axis))
    route = [((i - distance) % len(devices), i) for i in devices]
    return lax.ppermute(block, axis, route)


def from_everyone(value, axis):
    copies = jnp.broadcast_to(value, (lax.axis_size(axis), *value.shape))
    return lax.all_to_all(copies, axis, split_axis=0, concat_axis=0, tiled=True)


def in_order(pieces, dim):
    pieces = jnp.moveaxis(pieces, 0, dim)
    lengths = pieces.shape
    return pieces.reshape(*lengths[:dim], lengths[dim] * lengths[dim + 1], *lengths[dim + 2 :])


def collect(value, axis, dim):
    pieces = from_everyone(value, axis)
    return in_order(pieces, dim)


def in_one_piece(arrays, axis, dim, along):
    ends, at = ([], 0)
    for a in arrays[:-1]:
        at += a.shape[along]
        ends.append(at)
    both = jnp.concatenate(arrays, axis=along)
    return tuple(jnp.split(collect(both, axis, dim), ends, axis=along))


def reaction_terms(full_state, full_settled, uptake_weight, release_weight):
    highest = lax.Precision.HIGHEST
    uptake = jnp.dot(uptake_weight, full_state, precision=highest)
    pushed = jnp.dot(release_weight.T, full_settled, precision=highest)
    return (1.0 - jnp.tanh(uptake) ** 2) * pushed


def at_distance(offsets, tile_terms, distance):
    select = (offsets == distance).astype(jnp.float32)
    return jnp.sum(select[:, None, None] * tile_terms, axis=0)


def local(
    cotangent,
    states,
    implicit_inverse,
    wet_levels,
    explicit_tiles,
    tile_offset,
    tile_count,
    uptake_weight,
    release_weight,
):
    highest = lax.Precision.HIGHEST
    tr_dev, boxes = cotangent.shape
    columns, levels, _ = implicit_inverse.shape
    wet_mask = (
        (lax.broadcasted_iota(jnp.int32, (columns, levels), 1) < wet_levels[:, None])
        .astype(jnp.float32)
        .reshape(1, boxes)
    )
    tile_block = explicit_tiles[0]
    offsets = tile_offset[0]
    used_tiles = tile_count[0]
    slot_total = tile_block.shape[0]
    live_slots = (jnp.arange(slot_total, dtype=jnp.int32) < used_tiles).astype(jnp.float32)
    tracer_index = lax.axis_index("tracer")
    adjoint = cotangent
    for section in range(states.shape[0] - 1, -1, -1):
        settled = (
            jnp.einsum(
                "tcm,cml->tcl",
                adjoint.reshape(tr_dev, columns, levels),
                implicit_inverse,
                precision=highest,
            ).reshape(tr_dev, boxes)
            * wet_mask
        )
        settled_half = settled.astype(jnp.bfloat16)
        tile_terms = (
            jnp.einsum("tb,kbc->ktc", settled_half, tile_block, preferred_element_type=jnp.float32)
            * live_slots[:, None, None]
        )
        inflow = at_distance(offsets, tile_terms, 0)
        for offset in range(-REACH, REACH + 1):
            if offset != 0:
                outgoing = at_distance(offsets, tile_terms, offset)
                inflow = inflow + from_behind(outgoing, "region", offset)
        state = states[section]
        full_state, full_settled = in_one_piece((state, settled), "tracer", 0, 1)
        weighted = reaction_terms(full_state, full_settled, uptake_weight, release_weight)
        own_rows = lax.dynamic_slice_in_dim(uptake_weight, tracer_index * tr_dev, tr_dev, 1)
        reacted = jnp.dot(own_rows.T, weighted, precision=highest)
        adjoint = wet_mask * (inflow + reacted)
    return adjoint


def solution(mesh):
    placed = (
        P("tracer", "region"),
        P(None, "tracer", "region"),
        P("region", None, None),
        P("region"),
        P("region", None, None, None),
        P("region", None),
        P("region"),
        P(),
        P(),
    )
    return jax.shard_map(
        local, mesh=mesh, in_specs=placed, out_specs=P("tracer", "region"), check_vma=False
    )
```

profile of v0, /device:TPU:1, one launch (start us, length us, event | category | flops | bytes accessed | tf_op | source)
XLA Modules:
  0.0 170.9 jit_solution(17779524703087378968)
XLA Ops:
  0.0 0.9 fusion.72
  0.9 0.8 reshape.164
  1.7 1.4 multiply_convert_fusion.5
  3.2 0.8 slice_bitcast_fusion
  4.0 0.7 broadcast_in_dim.12
  4.7 5.9 %all-to-all-start = ((f32[8,4,1024]{2,1,0:T(4,128)}), f32[8,4,1024]{2,1,0:T(4,128)S(1)}, u32[]{:S(2)}, u32[]{:S(2)}) async-start(f32[8,4,1024]{2,1,0:T(4,128)} %broadcast_in_dim.12), calls=%async_computation | async-start | bytes 262144 | tf_op jit(solution)/shard_map/all_to_all | solution.py:17
  10.5 0.7 fusion.73
  12.4 13.5 %collective-permute-start = (f32[4,512]{1,0:T(4,128)S(1)}, f32[4,512]{1,0:T(4,128)S(1)}, u32[]{:S(2)}, u32[]{:S(2)}) collective-permute-start(f32[4,512]{1,0:T(4,128)S(1)} %get-tuple-element.30), channel_id=1, source_target_pairs={{16,0},{24,8},{32,16},{40,24},{48,32},{56,40},{64,48},{72,56},{80,... | collective-permute-start | bytes 24584 | tf_op jit(solution)/shard_map/ppermute | solution.py:12
  25.9 3.1 %collective-permute-start.1 = (f32[4,512]{1,0:T(4,128)S(1)}, f32[4,512]{1,0:T(4,128)S(1)}, u32[]{:S(2)}, u32[]{:S(2)}) collective-permute-start(f32[4,512]{1,0:T(4,128)S(1)} %get-tuple-element.33), channel_id=1, source_target_pairs={{8,0},{16,8},{24,16},{32,24},{40,32},{48,40},{56,48},{64,56},{72,6... | collective-permute-start | bytes 24584 | tf_op jit(solution)/shard_map/ppermute | solution.py:12
  29.1 3.9 %collective-permute-start.2 = (f32[4,512]{1,0:T(4,128)S(1)}, f32[4,512]{1,0:T(4,128)S(1)}, u32[]{:S(2)}, u32[]{:S(2)}) collective-permute-start(f32[4,512]{1,0:T(4,128)S(1)} %get-tuple-element.32), channel_id=1, source_target_pairs={{504,0},{0,8},{8,16},{16,24},{24,32},{32,40},{40,48},{48,56},{56,6... | collective-permute-start | bytes 24584 | tf_op jit(solution)/shard_map/ppermute | solution.py:12
  33.0 1.9 %collective-permute-start.3 = (f32[4,512]{1,0:T(4,128)S(1)}, f32[4,512]{1,0:T(4,128)S(1)}, u32[]{:S(2)}, u32[]{:S(2)}) collective-permute-start(f32[4,512]{1,0:T(4,128)S(1)} %get-tuple-element.31), channel_id=1, source_target_pairs={{496,0},{504,8},{0,16},{8,24},{16,32},{24,40},{32,48},{40,56},{48,... | collective-permute-start | bytes 24584 | tf_op jit(solution)/shard_map/ppermute | solution.py:12
  36.3 4.7 %collective-permute-done.3 = f32[4,512]{1,0:T(4,128)S(1)} collective-permute-done((f32[4,512]{1,0:T(4,128)S(1)}, f32[4,512]{1,0:T(4,128)S(1)}, u32[]{:S(2)}, u32[]{:S(2)}) %collective-permute-start.3) | collective-permute-done | bytes 8224 | tf_op jit(solution)/shard_map/ppermute | solution.py:12
  42.0 0.7 broadcast_in_dim.13
  42.6 4.5 %all-to-all-start.1 = ((f32[8,4,1024]{2,1,0:T(4,128)}), f32[8,4,1024]{2,1,0:T(4,128)S(1)}, u32[]{:S(2)}, u32[]{:S(2)}) async-start(f32[8,4,1024]{2,1,0:T(4,128)} %broadcast_in_dim.13), calls=%async_computation.1 | async-start | bytes 262144 | tf_op jit(solution)/shard_map/all_to_all | solution.py:17
  47.7 3.6 %collective-permute-start.4 = (f32[4,512]{1,0:T(4,128)S(1)}, f32[4,512]{1,0:T(4,128)S(1)}, u32[]{:S(2)}, u32[]{:S(2)}) collective-permute-start(f32[4,512]{1,0:T(4,128)S(1)} %get-tuple-element.25), channel_id=1, source_target_pairs={{16,0},{24,8},{32,16},{40,24},{48,32},{56,40},{64,48},{72,56},{80,... | collective-permute-start | bytes 24584 | tf_op jit(solution)/shard_map/ppermute | solution.py:12
  51.4 1.9 %collective-permute-start.5 = (f32[4,512]{1,0:T(4,128)S(1)}, f32[4,512]{1,0:T(4,128)S(1)}, u32[]{:S(2)}, u32[]{:S(2)}) collective-permute-start(f32[4,512]{1,0:T(4,128)S(1)} %get-tuple-element.28), channel_id=1, source_target_pairs={{8,0},{16,8},{24,16},{32,24},{40,32},{48,40},{56,48},{64,56},{72,6... | collective-permute-start | bytes 24584 | tf_op jit(solution)/shard_map/ppermute | solution.py:12
  53.3 5.1 %collective-permute-start.6 = (f32[4,512]{1,0:T(4,128)S(1)}, f32[4,512]{1,0:T(4,128)S(1)}, u32[]{:S(2)}, u32[]{:S(2)}) collective-permute-start(f32[4,512]{1,0:T(4,128)S(1)} %get-tuple-element.27), channel_id=1, source_target_pairs={{504,0},{0,8},{8,16},{16,24},{24,32},{32,40},{40,48},{48,56},{56,6... | collective-permute-start | bytes 24584 | tf_op jit(solution)/shard_map/ppermute | solution.py:12
  58.5 4.0 %collective-permute-start.7 = (f32[4,512]{1,0:T(4,128)S(1)}, f32[4,512]{1,0:T(4,128)S(1)}, u32[]{:S(2)}, u32[]{:S(2)}) collective-permute-start(f32[4,512]{1,0:T(4,128)S(1)} %get-tuple-element.26), channel_id=1, source_target_pairs={{496,0},{504,8},{0,16},{8,24},{16,32},{24,40},{32,48},{40,56},{48,... | collective-permute-start | bytes 24584 | tf_op jit(solution)/shard_map/ppermute | solution.py:12
  63.8 2.6 %collective-permute-done.7 = f32[4,512]{1,0:T(4,128)S(1)} collective-permute-done((f32[4,512]{1,0:T(4,128)S(1)}, f32[4,512]{1,0:T(4,128)S(1)}, u32[]{:S(2)}, u32[]{:S(2)}) %collective-permute-start.7) | collective-permute-done | bytes 8224 | tf_op jit(solution)/shard_map/ppermute | solution.py:12
  67.5 0.7 broadcast_in_dim.14
  68.1 4.5 %all-to-all-start.2 = ((f32[8,4,1024]{2,1,0:T(4,128)}), f32[8,4,1024]{2,1,0:T(4,128)S(1)}, u32[]{:S(2)}, u32[]{:S(2)}) async-start(f32[8,4,1024]{2,1,0:T(4,128)} %broadcast_in_dim.14), calls=%async_computation.2 | async-start | bytes 262144 | tf_op jit(solution)/shard_map/all_to_all | solution.py:17
  73.2 1.9 %collective-permute-start.10 = (f32[4,512]{1,0:T(4,128)S(1)}, f32[4,512]{1,0:T(4,128)S(1)}, u32[]{:S(2)}, u32[]{:S(2)}) collective-permute-start(f32[4,512]{1,0:T(4,128)S(1)} %get-tuple-element.22), channel_id=1, source_target_pairs={{504,0},{0,8},{8,16},{16,24},{24,32},{32,40},{40,48},{48,56},{56,6... | collective-permute-start | bytes 24584 | tf_op jit(solution)/shard_map/ppermute | solution.py:12
  75.2 4.9 %collective-permute-start.11 = (f32[4,512]{1,0:T(4,128)S(1)}, f32[4,512]{1,0:T(4,128)S(1)}, u32[]{:S(2)}, u32[]{:S(2)}) collective-permute-start(f32[4,512]{1,0:T(4,128)S(1)} %get-tuple-element.21), channel_id=1, source_target_pairs={{496,0},{504,8},{0,16},{8,24},{16,32},{24,40},{32,48},{40,56},{48,... | collective-permute-start | bytes 24584 | tf_op jit(solution)/shard_map/ppermute | solution.py:12
  80.0 4.0 %collective-permute-start.8 = (f32[4,512]{1,0:T(4,128)S(1)}, f32[4,512]{1,0:T(4,128)S(1)}, u32[]{:S(2)}, u32[]{:S(2)}) collective-permute-start(f32[4,512]{1,0:T(4,128)S(1)} %get-tuple-element.20), channel_id=1, source_target_pairs={{16,0},{24,8},{32,16},{40,24},{48,32},{56,40},{64,48},{72,56},{80,... | collective-permute-start | bytes 24584 | tf_op jit(solution)/shard_map/ppermute | solution.py:12
  84.1 3.0 %collective-permute-start.9 = (f32[4,512]{1,0:T(4,128)S(1)}, f32[4,512]{1,0:T(4,128)S(1)}, u32[]{:S(2)}, u32[]{:S(2)}) collective-permute-start(f32[4,512]{1,0:T(4,128)S(1)} %get-tuple-element.23), channel_id=1, source_target_pairs={{8,0},{16,8},{24,16},{32,24},{40,32},{48,40},{56,48},{64,56},{72,6... | collective-permute-start | bytes 24584 | tf_op jit(solution)/shard_map/ppermute | solution.py:12
  88.4 2.2 %collective-permute-done.9 = f32[4,512]{1,0:T(4,128)S(1)} collective-permute-done((f32[4,512]{1,0:T(4,128)S(1)}, f32[4,512]{1,0:T(4,128)S(1)}, u32[]{:S(2)}, u32[]{:S(2)}) %collective-permute-start.9) | collective-permute-done | bytes 8224 | tf_op jit(solution)/shard_map/ppermute | solution.py:12
  91.5 0.7 broadcast_in_dim.15
  92.2 5.1 %all-to-all-start.3 = ((f32[8,4,1024]{2,1,0:T(4,128)}), f32[8,4,1024]{2,1,0:T(4,128)S(1)}, u32[]{:S(2)}, u32[]{:S(2)}) async-start(f32[8,4,1024]{2,1,0:T(4,128)} %broadcast_in_dim.15), calls=%async_computation.3 | async-start | bytes 262144 | tf_op jit(solution)/shard_map/all_to_all | solution.py:17
  97.9 7.4 %collective-permute-start.12 = (f32[4,512]{1,0:T(4,128)S(1)}, f32[4,512]{1,0:T(4,128)S(1)}, u32[]{:S(2)}, u32[]{:S(2)}) collective-permute-start(f32[4,512]{1,0:T(4,128)S(1)} %get-tuple-element.15), channel_id=1, source_target_pairs={{16,0},{24,8},{32,16},{40,24},{48,32},{56,40},{64,48},{72,56},{80,... | collective-permute-start | bytes 24584 | tf_op jit(solution)/shard_map/ppermute | solution.py:12
  105.3 1.9 %collective-permute-start.13 = (f32[4,512]{1,0:T(4,128)S(1)}, f32[4,512]{1,0:T(4,128)S(1)}, u32[]{:S(2)}, u32[]{:S(2)}) collective-permute-start(f32[4,512]{1,0:T(4,128)S(1)} %get-tuple-element.18), channel_id=1, source_target_pairs={{8,0},{16,8},{24,16},{32,24},{40,32},{48,40},{56,48},{64,56},{72,6... | collective-permute-start | bytes 24584 | tf_op jit(solution)/shard_map/ppermute | solution.py:12
  107.2 5.1 %collective-permute-start.14 = (f32[4,512]{1,0:T(4,128)S(1)}, f32[4,512]{1,0:T(4,128)S(1)}, u32[]{:S(2)}, u32[]{:S(2)}) collective-permute-start(f32[4,512]{1,0:T(4,128)S(1)} %get-tuple-element.17), channel_id=1, source_target_pairs={{504,0},{0,8},{8,16},{16,24},{24,32},{32,40},{40,48},{48,56},{56,6... | collective-permute-start | bytes 24584 | tf_op jit(solution)/shard_map/ppermute | solution.py:12
  112.4 1.9 %collective-permute-start.15 = (f32[4,512]{1,0:T(4,128)S(1)}, f32[4,512]{1,0:T(4,128)S(1)}, u32[]{:S(2)}, u32[]{:S(2)}) collective-permute-start(f32[4,512]{1,0:T(4,128)S(1)} %get-tuple-element.16), channel_id=1, source_target_pairs={{496,0},{504,8},{0,16},{8,24},{16,32},{24,40},{32,48},{40,56},{48,... | collective-permute-start | bytes 24584 | tf_op jit(solution)/shard_map/ppermute | solution.py:12
  115.6 4.8 %collective-permute-done.15 = f32[4,512]{1,0:T(4,128)S(1)} collective-permute-done((f32[4,512]{1,0:T(4,128)S(1)}, f32[4,512]{1,0:T(4,128)S(1)}, u32[]{:S(2)}, u32[]{:S(2)}) %collective-permute-start.15) | collective-permute-done | bytes 8224 | tf_op jit(solution)/shard_map/ppermute | solution.py:12
  121.3 0.7 broadcast_in_dim.16
  122.0 4.5 %all-to-all-start.4 = ((f32[8,4,1024]{2,1,0:T(4,128)}), f32[8,4,1024]{2,1,0:T(4,128)S(1)}, u32[]{:S(2)}, u32[]{:S(2)}) async-start(f32[8,4,1024]{2,1,0:T(4,128)} %broadcast_in_dim.16), calls=%async_computation.4 | async-start | bytes 262144 | tf_op jit(solution)/shard_map/all_to_all | solution.py:17
  127.1 2.8 %collective-permute-start.16 = (f32[4,512]{1,0:T(4,128)S(1)}, f32[4,512]{1,0:T(4,128)S(1)}, u32[]{:S(2)}, u32[]{:S(2)}) collective-permute-start(f32[4,512]{1,0:T(4,128)S(1)} %get-tuple-element.10), channel_id=1, source_target_pairs={{16,0},{24,8},{32,16},{40,24},{48,32},{56,40},{64,48},{72,56},{80,... | collective-permute-start | bytes 24584 | tf_op jit(solution)/shard_map/ppermute | solution.py:12
  130.0 1.9 %collective-permute-start.17 = (f32[4,512]{1,0:T(4,128)S(1)}, f32[4,512]{1,0:T(4,128)S(1)}, u32[]{:S(2)}, u32[]{:S(2)}) collective-permute-start(f32[4,512]{1,0:T(4,128)S(1)} %get-tuple-element.13), channel_id=1, source_target_pairs={{8,0},{16,8},{24,16},{32,24},{40,32},{48,40},{56,48},{64,56},{72,6... | collective-permute-start | bytes 24584 | tf_op jit(solution)/shard_map/ppermute | solution.py:12
  131.9 5.1 %collective-permute-start.18 = (f32[4,512]{1,0:T(4,128)S(1)}, f32[4,512]{1,0:T(4,128)S(1)}, u32[]{:S(2)}, u32[]{:S(2)}) collective-permute-start(f32[4,512]{1,0:T(4,128)S(1)} %get-tuple-element.12), channel_id=1, source_target_pairs={{504,0},{0,8},{8,16},{16,24},{24,32},{32,40},{40,48},{48,56},{56,6... | collective-permute-start | bytes 24584 | tf_op jit(solution)/shard_map/ppermute | solution.py:12
  137.0 5.0 %collective-permute-start.19 = (f32[4,512]{1,0:T(4,128)S(1)}, f32[4,512]{1,0:T(4,128)S(1)}, u32[]{:S(2)}, u32[]{:S(2)}) collective-permute-start(f32[4,512]{1,0:T(4,128)S(1)} %get-tuple-element.11), channel_id=1, source_target_pairs={{496,0},{504,8},{0,16},{8,24},{16,32},{24,40},{32,48},{40,56},{48,... | collective-permute-start | bytes 24584 | tf_op jit(solution)/shard_map/ppermute | solution.py:12
  143.4 1.6 collective-permute-done.19
  146.0 0.7 broadcast_in_dim.17
  146.7 4.5 %all-to-all-start.5 = ((f32[8,4,1024]{2,1,0:T(4,128)}), f32[8,4,1024]{2,1,0:T(4,128)S(1)}, u32[]{:S(2)}, u32[]{:S(2)}) async-start(f32[8,4,1024]{2,1,0:T(4,128)} %broadcast_in_dim.17), calls=%async_computation.5 | async-start | bytes 262144 | tf_op jit(solution)/shard_map/all_to_all | solution.py:17
  151.8 3.0 %collective-permute-start.20 = (f32[4,512]{1,0:T(4,128)S(1)}, f32[4,512]{1,0:T(4,128)S(1)}, u32[]{:S(2)}, u32[]{:S(2)}) collective-permute-start(f32[4,512]{1,0:T(4,128)S(1)} %get-tuple-element.5), channel_id=1, source_target_pairs={{16,0},{24,8},{32,16},{40,24},{48,32},{56,40},{64,48},{72,56},{80,... | collective-permute-start | bytes 24584 | tf_op jit(solution)/shard_map/ppermute | solution.py:12
  154.8 1.9 %collective-permute-start.21 = (f32[4,512]{1,0:T(4,128)S(1)}, f32[4,512]{1,0:T(4,128)S(1)}, u32[]{:S(2)}, u32[]{:S(2)}) collective-permute-start(f32[4,512]{1,0:T(4,128)S(1)} %get-tuple-element.8), channel_id=1, source_target_pairs={{8,0},{16,8},{24,16},{32,24},{40,32},{48,40},{56,48},{64,56},{72,6... | collective-permute-start | bytes 24584 | tf_op jit(solution)/shard_map/ppermute | solution.py:12
  156.7 5.1 %collective-permute-start.22 = (f32[4,512]{1,0:T(4,128)S(1)}, f32[4,512]{1,0:T(4,128)S(1)}, u32[]{:S(2)}, u32[]{:S(2)}) collective-permute-start(f32[4,512]{1,0:T(4,128)S(1)} %get-tuple-element.7), channel_id=1, source_target_pairs={{504,0},{0,8},{8,16},{16,24},{24,32},{32,40},{40,48},{48,56},{56,6... | collective-permute-start | bytes 24584 | tf_op jit(solution)/shard_map/ppermute | solution.py:12
  161.9 4.7 %collective-permute-start.23 = (f32[4,512]{1,0:T(4,128)S(1)}, f32[4,512]{1,0:T(4,128)S(1)}, u32[]{:S(2)}, u32[]{:S(2)}) collective-permute-start(f32[4,512]{1,0:T(4,128)S(1)} %get-tuple-element.6), channel_id=1, source_target_pairs={{496,0},{504,8},{0,16},{8,24},{16,32},{24,40},{32,48},{40,56},{48,... | collective-permute-start | bytes 24584 | tf_op jit(solution)/shard_map/ppermute | solution.py:12
  167.9 2.0 %collective-permute-done.23 = f32[4,512]{1,0:T(4,128)S(1)} collective-permute-done((f32[4,512]{1,0:T(4,128)S(1)}, f32[4,512]{1,0:T(4,128)S(1)}, u32[]{:S(2)}, u32[]{:S(2)}) %collective-permute-start.23) | collective-permute-done | bytes 8224 | tf_op jit(solution)/shard_map/ppermute | solution.py:12
  169.9 1.0 add_multiply_fusion
  (109 shorter events, 15.9 us)
Async XLA Ops:
  0.0 11.9 %copy-start = (bf16[1,5,512,512]{3,2,1,0:T(8,128)(2,1)S(1)}, bf16[1,5,512,512]{3,2,1,0:T(8,128)(2,1)}, u32[]{:S(2)}) copy-start(bf16[1,5,512,512]{3,2,1,0:T(8,128)(2,1)} %param.13) | copy-start | bytes 7864324
  0.0 35.0 %copy-start.2 = (f32[32,32]{1,0:T(8,128)S(1)}, f32[32,32]{1,0:T(8,128)}, u32[]{:S(2)}) copy-start(f32[32,32]{1,0:T(8,128)} %param.16) | copy-start | bytes 12292
  0.0 35.6 %copy-start.3 = (f32[32,32]{1,0:T(8,128)S(1)}, f32[32,32]{1,0:T(8,128)}, u32[]{:S(2)}) copy-start(f32[32,32]{1,0:T(8,128)} %param.17) | copy-start | bytes 12292
  1.7 39.8 %copy-start.1 = (f32[16,32,32]{2,1,0:T(8,128)S(1)}, f32[16,32,32]{2,1,0:T(8,128)}, u32[]{:S(2)}) copy-start(f32[16,32,32]{2,1,0:T(8,128)} %param.11) | copy-start | bytes 196612
  4.7 30.3 %all-to-all-start = ((f32[8,4,1024]{2,1,0:T(4,128)}), f32[8,4,1024]{2,1,0:T(4,128)S(1)}, u32[]{:S(2)}, u32[]{:S(2)}) async-start(f32[8,4,1024]{2,1,0:T(4,128)} %broadcast_in_dim.12), calls=%async_computation | async-start | bytes 262144 | tf_op jit(solution)/shard_map/all_to_all | solution.py:17
  12.4 23.8 %collective-permute-start = (f32[4,512]{1,0:T(4,128)S(1)}, f32[4,512]{1,0:T(4,128)S(1)}, u32[]{:S(2)}, u32[]{:S(2)}) collective-permute-start(f32[4,512]{1,0:T(4,128)S(1)} %get-tuple-element.30), channel_id=1, source_target_pairs={{16,0},{24,8},{32,16},{40,24},{48,32},{56,40},{64,48},{72,56},{80,... | collective-permute-start | bytes 24584 | tf_op jit(solution)/shard_map/ppermute | solution.py:12
  25.9 10.3 %collective-permute-start.1 = (f32[4,512]{1,0:T(4,128)S(1)}, f32[4,512]{1,0:T(4,128)S(1)}, u32[]{:S(2)}, u32[]{:S(2)}) collective-permute-start(f32[4,512]{1,0:T(4,128)S(1)} %get-tuple-element.33), channel_id=1, source_target_pairs={{8,0},{16,8},{24,16},{32,24},{40,32},{48,40},{56,48},{64,56},{72,6... | collective-permute-start | bytes 24584 | tf_op jit(solution)/shard_map/ppermute | solution.py:12
  29.1 7.2 %collective-permute-start.2 = (f32[4,512]{1,0:T(4,128)S(1)}, f32[4,512]{1,0:T(4,128)S(1)}, u32[]{:S(2)}, u32[]{:S(2)}) collective-permute-start(f32[4,512]{1,0:T(4,128)S(1)} %get-tuple-element.32), channel_id=1, source_target_pairs={{504,0},{0,8},{8,16},{16,24},{24,32},{32,40},{40,48},{48,56},{56,6... | collective-permute-start | bytes 24584 | tf_op jit(solution)/shard_map/ppermute | solution.py:12
  33.0 8.0 %collective-permute-start.3 = (f32[4,512]{1,0:T(4,128)S(1)}, f32[4,512]{1,0:T(4,128)S(1)}, u32[]{:S(2)}, u32[]{:S(2)}) collective-permute-start(f32[4,512]{1,0:T(4,128)S(1)} %get-tuple-element.31), channel_id=1, source_target_pairs={{496,0},{504,8},{0,16},{8,24},{16,32},{24,40},{32,48},{40,56},{48,... | collective-permute-start | bytes 24584 | tf_op jit(solution)/shard_map/ppermute | solution.py:12
  42.6 19.9 %all-to-all-start.1 = ((f32[8,4,1024]{2,1,0:T(4,128)}), f32[8,4,1024]{2,1,0:T(4,128)S(1)}, u32[]{:S(2)}, u32[]{:S(2)}) async-start(f32[8,4,1024]{2,1,0:T(4,128)} %broadcast_in_dim.13), calls=%async_computation.1 | async-start | bytes 262144 | tf_op jit(solution)/shard_map/all_to_all | solution.py:17
  47.7 16.1 %collective-permute-start.4 = (f32[4,512]{1,0:T(4,128)S(1)}, f32[4,512]{1,0:T(4,128)S(1)}, u32[]{:S(2)}, u32[]{:S(2)}) collective-permute-start(f32[4,512]{1,0:T(4,128)S(1)} %get-tuple-element.25), channel_id=1, source_target_pairs={{16,0},{24,8},{32,16},{40,24},{48,32},{56,40},{64,48},{72,56},{80,... | collective-permute-start | bytes 24584 | tf_op jit(solution)/shard_map/ppermute | solution.py:12
  51.4 12.4 %collective-permute-start.5 = (f32[4,512]{1,0:T(4,128)S(1)}, f32[4,512]{1,0:T(4,128)S(1)}, u32[]{:S(2)}, u32[]{:S(2)}) collective-permute-start(f32[4,512]{1,0:T(4,128)S(1)} %get-tuple-element.28), channel_id=1, source_target_pairs={{8,0},{16,8},{24,16},{32,24},{40,32},{48,40},{56,48},{64,56},{72,6... | collective-permute-start | bytes 24584 | tf_op jit(solution)/shard_map/ppermute | solution.py:12
  53.3 10.5 %collective-permute-start.6 = (f32[4,512]{1,0:T(4,128)S(1)}, f32[4,512]{1,0:T(4,128)S(1)}, u32[]{:S(2)}, u32[]{:S(2)}) collective-permute-start(f32[4,512]{1,0:T(4,128)S(1)} %get-tuple-element.27), channel_id=1, source_target_pairs={{504,0},{0,8},{8,16},{16,24},{24,32},{32,40},{40,48},{48,56},{56,6... | collective-permute-start | bytes 24584 | tf_op jit(solution)/shard_map/ppermute | solution.py:12
  58.5 8.0 %collective-permute-start.7 = (f32[4,512]{1,0:T(4,128)S(1)}, f32[4,512]{1,0:T(4,128)S(1)}, u32[]{:S(2)}, u32[]{:S(2)}) collective-permute-start(f32[4,512]{1,0:T(4,128)S(1)} %get-tuple-element.26), channel_id=1, source_target_pairs={{496,0},{504,8},{0,16},{8,24},{16,32},{24,40},{32,48},{40,56},{48,... | collective-permute-start | bytes 24584 | tf_op jit(solution)/shard_map/ppermute | solution.py:12
  68.1 18.9 %all-to-all-start.2 = ((f32[8,4,1024]{2,1,0:T(4,128)}), f32[8,4,1024]{2,1,0:T(4,128)S(1)}, u32[]{:S(2)}, u32[]{:S(2)}) async-start(f32[8,4,1024]{2,1,0:T(4,128)} %broadcast_in_dim.14), calls=%async_computation.2 | async-start | bytes 262144 | tf_op jit(solution)/shard_map/all_to_all | solution.py:17
  73.2 15.1 %collective-permute-start.10 = (f32[4,512]{1,0:T(4,128)S(1)}, f32[4,512]{1,0:T(4,128)S(1)}, u32[]{:S(2)}, u32[]{:S(2)}) collective-permute-start(f32[4,512]{1,0:T(4,128)S(1)} %get-tuple-element.22), channel_id=1, source_target_pairs={{504,0},{0,8},{8,16},{16,24},{24,32},{32,40},{40,48},{48,56},{56,6... | collective-permute-start | bytes 24584 | tf_op jit(solution)/shard_map/ppermute | solution.py:12
  75.2 13.2 %collective-permute-start.11 = (f32[4,512]{1,0:T(4,128)S(1)}, f32[4,512]{1,0:T(4,128)S(1)}, u32[]{:S(2)}, u32[]{:S(2)}) collective-permute-start(f32[4,512]{1,0:T(4,128)S(1)} %get-tuple-element.21), channel_id=1, source_target_pairs={{496,0},{504,8},{0,16},{8,24},{16,32},{24,40},{32,48},{40,56},{48,... | collective-permute-start | bytes 24584 | tf_op jit(solution)/shard_map/ppermute | solution.py:12
  80.0 8.3 %collective-permute-start.8 = (f32[4,512]{1,0:T(4,128)S(1)}, f32[4,512]{1,0:T(4,128)S(1)}, u32[]{:S(2)}, u32[]{:S(2)}) collective-permute-start(f32[4,512]{1,0:T(4,128)S(1)} %get-tuple-element.20), channel_id=1, source_target_pairs={{16,0},{24,8},{32,16},{40,24},{48,32},{56,40},{64,48},{72,56},{80,... | collective-permute-start | bytes 24584 | tf_op jit(solution)/shard_map/ppermute | solution.py:12
  84.1 6.5 %collective-permute-start.9 = (f32[4,512]{1,0:T(4,128)S(1)}, f32[4,512]{1,0:T(4,128)S(1)}, u32[]{:S(2)}, u32[]{:S(2)}) collective-permute-start(f32[4,512]{1,0:T(4,128)S(1)} %get-tuple-element.23), channel_id=1, source_target_pairs={{8,0},{16,8},{24,16},{32,24},{40,32},{48,40},{56,48},{64,56},{72,6... | collective-permute-start | bytes 24584 | tf_op jit(solution)/shard_map/ppermute | solution.py:12
  92.2 22.1 %all-to-all-start.3 = ((f32[8,4,1024]{2,1,0:T(4,128)}), f32[8,4,1024]{2,1,0:T(4,128)S(1)}, u32[]{:S(2)}, u32[]{:S(2)}) async-start(f32[8,4,1024]{2,1,0:T(4,128)} %broadcast_in_dim.15), calls=%async_computation.3 | async-start | bytes 262144 | tf_op jit(solution)/shard_map/all_to_all | solution.py:17
  97.9 17.7 %collective-permute-start.12 = (f32[4,512]{1,0:T(4,128)S(1)}, f32[4,512]{1,0:T(4,128)S(1)}, u32[]{:S(2)}, u32[]{:S(2)}) collective-permute-start(f32[4,512]{1,0:T(4,128)S(1)} %get-tuple-element.15), channel_id=1, source_target_pairs={{16,0},{24,8},{32,16},{40,24},{48,32},{56,40},{64,48},{72,56},{80,... | collective-permute-start | bytes 24584 | tf_op jit(solution)/shard_map/ppermute | solution.py:12
  105.3 10.3 %collective-permute-start.13 = (f32[4,512]{1,0:T(4,128)S(1)}, f32[4,512]{1,0:T(4,128)S(1)}, u32[]{:S(2)}, u32[]{:S(2)}) collective-permute-start(f32[4,512]{1,0:T(4,128)S(1)} %get-tuple-element.18), channel_id=1, source_target_pairs={{8,0},{16,8},{24,16},{32,24},{40,32},{48,40},{56,48},{64,56},{72,6... | collective-permute-start | bytes 24584 | tf_op jit(solution)/shard_map/ppermute | solution.py:12
  107.2 8.4 %collective-permute-start.14 = (f32[4,512]{1,0:T(4,128)S(1)}, f32[4,512]{1,0:T(4,128)S(1)}, u32[]{:S(2)}, u32[]{:S(2)}) collective-permute-start(f32[4,512]{1,0:T(4,128)S(1)} %get-tuple-element.17), channel_id=1, source_target_pairs={{504,0},{0,8},{8,16},{16,24},{24,32},{32,40},{40,48},{48,56},{56,6... | collective-permute-start | bytes 24584 | tf_op jit(solution)/shard_map/ppermute | solution.py:12
  112.4 8.0 %collective-permute-start.15 = (f32[4,512]{1,0:T(4,128)S(1)}, f32[4,512]{1,0:T(4,128)S(1)}, u32[]{:S(2)}, u32[]{:S(2)}) collective-permute-start(f32[4,512]{1,0:T(4,128)S(1)} %get-tuple-element.16), channel_id=1, source_target_pairs={{496,0},{504,8},{0,16},{8,24},{16,32},{24,40},{32,48},{40,56},{48,... | collective-permute-start | bytes 24584 | tf_op jit(solution)/shard_map/ppermute | solution.py:12
  122.0 20.1 %all-to-all-start.4 = ((f32[8,4,1024]{2,1,0:T(4,128)}), f32[8,4,1024]{2,1,0:T(4,128)S(1)}, u32[]{:S(2)}, u32[]{:S(2)}) async-start(f32[8,4,1024]{2,1,0:T(4,128)} %broadcast_in_dim.16), calls=%async_computation.4 | async-start | bytes 262144 | tf_op jit(solution)/shard_map/all_to_all | solution.py:17
  127.1 16.3 %collective-permute-start.16 = (f32[4,512]{1,0:T(4,128)S(1)}, f32[4,512]{1,0:T(4,128)S(1)}, u32[]{:S(2)}, u32[]{:S(2)}) collective-permute-start(f32[4,512]{1,0:T(4,128)S(1)} %get-tuple-element.10), channel_id=1, source_target_pairs={{16,0},{24,8},{32,16},{40,24},{48,32},{56,40},{64,48},{72,56},{80,... | collective-permute-start | bytes 24584 | tf_op jit(solution)/shard_map/ppermute | solution.py:12
  130.0 13.4 %collective-permute-start.17 = (f32[4,512]{1,0:T(4,128)S(1)}, f32[4,512]{1,0:T(4,128)S(1)}, u32[]{:S(2)}, u32[]{:S(2)}) collective-permute-start(f32[4,512]{1,0:T(4,128)S(1)} %get-tuple-element.13), channel_id=1, source_target_pairs={{8,0},{16,8},{24,16},{32,24},{40,32},{48,40},{56,48},{64,56},{72,6... | collective-permute-start | bytes 24584 | tf_op jit(solution)/shard_map/ppermute | solution.py:12
  131.9 11.5 %collective-permute-start.18 = (f32[4,512]{1,0:T(4,128)S(1)}, f32[4,512]{1,0:T(4,128)S(1)}, u32[]{:S(2)}, u32[]{:S(2)}) collective-permute-start(f32[4,512]{1,0:T(4,128)S(1)} %get-tuple-element.12), channel_id=1, source_target_pairs={{504,0},{0,8},{8,16},{16,24},{24,32},{32,40},{40,48},{48,56},{56,6... | collective-permute-start | bytes 24584 | tf_op jit(solution)/shard_map/ppermute | solution.py:12
  137.0 8.0 %collective-permute-start.19 = (f32[4,512]{1,0:T(4,128)S(1)}, f32[4,512]{1,0:T(4,128)S(1)}, u32[]{:S(2)}, u32[]{:S(2)}) collective-permute-start(f32[4,512]{1,0:T(4,128)S(1)} %get-tuple-element.11), channel_id=1, source_target_pairs={{496,0},{504,8},{0,16},{8,24},{16,32},{24,40},{32,48},{40,56},{48,... | collective-permute-start | bytes 24584 | tf_op jit(solution)/shard_map/ppermute | solution.py:12
  146.7 19.9 %all-to-all-start.5 = ((f32[8,4,1024]{2,1,0:T(4,128)}), f32[8,4,1024]{2,1,0:T(4,128)S(1)}, u32[]{:S(2)}, u32[]{:S(2)}) async-start(f32[8,4,1024]{2,1,0:T(4,128)} %broadcast_in_dim.17), calls=%async_computation.5 | async-start | bytes 262144 | tf_op jit(solution)/shard_map/all_to_all | solution.py:17
  151.8 16.1 %collective-permute-start.20 = (f32[4,512]{1,0:T(4,128)S(1)}, f32[4,512]{1,0:T(4,128)S(1)}, u32[]{:S(2)}, u32[]{:S(2)}) collective-permute-start(f32[4,512]{1,0:T(4,128)S(1)} %get-tuple-element.5), channel_id=1, source_target_pairs={{16,0},{24,8},{32,16},{40,24},{48,32},{56,40},{64,48},{72,56},{80,... | collective-permute-start | bytes 24584 | tf_op jit(solution)/shard_map/ppermute | solution.py:12
  154.8 13.1 %collective-permute-start.21 = (f32[4,512]{1,0:T(4,128)S(1)}, f32[4,512]{1,0:T(4,128)S(1)}, u32[]{:S(2)}, u32[]{:S(2)}) collective-permute-start(f32[4,512]{1,0:T(4,128)S(1)} %get-tuple-element.8), channel_id=1, source_target_pairs={{8,0},{16,8},{24,16},{32,24},{40,32},{48,40},{56,48},{64,56},{72,6... | collective-permute-start | bytes 24584 | tf_op jit(solution)/shard_map/ppermute | solution.py:12
  156.7 11.1 %collective-permute-start.22 = (f32[4,512]{1,0:T(4,128)S(1)}, f32[4,512]{1,0:T(4,128)S(1)}, u32[]{:S(2)}, u32[]{:S(2)}) collective-permute-start(f32[4,512]{1,0:T(4,128)S(1)} %get-tuple-element.7), channel_id=1, source_target_pairs={{504,0},{0,8},{8,16},{16,24},{24,32},{32,40},{40,48},{48,56},{56,6... | collective-permute-start | bytes 24584 | tf_op jit(solution)/shard_map/ppermute | solution.py:12
  161.9 8.0 %collective-permute-start.23 = (f32[4,512]{1,0:T(4,128)S(1)}, f32[4,512]{1,0:T(4,128)S(1)}, u32[]{:S(2)}, u32[]{:S(2)}) collective-permute-start(f32[4,512]{1,0:T(4,128)S(1)} %get-tuple-element.6), channel_id=1, source_target_pairs={{496,0},{504,8},{0,16},{8,24},{16,32},{24,40},{32,48},{40,56},{48,... | collective-permute-start | bytes 24584 | tf_op jit(solution)/shard_map/ppermute | solution.py:12
where the time goes:
time: 173 us; the launch traced here: 171 us
  starting transfers between devices  126 us (73%)
  waiting for transfers between devices  18.1 us (10%)
  matrix products  16.2 us (9%)
  local copies, waits for them, and re-layouts  7.43 us (4%)
    ppermute x24, starting transfers between devices, from_behind(): return lax.ppermute(block, axis, route)  97.1 us
    all_to_all x6, starting transfers between devices, from_everyone(): return lax.all_to_all(copies, axis, split_axis=0, concat_axis=0, tiled=True)  29.1 us
    ppermute x24, waiting for transfers between devices, from_behind(): return lax.ppermute(block, axis, route)  18 us
    broadcast_in_dim x6, local copies, waits for them, and re-layouts, from_everyone(): copies = jnp.broadcast_to(value, (lax.axis_size(axis), *value.shape))  3.93 us
    dot_general x6, matrix products, reaction_terms(): uptake = jnp.dot(uptake_weight, full_state, precision=highest)  3.63 us
    dot_general x6, matrix products, reaction_terms(): pushed = jnp.dot(release_weight.T, full_settled, precision=highest)  3.59 us
  transfers between devices with their start and end apart: 30, of which 6 were waited for; matrix products, arithmetic and copies ran while one was open for 7% of the time, Pallas kernels for 0%

commit v1 on v0

v1 whole, which is shorter than its diff:
```python
import jax
import jax.numpy as jnp
from jax import lax
from jax.experimental import pallas as pl
from jax.experimental.pallas import tpu as pltpu
from jax.sharding import Mesh, PartitionSpec as P

REGION = ("z", "yhi", "core")
TRACER = ("x", "ylo")
EVERY = REGION + TRACER
SPAN = 128


def device_at(sizes, chip, core, x, ylo):
    nq, nx, ny = sizes
    return (((chip % nq) * 2 + core) * nx + x) * ny + ylo


def neighbour_groups(sizes):
    nq, nx, ny = sizes
    return [
        [device_at(sizes, q, 1, x, yl), device_at(sizes, q + 1, 0, x, ny - 1 - yl)]
        for q in range(nq)
        for x in range(nx)
        for yl in range(ny)
    ]


def halves(value):
    high = value.astype(jnp.bfloat16)
    low = (value - high.astype(jnp.float32)).astype(jnp.bfloat16)
    return high, low


def dot(a, b):
    return lax.dot_general(a, b, (((1,), (0,)), ((), ())), preferred_element_type=jnp.float32)


def dot_split(a_high, a_low, b_high, b_low):
    rows = a_high.shape[0]
    both = dot(jnp.concatenate([a_high, a_low], axis=0), b_high)
    return both[:rows] + both[rows:] + dot(a_high, b_low)


def slot_at(offsets, distance):
    slots = offsets.shape[0]
    slot = jnp.int32(0)
    for k in range(slots):
        slot = slot + jnp.where(offsets[k] == distance, k, 0)
    return slot


def slot_live(offsets, count, distance):
    slots = offsets.shape[0]
    live = jnp.int32(0)
    for k in range(slots):
        live = live + jnp.where((offsets[k] == distance) & (k < count[0]), 1, 0)
    return live > 0


def away(core):
    return 2 * core[0] - 1


def lend_kernel(offsets, count, core, wet, tile, inverse, cotangent, lent, shared):
    live = slot_live(offsets, count, -2 * away(core))
    lent[...] = jnp.where(live, tile[0, 0].astype(jnp.float32), 0.0)
    columns, levels, _ = inverse.shape
    lane = lax.broadcasted_iota(jnp.int32, (levels, levels), 1)
    row = lax.broadcasted_iota(jnp.int32, (8, levels), 1)
    tracers = cotangent.shape[0]
    for c in range(columns):
        at = slice(c * levels, (c + 1) * levels)
        shared[0:levels, at] = jnp.where(lane < wet[c], inverse[c], 0.0)
        shared[levels : levels + 8, at] = jnp.where(row < wet[c], 1.0, 0.0)
    shared[levels + 8 - tracers :, :] = cotangent[...]


def prepare_kernel(core, shared, gathered, borrowed, uptake_weight, tile_out, block_high, block_low, wet_out, slopes, start):
    tile_out[...] = borrowed[...].astype(jnp.bfloat16)
    own = core[0]
    levels = 32
    boxes = shared.shape[2]
    spans = boxes // SPAN
    same = (
        lax.broadcasted_iota(jnp.int32, (SPAN, SPAN), 0) // levels
        == lax.broadcasted_iota(jnp.int32, (SPAN, SPAN), 1) // levels
    )
    for which in range(2):
        side = own if which == 0 else 1 - own
        for s in range(spans):
            part = shared[side, 0:levels, s * SPAN : (s + 1) * SPAN]
            full = jnp.concatenate([part] * (SPAN // levels), axis=0)
            high, low = halves(jnp.where(same, full, 0.0))
            block_high[which * spans + s] = high
            block_low[which * spans + s] = low
        wet_out[which : which + 1, :] = shared[side, levels : levels + 1, :]
    peers = gathered.shape[0]
    tracers = 4
    for t in range(peers):
        at = slice(t * tracers, (t + 1) * tracers)
        start[at, :] = gathered[t, 0:tracers, :]
        start[slice(t * tracers + peers * tracers, (t + 1) * tracers + peers * tracers), :] = gathered[
            t, tracers : 2 * tracers, :
        ]
        for n in range(slopes.shape[0]):
            slopes[n, at, :] = gathered[t, (2 + n) * tracers : (3 + n) * tracers, :]
    weight_high, weight_low = halves(uptake_weight[...])
    for n in range(slopes.shape[0]):
        state_high, state_low = halves(slopes[n])
        reach = jnp.tanh(dot_split(weight_high, weight_low, state_high, state_low))
        slopes[n] = 1.0 - reach * reach


def step_kernel(
    offsets, count, core, adjoint, tiles, borrowed, block_high, block_low, wet, slope, uptake_t, release_t, send, keep, settled,
    *, first,
):
    own = core[0]
    direction = away(core)
    boxes = tiles.shape[3]
    tracers = send.shape[0] // 2
    spans = boxes // SPAN
    if first:
        pair = (adjoint[0:tracers, :], adjoint[tracers:, :])
    else:
        pair = (
            wet[0:1, :] * (adjoint[own, 0:tracers, :] + adjoint[1 - own, tracers:, :]),
            wet[1:2, :] * (adjoint[own, tracers:, :] + adjoint[1 - own, 0:tracers, :]),
        )
    for which in range(2):
        high, low = halves(pair[which])
        for s in range(spans):
            at = slice(s * SPAN, (s + 1) * SPAN)
            k = which * spans + s
            settled[which, :, at] = dot_split(high[:, at], low[:, at], block_high[k], block_low[k])
    own_high, own_low = halves(settled[0])
    other = settled[1].astype(jnp.bfloat16)

    def term(distance):
        product = dot(own_high, tiles[0, slot_at(offsets, distance)])
        return jnp.where(slot_live(offsets, count, distance), product, 0.0)

    send[0:tracers, :] = term(direction) + dot(other, borrowed[...])
    send[tracers:, :] = term(2 * direction)
    release_high, release_low = halves(release_t[...])
    pushed = slope[0] * dot_split(release_high, release_low, own_high, own_low)
    pushed_high, pushed_low = halves(pushed)
    uptake_high, uptake_low = halves(uptake_t[...])
    keep[0:tracers, :] = term(0) + dot_split(uptake_high, uptake_low, pushed_high, pushed_low)
    keep[tracers:, :] = term(-direction)


def local(
    cotangent,
    states,
    implicit_inverse,
    wet_levels,
    explicit_tiles,
    tile_offset,
    tile_count,
    uptake_weight,
    release_weight,
    *,
    sizes,
):
    tracers_here, boxes = cotangent.shape
    sections = states.shape[0]
    columns, levels, _ = implicit_inverse.shape
    tracers = uptake_weight.shape[0]
    spans = boxes // SPAN
    peers = tracers // tracers_here
    f32, bf16 = jnp.float32, jnp.bfloat16
    shape = jax.ShapeDtypeStruct
    vmem = pl.BlockSpec(memory_space=pltpu.VMEM)
    smem = pl.BlockSpec(memory_space=pltpu.SMEM)
    core_index = lax.axis_index("core")
    core = core_index.astype(jnp.int32).reshape(1)
    offsets = tile_offset.reshape(-1)
    groups = neighbour_groups(sizes)

    def whole(dims):
        return pl.BlockSpec(dims, lambda i, *_: (0,) * len(dims))

    lent, shared = pl.pallas_call(
        lend_kernel,
        grid_spec=pltpu.PrefetchScalarGridSpec(
            num_scalar_prefetch=4,
            grid=(1,),
            in_specs=[
                pl.BlockSpec((1, 1, boxes, boxes), lambda i, o, n, c, w: (0, slot_at(o, -2 * away(c)), 0, 0)),
                whole((columns, levels, levels)),
                whole((tracers_here, boxes)),
            ],
            out_specs=[whole((boxes, boxes)), whole((levels + 8, boxes))],
        ),
        out_shape=[shape((boxes, boxes), f32), shape((levels + 8, boxes), f32)],
        name="lend",
    )(offsets, tile_count, core, wet_levels, explicit_tiles, implicit_inverse, cotangent)
    borrowed = lax.ppermute(lent, "core", [(0, 1), (1, 0)])
    shared = lax.all_gather(shared, "core")
    other_cotangent = lax.dynamic_index_in_dim(shared, 1 - core_index, 0, keepdims=False)[levels + 8 - tracers_here :]
    outgoing = jnp.concatenate([cotangent, other_cotangent, states.reshape(-1, boxes)], axis=0)
    gathered = lax.all_to_all(
        jnp.broadcast_to(outgoing, (peers, *outgoing.shape)), TRACER, split_axis=0, concat_axis=0, tiled=True
    )
    borrowed, block_high, block_low, wet, slopes, adjoint = pl.pallas_call(
        prepare_kernel,
        in_specs=[smem] + [vmem] * 4,
        out_specs=[vmem] * 6,
        out_shape=[
            shape((boxes, boxes), bf16),
            shape((2 * spans, SPAN, SPAN), bf16),
            shape((2 * spans, SPAN, SPAN), bf16),
            shape((2, boxes), f32),
            shape((sections, tracers, boxes), f32),
            shape((2 * tracers, boxes), f32),
        ],
        name="prepare",
    )(core, shared, gathered, borrowed, uptake_weight)
    uptake_t, release_t = uptake_weight.T, release_weight.T
    for section in range(sections - 1, -1, -1):
        first = section == sections - 1

        def step(*refs, first=first):
            step_kernel(*refs, first=first)

        send, keep = pl.pallas_call(
            step,
            in_specs=[smem] * 3 + [vmem] * 9,
            out_specs=[vmem] * 2,
            out_shape=[shape((2 * tracers, boxes), f32)] * 2,
            scratch_shapes=[pltpu.VMEM((2, tracers, boxes), f32)],
            name="step_first" if first else "step",
        )(offsets, tile_count, core, adjoint, explicit_tiles, borrowed, block_high, block_low, wet,
          slopes[section : section + 1], uptake_t, release_t)
        arrived = lax.all_gather(send, EVERY, axis_index_groups=groups)
        keep = keep + lax.dynamic_index_in_dim(arrived, core_index, 0, keepdims=False)
        adjoint = lax.all_gather(keep, "core")
    row = (lax.axis_index("x") * lax.axis_size("ylo") + lax.axis_index("ylo")) * tracers_here
    mine = lax.dynamic_slice(adjoint, (core_index, row, 0), (1, tracers_here, boxes))[0]
    theirs = lax.dynamic_slice(adjoint, (1 - core_index, tracers + row, 0), (1, tracers_here, boxes))[0]
    return wet[0:1] * (mine + theirs)


def solution(mesh):
    regions, tracer_devices = mesh.devices.shape
    nq, nx, ny = regions // 2, tracer_devices // 2, 2
    fine = Mesh(mesh.devices.reshape(nq // 2, 2, 2, nx, ny), EVERY)
    placed = (
        P(TRACER, REGION),
        P(None, TRACER, REGION),
        P(REGION, None, None),
        P(REGION),
        P(REGION, None, None, None),
        P(REGION, None),
        P(REGION),
        P(),
        P(),
    )

    def body(*args):
        return local(*args, sizes=(nq, nx, ny))

    return jax.shard_map(body, mesh=fine, in_specs=placed, out_specs=P(TRACER, REGION), check_vma=False)
```

time: 173 us -> 131 us (0.76)
  starting transfers between devices: 126 us -> 12.2 us
  blocking collectives: 0 us -> 69.4 us
  Pallas kernels: 0 us -> 27.2 us
  matrix products: 16.2 us -> 0 us
  waiting for transfers between devices: 18.1 us -> 7.76 us
  other arithmetic: 1.63 us -> 6.17 us
    ppermute x24 -> x1, starting transfers between devices: 97.1 us -> 8.73 us  [local(): borrowed = lax.ppermute(lent, 'core', [(0, 1), (1, 0)])]
    all_gather x0 -> x13, blocking collectives: none -> 69.4 us  [the longest x6 40.4 us: local(): arrived = lax.all_gather(send, EVERY, axis_index_groups=groups)]
    pallas_call x0 -> x8, Pallas kernels: none -> 27.2 us  [the longest x6 21.3 us: local(): pl.pallas_call(step, in_specs=[smem] * 3 + [vmem] * 9, out_specs=[vmem] *...]
    all_to_all x6 -> x1, starting transfers between devices: 29.1 us -> 3.49 us  [local(): lax.all_to_all(jnp.broadcast_to(outgoing, (peers, *outgoing.shape)), TRAC...]
    ppermute x24 -> x1, waiting for transfers between devices: 18 us -> 0.01 us  [local(): borrowed = lax.ppermute(lent, 'core', [(0, 1), (1, 0)])]
    dot_general x30 -> x0, matrix products: 16.2 us -> none  [the longest x6 3.63 us: reaction_terms(): uptake = jnp.dot(uptake_weight, full_state, precision=highest)]
    all_to_all x6 -> x1, waiting for transfers between devices: 0.02 us -> 7.76 us  [local(): lax.all_to_all(jnp.broadcast_to(outgoing, (peers, *outgoing.shape)), TRAC...]
    add x0 -> x6, other arithmetic: none -> 5.55 us  [local(): keep + lax.dynamic_index_in_dim(arrived, core_index, 0, keepdims=False)]
  transfers between devices with their start and end apart: 30 -> 2, of which waited for: 6 -> 1; matrix products, arithmetic and copies ran while one was open for 7% -> 2% of each run, Pallas kernels for 0% -> 0%
where the time goes in v1:
time: 131 us; the launch traced here: 130 us
  blocking collectives  69.4 us (53%)
  Pallas kernels  27.2 us (21%)
  starting transfers between devices  12.2 us (9%)
  waiting for transfers between devices  7.76 us (6%)
  local copies, waits for them, and re-layouts  6.51 us (5%)
  other arithmetic  6.17 us (5%)
    all_gather x6, blocking collectives, local(): arrived = lax.all_gather(send, EVERY, axis_index_groups=groups)  40.4 us
    all_gather x6, blocking collectives, local(): adjoint = lax.all_gather(keep, 'core')  26.5 us
    pallas_call x6, Pallas kernels, local(): pl.pallas_call(step, in_specs=[smem] * 3 + [vmem] * 9, out_specs=[vmem] *...  21.3 us
    ppermute x1, starting transfers between devices, local(): borrowed = lax.ppermute(lent, 'core', [(0, 1), (1, 0)])  8.73 us
    all_to_all x1, waiting for transfers between devices, local(): lax.all_to_all(jnp.broadcast_to(outgoing, (peers, *outgoing.shape)), TRAC...  7.76 us
    add x6, other arithmetic, local(): keep + lax.dynamic_index_in_dim(arrived, core_index, 0, keepdims=False)  5.55 us
    all_to_all x1, starting transfers between devices, local(): lax.all_to_all(jnp.broadcast_to(outgoing, (peers, *outgoing.shape)), TRAC...  3.49 us
    unnamed x16, local copies, waits for them, and re-layouts  3.15 us
  transfers between devices with their start and end apart: 2, of which 1 were waited for; matrix products, arithmetic and copies ran while one was open for 2% of the time, Pallas kernels for 0%

profile of v1, /device:TPU:1, one launch (start us, length us, event | category | flops | bytes accessed | tf_op | source)
XLA Modules:
  0.0 130.0 jit_solution(17722202456345752089)
XLA Ops:
  0.0 0.0 copy-start.5
  0.0 0.0 copy-start.4
  0.0 0.0 copy-start.3
  0.0 0.0 copy-start.6
  0.7 3.0 %lend.1 = (f32[512,512]{1,0:T(8,128)}, f32[40,512]{1,0:T(8,128)}) custom-call(s32[5]{0:T(128)} %bitcast.60, s32[1]{0:T(128)S(6)} %copy.12.count.refs_1_, s32[1]{0:T(128)} %bitcast.core.refs_2_, s32[16]{0:T(128)} %wet.1, bf16[1,5,512,512]{3,2,1,0:T(8,128)(2,1)} %refs_4_.11, f32[16,32,32]{2,1,0:T(8,128)} %inverse.1, f32[4,512]{1,0:T(4,128)} %cotangent.1), custom_call_target="tpu_custom_call" | custom-call | tf_op jit(solution)/shard_map/lend/pallas_call | solution.py:185
  3.7 8.7 %collective-permute-start = (f32[512,512]{1,0:T(8,128)}, f32[512,512]{1,0:T(8,128)S(1)}, u32[]{:S(2)}, u32[]{:S(2)}) collective-permute-start(f32[512,512]{1,0:T(8,128)} %get-tuple-element.26), channel_id=1, source_target_pairs={{0,8},{8,0},{1,9},{9,1},{2,10},{10,2},{3,11},{11,3},{4,12},{12,4},... | collective-permute-start | bytes 3145736 | tf_op jit(solution)/shard_map/ppermute | solution.py:200
  12.4 0.0 copy-done.4
  12.5 2.6 %all-gather = f32[80,512]{1,0:T(8,128)S(1)} all-gather(f32[40,512]{1,0:T(8,128)} %get-tuple-element.25), channel_id=2, replica_groups=mesh['z'=16,'yhi'=2,'core'=2,'x'=4,'ylo'=2] {'core'}, dimensions={0}, use_global_device_ids=true | all-gather | bytes 245760 | tf_op jit(solution)/shard_map/all_gather | solution.py:201
  15.0 0.0 copy-done.5
  15.0 0.9 broadcast_in_dim.3
  15.9 3.5 %all-to-all-start = ((f32[8,32,512]{2,1,0:T(8,128)}), f32[8,32,512]{2,1,0:T(8,128)S(1)}, u32[]{:S(2)}, u32[]{:S(2)}) async-start(f32[8,32,512]{2,1,0:T(8,128)} %broadcast_in_dim.3), calls=%async_computation | async-start | bytes 1048576 | tf_op jit(solution)/shard_map/all_to_all | solution.py:204
  19.4 0.0 copy-done.3
  19.4 0.7 copy.10
  20.1 0.0 copy-done.6
  20.1 0.7 copy.11
  20.8 7.8 %all-to-all-done.gathered = f32[8,32,512]{2,1,0:T(8,128)S(1)} async-done(((f32[8,32,512]{2,1,0:T(8,128)}), f32[8,32,512]{2,1,0:T(8,128)S(1)}, u32[]{:S(2)}, u32[]{:S(2)}) %all-to-all-start) | async-done | bytes 524320 | tf_op jit(solution)/shard_map/all_to_all | solution.py:204
  28.6 0.0 collective-permute-done.borrowed
  28.6 0.0 copy-done.2
  28.6 0.8 copy-done
  29.4 1.0 copy-done.1
  30.3 2.9 %prepare.1 = (bf16[512,512]{1,0:T(8,128)(2,1)}, bf16[8,128,128]{2,1,0:T(8,128)(2,1)}, bf16[8,128,128]{2,1,0:T(8,128)(2,1)}, f32[2,512]{1,0:T(2,128)}, f32[6,32,512]{2,1,0:T(8,128)}, /*index=5*/f32[64,512]{1,0:T(8,128)}) custom-call(s32[1]{0:T(128)} %bitcast.core.refs_2_, f32[2,40,512]{2,1,0:T(8,128)} %bitcast.52, f32[8,32,512]{2,1,0:T(8,128)} %copy-done, ...), custom_call_target="tpu_custom_call" | custom-call | tf_op jit(solution)/shard_map/prepare/pallas_call | solution.py:207
  33.3 1.8 %fusion = (f32[1,32,512]{2,1,0:T(8,128)}, f32[1,32,512]{2,1,0:T(8,128)}, f32[1,32,512]{2,1,0:T(8,128)}, f32[1,32,512]{2,1,0:T(8,128)}, f32[1,32,512]{2,1,0:T(8,128)}, /*index=5*/f32[1,32,512]{2,1,0:T(8,128)}) fusion(f32[6,32,512]{2,1,0:T(8,128)} %get-tuple-element.32), kind=kLoop, calls=%fused_computation.9 | loop fusion | bytes 786432 | tf_op jit(solution)/shard_map/slice | solution.py:236
  35.0 0.7 slice.29
  35.7 3.5 %step_first.1 = (f32[64,512]{1,0:T(8,128)}, f32[64,512]{1,0:T(8,128)}) custom-call(s32[5]{0:T(128)} %bitcast.61, s32[1]{0:T(128)S(6)} %copy.12.count.refs_1_, s32[1]{0:T(128)} %bitcast.core.refs_2_, f32[64,512]{1,0:T(8,128)} %get-tuple-element.28.refs_3_, bf16[1,5,512,512]{3,2,1,0:T(8,128)(2,1)} %refs_4_.11, bf16[512,512]{1,0:T(8,128)(2,1)} %get-tuple-element.29.refs_5_, ...), custom_call_target="tpu_custom_call" | custom-call | tf_op jit(solution)/shard_map/step_first/pallas_call | solution.py:228
  39.2 6.5 %all-gather.1 = f32[128,512]{1,0:T(8,128)S(1)} all-gather(f32[64,512]{1,0:T(8,128)} %get-tuple-element.34), channel_id=3, replica_groups={{8,17},{9,16},{10,19},{11,18},{12,21},{13,20},{14,23},{15,22},{24,33},{..., dimensions={0}, use_global_device_ids=true | all-gather | bytes 393216 | tf_op jit(solution)/shard_map/all_gather | solution.py:237
  45.7 0.9 bitcast_add_fusion.5
  46.6 6.8 %all-gather.2 = f32[128,512]{1,0:T(8,128)} all-gather(f32[64,512]{1,0:T(8,128)S(1)} %bitcast_add_fusion.5), channel_id=4, replica_groups=mesh['z'=16,'yhi'=2,'core'=2,'x'=4,'ylo'=2] {'core'}, dimensions={0}, use_global_device_ids=true | all-gather | bytes 393216 | tf_op jit(solution)/shard_map/all_gather | solution.py:239
  53.4 3.6 %step.5 = (f32[64,512]{1,0:T(8,128)}, f32[64,512]{1,0:T(8,128)}) custom-call(s32[5]{0:T(128)} %bitcast.62, s32[1]{0:T(128)S(6)} %copy.12.count.refs_1_, s32[1]{0:T(128)} %bitcast.core.refs_2_, f32[2,64,512]{2,1,0:T(8,128)} %bitcast.35, bf16[1,5,512,512]{3,2,1,0:T(8,128)(2,1)} %refs_4_.11, bf16[512,512]{1,0:T(8,128)(2,1)} %get-tuple-element.29.refs_5_, ...), custom_call_target="tpu_custom_call" | custom-call | tf_op jit(solution)/shard_map/step/pallas_call | solution.py:228
  57.0 6.8 %all-gather.3 = f32[128,512]{1,0:T(8,128)S(1)} all-gather(f32[64,512]{1,0:T(8,128)} %get-tuple-element.36), channel_id=5, replica_groups={{8,17},{9,16},{10,19},{11,18},{12,21},{13,20},{14,23},{15,22},{24,33},{..., dimensions={0}, use_global_device_ids=true | all-gather | bytes 393216 | tf_op jit(solution)/shard_map/all_gather | solution.py:237
  63.8 0.9 bitcast_add_fusion.4
  64.7 4.0 %all-gather.4 = f32[128,512]{1,0:T(8,128)} all-gather(f32[64,512]{1,0:T(8,128)S(1)} %bitcast_add_fusion.4), channel_id=6, replica_groups=mesh['z'=16,'yhi'=2,'core'=2,'x'=4,'ylo'=2] {'core'}, dimensions={0}, use_global_device_ids=true | all-gather | bytes 393216 | tf_op jit(solution)/shard_map/all_gather | solution.py:239
  68.7 3.6 %step.6 = (f32[64,512]{1,0:T(8,128)}, f32[64,512]{1,0:T(8,128)}) custom-call(s32[5]{0:T(128)} %bitcast.63, s32[1]{0:T(128)S(6)} %copy.12.count.refs_1_, s32[1]{0:T(128)} %bitcast.core.refs_2_, f32[2,64,512]{2,1,0:T(8,128)} %bitcast.36, bf16[1,5,512,512]{3,2,1,0:T(8,128)(2,1)} %refs_4_.11, bf16[512,512]{1,0:T(8,128)(2,1)} %get-tuple-element.29.refs_5_, ...), custom_call_target="tpu_custom_call" | custom-call | tf_op jit(solution)/shard_map/step/pallas_call | solution.py:228
  72.3 6.8 %all-gather.5 = f32[128,512]{1,0:T(8,128)S(1)} all-gather(f32[64,512]{1,0:T(8,128)} %get-tuple-element.38), channel_id=7, replica_groups={{8,17},{9,16},{10,19},{11,18},{12,21},{13,20},{14,23},{15,22},{24,33},{..., dimensions={0}, use_global_device_ids=true | all-gather | bytes 393216 | tf_op jit(solution)/shard_map/all_gather | solution.py:237
  79.1 0.9 bitcast_add_fusion.3
  80.0 3.9 %all-gather.6 = f32[128,512]{1,0:T(8,128)} all-gather(f32[64,512]{1,0:T(8,128)S(1)} %bitcast_add_fusion.3), channel_id=8, replica_groups=mesh['z'=16,'yhi'=2,'core'=2,'x'=4,'ylo'=2] {'core'}, dimensions={0}, use_global_device_ids=true | all-gather | bytes 393216 | tf_op jit(solution)/shard_map/all_gather | solution.py:239
  83.9 3.6 %step.7 = (f32[64,512]{1,0:T(8,128)}, f32[64,512]{1,0:T(8,128)}) custom-call(s32[5]{0:T(128)} %bitcast.64, s32[1]{0:T(128)S(6)} %copy.12.count.refs_1_, s32[1]{0:T(128)} %bitcast.core.refs_2_, f32[2,64,512]{2,1,0:T(8,128)} %bitcast.37, bf16[1,5,512,512]{3,2,1,0:T(8,128)(2,1)} %refs_4_.11, bf16[512,512]{1,0:T(8,128)(2,1)} %get-tuple-element.29.refs_5_, ...), custom_call_target="tpu_custom_call" | custom-call | tf_op jit(solution)/shard_map/step/pallas_call | solution.py:228
  87.5 6.8 %all-gather.7 = f32[128,512]{1,0:T(8,128)S(1)} all-gather(f32[64,512]{1,0:T(8,128)} %get-tuple-element.40), channel_id=9, replica_groups={{8,17},{9,16},{10,19},{11,18},{12,21},{13,20},{14,23},{15,22},{24,33},{..., dimensions={0}, use_global_device_ids=true | all-gather | bytes 393216 | tf_op jit(solution)/shard_map/all_gather | solution.py:237
  94.3 0.9 bitcast_add_fusion.2
  95.2 3.9 %all-gather.8 = f32[128,512]{1,0:T(8,128)} all-gather(f32[64,512]{1,0:T(8,128)S(1)} %bitcast_add_fusion.2), channel_id=10, replica_groups=mesh['z'=16,'yhi'=2,'core'=2,'x'=4,'ylo'=2] {'core'}, dimensions={0}, use_global_device_ids=true | all-gather | bytes 393216 | tf_op jit(solution)/shard_map/all_gather | solution.py:239
  99.1 3.6 %step.8 = (f32[64,512]{1,0:T(8,128)}, f32[64,512]{1,0:T(8,128)}) custom-call(s32[5]{0:T(128)} %bitcast.65, s32[1]{0:T(128)S(6)} %copy.12.count.refs_1_, s32[1]{0:T(128)} %bitcast.core.refs_2_, f32[2,64,512]{2,1,0:T(8,128)} %bitcast.38, bf16[1,5,512,512]{3,2,1,0:T(8,128)(2,1)} %refs_4_.11, bf16[512,512]{1,0:T(8,128)(2,1)} %get-tuple-element.29.refs_5_, ...), custom_call_target="tpu_custom_call" | custom-call | tf_op jit(solution)/shard_map/step/pallas_call | solution.py:228
  102.7 6.8 %all-gather.9 = f32[128,512]{1,0:T(8,128)S(1)} all-gather(f32[64,512]{1,0:T(8,128)} %get-tuple-element.42), channel_id=11, replica_groups={{8,17},{9,16},{10,19},{11,18},{12,21},{13,20},{14,23},{15,22},{24,33},{..., dimensions={0}, use_global_device_ids=true | all-gather | bytes 393216 | tf_op jit(solution)/shard_map/all_gather | solution.py:237
  109.5 0.9 bitcast_add_fusion.1
  110.4 3.9 %all-gather.10 = f32[128,512]{1,0:T(8,128)} all-gather(f32[64,512]{1,0:T(8,128)S(1)} %bitcast_add_fusion.1), channel_id=12, replica_groups=mesh['z'=16,'yhi'=2,'core'=2,'x'=4,'ylo'=2] {'core'}, dimensions={0}, use_global_device_ids=true | all-gather | bytes 393216 | tf_op jit(solution)/shard_map/all_gather | solution.py:239
  114.3 3.6 %step.9 = (f32[64,512]{1,0:T(8,128)}, f32[64,512]{1,0:T(8,128)}) custom-call(s32[5]{0:T(128)} %bitcast.66, s32[1]{0:T(128)S(6)} %copy.12.count.refs_1_, s32[1]{0:T(128)} %bitcast.core.refs_2_, f32[2,64,512]{2,1,0:T(8,128)} %bitcast.34, bf16[1,5,512,512]{3,2,1,0:T(8,128)(2,1)} %refs_4_.11, bf16[512,512]{1,0:T(8,128)(2,1)} %get-tuple-element.29.refs_5_, ...), custom_call_target="tpu_custom_call" | custom-call | tf_op jit(solution)/shard_map/step/pallas_call | solution.py:228
  117.9 6.8 %all-gather.11 = f32[128,512]{1,0:T(8,128)S(1)} all-gather(f32[64,512]{1,0:T(8,128)} %get-tuple-element.44), channel_id=13, replica_groups={{8,17},{9,16},{10,19},{11,18},{12,21},{13,20},{14,23},{15,22},{24,33},{..., dimensions={0}, use_global_device_ids=true | all-gather | bytes 393216 | tf_op jit(solution)/shard_map/all_gather | solution.py:237
  124.7 0.9 bitcast_add_fusion
  125.6 3.8 %all-gather.12 = f32[128,512]{1,0:T(8,128)S(1)} all-gather(f32[64,512]{1,0:T(8,128)S(1)} %bitcast_add_fusion), channel_id=14, replica_groups=mesh['z'=16,'yhi'=2,'core'=2,'x'=4,'ylo'=2] {'core'}, dimensions={0}, use_global_device_ids=true | all-gather | bytes 393216 | tf_op jit(solution)/shard_map/all_gather | solution.py:239
  129.4 0.6 bitcast_multiply_fusion
  (6 shorter events, 0.0 us)
Async XLA Ops:
  0.0 15.0 %copy-start.5 = (f32[4,512]{1,0:T(4,128)S(1)}, f32[4,512]{1,0:T(4,128)}, u32[]{:S(2)}) copy-start(f32[4,512]{1,0:T(4,128)} %cotangent.1) | copy-start | bytes 24580
  0.0 12.4 %copy-start.4 = (f32[6,4,512]{2,1,0:T(4,128)S(1)}, f32[6,4,512]{2,1,0:T(4,128)}, u32[]{:S(2)}) copy-start(f32[6,4,512]{2,1,0:T(4,128)} %param.10) | copy-start | bytes 147460
  0.0 19.4 %copy-start.3 = (f32[32,32]{1,0:T(8,128)S(1)}, f32[32,32]{1,0:T(8,128)}, u32[]{:S(2)}) copy-start(f32[32,32]{1,0:T(8,128)} %uptake_weight.1) | copy-start | bytes 12292
  0.0 20.1 %copy-start.6 = (f32[32,32]{1,0:T(8,128)S(1)}, f32[32,32]{1,0:T(8,128)}, u32[]{:S(2)}) copy-start(f32[32,32]{1,0:T(8,128)} %param.17) | copy-start | bytes 12292
  3.7 24.9 %collective-permute-start = (f32[512,512]{1,0:T(8,128)}, f32[512,512]{1,0:T(8,128)S(1)}, u32[]{:S(2)}, u32[]{:S(2)}) collective-permute-start(f32[512,512]{1,0:T(8,128)} %get-tuple-element.26), channel_id=1, source_target_pairs={{0,8},{8,0},{1,9},{9,1},{2,10},{10,2},{3,11},{11,3},{4,12},{12,4},... | collective-permute-start | bytes 3145736 | tf_op jit(solution)/shard_map/ppermute | solution.py:200
  15.0 13.5 %copy-start.2 = (f32[80,512]{1,0:T(8,128)}, f32[80,512]{1,0:T(8,128)S(1)}, u32[]{:S(2)}) copy-start(f32[80,512]{1,0:T(8,128)S(1)} %all-gather) | copy-start | bytes 491524
  15.9 12.6 %all-to-all-start = ((f32[8,32,512]{2,1,0:T(8,128)}), f32[8,32,512]{2,1,0:T(8,128)S(1)}, u32[]{:S(2)}, u32[]{:S(2)}) async-start(f32[8,32,512]{2,1,0:T(8,128)} %broadcast_in_dim.3), calls=%async_computation | async-start | bytes 1048576 | tf_op jit(solution)/shard_map/all_to_all | solution.py:204
  28.6 0.8 copy-start
  29.4 1.0 copy-start.1

commit v2 on v1

--- a/solution.py
+++ b/solution.py
@@ -9,6 +9,7 @@
 TRACER = ("x", "ylo")
 EVERY = REGION + TRACER
 SPAN = 128
+VMEM_LIMIT = 16 * 2**20
 
 
 def device_at(sizes, chip, core, x, ylo):
@@ -195,6 +196,7 @@
             out_specs=[whole((boxes, boxes)), whole((levels + 8, boxes))],
         ),
         out_shape=[shape((boxes, boxes), f32), shape((levels + 8, boxes), f32)],
+        compiler_params=pltpu.CompilerParams(vmem_limit_bytes=VMEM_LIMIT),
         name="lend",
     )(offsets, tile_count, core, wet_levels, explicit_tiles, implicit_inverse, cotangent)
     borrowed = lax.ppermute(lent, "core", [(0, 1), (1, 0)])
@@ -216,6 +218,7 @@
             shape((sections, tracers, boxes), f32),
             shape((2 * tracers, boxes), f32),
         ],
+        compiler_params=pltpu.CompilerParams(vmem_limit_bytes=VMEM_LIMIT),
         name="prepare",
     )(core, shared, gathered, borrowed, uptake_weight)
     uptake_t, release_t = uptake_weight.T, release_weight.T
@@ -231,6 +234,7 @@
             out_specs=[vmem] * 2,
             out_shape=[shape((2 * tracers, boxes), f32)] * 2,
             scratch_shapes=[pltpu.VMEM((2, tracers, boxes), f32)],
+            compiler_params=pltpu.CompilerParams(vmem_limit_bytes=VMEM_LIMIT),
             name="step_first" if first else "step",
         )(offsets, tile_count, core, adjoint, explicit_tiles, borrowed, block_high, block_low, wet,
           slopes[section : section + 1], uptake_t, release_t)

time: 131 us -> 108 us (0.82)
  Pallas kernels: 27.2 us -> 11.5 us
  other arithmetic: 6.17 us -> 0.72 us
  blocking collectives: 69.4 us -> 67.8 us
    pallas_call x6, Pallas kernels: 21.3 us -> 8.06 us  [local(): pl.pallas_call(step, in_specs=[smem] * 3 + [vmem] * 9, out_specs=[vmem] *...]
    add x6, other arithmetic: 5.55 us -> 0.1 us  [local(): keep + lax.dynamic_index_in_dim(arrived, core_index, 0, keepdims=False)]
    slice x1, local copies, waits for them, and re-layouts: 1.76 us -> 0.03 us  [local(): slopes[section:section + 1]]
    unnamed x16 -> x24, local copies, waits for them, and re-layouts: 3.15 us -> 4.85 us
  transfers between devices with their start and end apart: 2 -> 2, of which waited for: 1 -> 1; matrix products, arithmetic and copies ran while one was open for 2% -> 1% of each run, Pallas kernels for 0% -> 0%
where the time goes in v2:
time: 108 us
  blocking collectives  67.8 us (63%)
  starting transfers between devices  12.5 us (12%)
  Pallas kernels  11.5 us (11%)
  waiting for transfers between devices  8.94 us (8%)
  local copies, waits for them, and re-layouts  5.76 us (5%)
    all_gather x6, blocking collectives, local(): arrived = lax.all_gather(send, EVERY, axis_index_groups=groups)  39.2 us
    all_gather x6, blocking collectives, local(): adjoint = lax.all_gather(keep, 'core')  26.1 us
    ppermute x1, starting transfers between devices, local(): borrowed = lax.ppermute(lent, 'core', [(0, 1), (1, 0)])  9 us
    all_to_all x1, waiting for transfers between devices, local(): lax.all_to_all(jnp.broadcast_to(outgoing, (peers, *outgoing.shape)), TRAC...  8.94 us
    pallas_call x6, Pallas kernels, local(): pl.pallas_call(step, in_specs=[smem] * 3 + [vmem] * 9, out_specs=[vmem] *...  8.06 us
    unnamed x24, local copies, waits for them, and re-layouts  4.85 us
    all_to_all x1, starting transfers between devices, local(): lax.all_to_all(jnp.broadcast_to(outgoing, (peers, *outgoing.shape)), TRAC...  3.49 us
    all_gather x1, blocking collectives, local(): shared = lax.all_gather(shared, 'core')  2.57 us
  transfers between devices with their start and end apart: 2, of which 1 were waited for; matrix products, arithmetic and copies ran while one was open for 1% of the time, Pallas kernels for 0%

profile of v2, /device:TPU:1, one launch (start us, length us, event | category | flops | bytes accessed | tf_op | source)
XLA Modules:
  0.0 108.0 jit_solution(740152014080499962)
XLA Ops:
  0.0 0.0 copy-start.5
  0.7 0.0 copy-start
  0.7 1.7 %copy-done = bf16[1,5,512,512]{3,2,1,0:T(8,128)(2,1)S(1)} copy-done((bf16[1,5,512,512]{3,2,1,0:T(8,128)(2,1)S(1)}, bf16[1,5,512,512]{3,2,1,0:T(8,128)(2,1)}, u32[]{:S(2)}) %copy-start) | copy-done | bytes 2621464
  2.4 0.0 copy-start.2
  2.4 0.9 copy-done.2
  3.4 0.0 copy-start.4
  3.4 0.7 copy-done.4
  4.1 0.0 copy-start.6
  4.1 0.7 copy-done.6
  4.7 0.0 copy-start.8
  4.7 0.7 copy-done.8
  5.4 0.0 copy-start.9
  5.4 0.0 copy-start.3
  5.4 1.7 %lend.1 = (f32[512,512]{1,0:T(8,128)}, f32[40,512]{1,0:T(8,128)S(1)}) custom-call(s32[5]{0:T(128)S(1)} %bitcast.53, s32[1]{0:T(128)S(6)} %copy.12.count.refs_1_, s32[1]{0:T(128)} %bitcast.core.refs_2_, s32[16]{0:T(128)S(1)} %copy-done.8, bf16[1,5,512,512]{3,2,1,0:T(8,128)(2,1)S(1)} %copy-done, f32[16,32,32]{2,1,0:T(8,128)S(1)} %copy-done.2, ...), custom_call_target="tpu_custom_call" | custom-call | tf_op jit(solution)/shard_map/lend/pallas_call | solution.py:186
  7.1 9.0 %collective-permute-start = (f32[512,512]{1,0:T(8,128)}, f32[512,512]{1,0:T(8,128)}, u32[]{:S(2)}, u32[]{:S(2)}) collective-permute-start(f32[512,512]{1,0:T(8,128)} %get-tuple-element.26), channel_id=1, source_target_pairs={{0,8},{8,0},{1,9},{9,1},{2,10},{10,2},{3,11},{11,3},{4,12},{12,4},... | collective-permute-start | bytes 3145736 | tf_op jit(solution)/shard_map/ppermute | solution.py:202
  16.1 0.0 copy-done.9
  16.1 2.6 %all-gather = f32[80,512]{1,0:T(8,128)S(1)} all-gather(f32[40,512]{1,0:T(8,128)S(1)} %get-tuple-element.25), channel_id=2, replica_groups=mesh['z'=16,'yhi'=2,'core'=2,'x'=4,'ylo'=2] {'core'}, dimensions={0}, use_global_device_ids=true | all-gather | bytes 245760 | tf_op jit(solution)/shard_map/all_gather | solution.py:203
  18.7 0.0 copy-done.5
  18.7 0.8 broadcast_in_dim.3
  19.6 3.5 %all-to-all-start = ((f32[8,32,512]{2,1,0:T(8,128)}), f32[8,32,512]{2,1,0:T(8,128)S(1)}, u32[]{:S(2)}, u32[]{:S(2)}) async-start(f32[8,32,512]{2,1,0:T(8,128)} %broadcast_in_dim.3), calls=%async_computation | async-start | bytes 1048576 | tf_op jit(solution)/shard_map/all_to_all | solution.py:206
  23.1 0.0 copy-done.3
  23.1 0.1 copy.10
  23.2 0.0 copy-done.10
  23.2 0.1 copy.11
  23.2 8.9 %all-to-all-done.gathered = f32[8,32,512]{2,1,0:T(8,128)S(1)} async-done(((f32[8,32,512]{2,1,0:T(8,128)}), f32[8,32,512]{2,1,0:T(8,128)S(1)}, u32[]{:S(2)}, u32[]{:S(2)}) %all-to-all-start) | async-done | bytes 524320 | tf_op jit(solution)/shard_map/all_to_all | solution.py:206
  32.2 0.0 collective-permute-done.borrowed
  32.2 1.7 %prepare.1 = (bf16[512,512]{1,0:T(8,128)(2,1)S(1)}, bf16[8,128,128]{2,1,0:T(8,128)(2,1)S(1)}, bf16[8,128,128]{2,1,0:T(8,128)(2,1)S(1)}, f32[2,512]{1,0:T(2,128)S...) custom-call(s32[1]{0:T(128)} %bitcast.core.refs_2_, f32[2,40,512]{2,1,0:T(8,128)S(1)} %bitcast.52, ...), custom_call_target="tpu_custom_call" | custom-call | tf_op jit(solution)/shard_map/prepare/pallas_call | solution.py:209
  33.9 0.0 copy-done.1
  33.9 0.0 copy-done.7
  33.9 1.3 %step_first.1 = (f32[64,512]{1,0:T(8,128)S(1)}, f32[64,512]{1,0:T(8,128)S(1)}) custom-call(s32[5]{0:T(128)S(1)} %bitcast.54, s32[1]{0:T(128)S(6)} %copy.12.count.refs_1_, s32[1]{0:T(128)} %bitcast.core.refs_2_, f32[64,512]{1,0:T(8,128)S(1)} %get-tuple-element.28.refs_3_, bf16[1,5,512,512]{3,2,1,0:T(8,128)(2,1)S(1)} %copy-done.1, ...), custom_call_target="tpu_custom_call" | custom-call | tf_op jit(solution)/shard_map/step_first/pallas_call | solution.py:231
  35.3 6.3 %all-gather.1 = f32[128,512]{1,0:T(8,128)S(1)} all-gather(f32[64,512]{1,0:T(8,128)S(1)} %get-tuple-element.34), channel_id=3, replica_groups={{8,17},{9,16},{10,19},{11,18},{12,21},{13,20},{14,23},{15,22},{24,33},{..., dimensions={0}, use_global_device_ids=true | all-gather | bytes 393216 | tf_op jit(solution)/shard_map/all_gather | solution.py:241
  41.6 6.6 %all-gather.2 = f32[128,512]{1,0:T(8,128)S(1)} all-gather(f32[64,512]{1,0:T(8,128)S(1)} %bitcast_add_fusion.5), channel_id=4, replica_groups=mesh['z'=16,'yhi'=2,'core'=2,'x'=4,'ylo'=2] {'core'}, dimensions={0}, use_global_device_ids=true | all-gather | bytes 393216 | tf_op jit(solution)/shard_map/all_gather | solution.py:243
  48.2 1.3 %step.5 = (f32[64,512]{1,0:T(8,128)S(1)}, f32[64,512]{1,0:T(8,128)S(1)}) custom-call(s32[5]{0:T(128)S(1)} %bitcast.55, s32[1]{0:T(128)S(6)} %copy.12.count.refs_1_, s32[1]{0:T(128)} %bitcast.core.refs_2_, f32[2,64,512]{2,1,0:T(8,128)S(1)} %bitcast.35, bf16[1,5,512,512]{3,2,1,0:T(8,128)(2,1)S(1)} %copy-done.1, ...), custom_call_target="tpu_custom_call" | custom-call | tf_op jit(solution)/shard_map/step/pallas_call | solution.py:231
  49.5 6.6 %all-gather.3 = f32[128,512]{1,0:T(8,128)S(1)} all-gather(f32[64,512]{1,0:T(8,128)S(1)} %get-tuple-element.36), channel_id=5, replica_groups={{8,17},{9,16},{10,19},{11,18},{12,21},{13,20},{14,23},{15,22},{24,33},{..., dimensions={0}, use_global_device_ids=true | all-gather | bytes 393216 | tf_op jit(solution)/shard_map/all_gather | solution.py:241
  56.1 4.3 %all-gather.4 = f32[128,512]{1,0:T(8,128)S(1)} all-gather(f32[64,512]{1,0:T(8,128)S(1)} %bitcast_add_fusion.4), channel_id=6, replica_groups=mesh['z'=16,'yhi'=2,'core'=2,'x'=4,'ylo'=2] {'core'}, dimensions={0}, use_global_device_ids=true | all-gather | bytes 393216 | tf_op jit(solution)/shard_map/all_gather | solution.py:243
  60.4 1.3 %step.6 = (f32[64,512]{1,0:T(8,128)S(1)}, f32[64,512]{1,0:T(8,128)S(1)}) custom-call(s32[5]{0:T(128)S(1)} %bitcast.56, s32[1]{0:T(128)S(6)} %copy.12.count.refs_1_, s32[1]{0:T(128)} %bitcast.core.refs_2_, f32[2,64,512]{2,1,0:T(8,128)S(1)} %bitcast.36, bf16[1,5,512,512]{3,2,1,0:T(8,128)(2,1)S(1)} %copy-done.1, ...), custom_call_target="tpu_custom_call" | custom-call | tf_op jit(solution)/shard_map/step/pallas_call | solution.py:231
  61.7 6.6 %all-gather.5 = f32[128,512]{1,0:T(8,128)S(1)} all-gather(f32[64,512]{1,0:T(8,128)S(1)} %get-tuple-element.38), channel_id=7, replica_groups={{8,17},{9,16},{10,19},{11,18},{12,21},{13,20},{14,23},{15,22},{24,33},{..., dimensions={0}, use_global_device_ids=true | all-gather | bytes 393216 | tf_op jit(solution)/shard_map/all_gather | solution.py:241
  68.3 3.8 %all-gather.6 = f32[128,512]{1,0:T(8,128)S(1)} all-gather(f32[64,512]{1,0:T(8,128)S(1)} %bitcast_add_fusion.3), channel_id=8, replica_groups=mesh['z'=16,'yhi'=2,'core'=2,'x'=4,'ylo'=2] {'core'}, dimensions={0}, use_global_device_ids=true | all-gather | bytes 393216 | tf_op jit(solution)/shard_map/all_gather | solution.py:243
  72.1 1.3 %step.7 = (f32[64,512]{1,0:T(8,128)S(1)}, f32[64,512]{1,0:T(8,128)S(1)}) custom-call(s32[5]{0:T(128)S(1)} %bitcast.57, s32[1]{0:T(128)S(6)} %copy.12.count.refs_1_, s32[1]{0:T(128)} %bitcast.core.refs_2_, f32[2,64,512]{2,1,0:T(8,128)S(1)} %bitcast.37, bf16[1,5,512,512]{3,2,1,0:T(8,128)(2,1)S(1)} %copy-done.1, ...), custom_call_target="tpu_custom_call" | custom-call | tf_op jit(solution)/shard_map/step/pallas_call | solution.py:231
  73.5 6.6 %all-gather.7 = f32[128,512]{1,0:T(8,128)S(1)} all-gather(f32[64,512]{1,0:T(8,128)S(1)} %get-tuple-element.40), channel_id=9, replica_groups={{8,17},{9,16},{10,19},{11,18},{12,21},{13,20},{14,23},{15,22},{24,33},{..., dimensions={0}, use_global_device_ids=true | all-gather | bytes 393216 | tf_op jit(solution)/shard_map/all_gather | solution.py:241
  80.1 3.8 %all-gather.8 = f32[128,512]{1,0:T(8,128)S(1)} all-gather(f32[64,512]{1,0:T(8,128)S(1)} %bitcast_add_fusion.2), channel_id=10, replica_groups=mesh['z'=16,'yhi'=2,'core'=2,'x'=4,'ylo'=2] {'core'}, dimensions={0}, use_global_device_ids=true | all-gather | bytes 393216 | tf_op jit(solution)/shard_map/all_gather | solution.py:243
  83.9 1.3 %step.8 = (f32[64,512]{1,0:T(8,128)S(1)}, f32[64,512]{1,0:T(8,128)S(1)}) custom-call(s32[5]{0:T(128)S(1)} %bitcast.58, s32[1]{0:T(128)S(6)} %copy.12.count.refs_1_, s32[1]{0:T(128)} %bitcast.core.refs_2_, f32[2,64,512]{2,1,0:T(8,128)S(1)} %bitcast.38, bf16[1,5,512,512]{3,2,1,0:T(8,128)(2,1)S(1)} %copy-done.1, ...), custom_call_target="tpu_custom_call" | custom-call | tf_op jit(solution)/shard_map/step/pallas_call | solution.py:231
  85.2 6.6 %all-gather.9 = f32[128,512]{1,0:T(8,128)S(1)} all-gather(f32[64,512]{1,0:T(8,128)S(1)} %get-tuple-element.42), channel_id=11, replica_groups={{8,17},{9,16},{10,19},{11,18},{12,21},{13,20},{14,23},{15,22},{24,33},{..., dimensions={0}, use_global_device_ids=true | all-gather | bytes 393216 | tf_op jit(solution)/shard_map/all_gather | solution.py:241
  91.8 3.8 %all-gather.10 = f32[128,512]{1,0:T(8,128)S(1)} all-gather(f32[64,512]{1,0:T(8,128)S(1)} %bitcast_add_fusion.1), channel_id=12, replica_groups=mesh['z'=16,'yhi'=2,'core'=2,'x'=4,'ylo'=2] {'core'}, dimensions={0}, use_global_device_ids=true | all-gather | bytes 393216 | tf_op jit(solution)/shard_map/all_gather | solution.py:243
  95.6 1.3 %step.9 = (f32[64,512]{1,0:T(8,128)S(1)}, f32[64,512]{1,0:T(8,128)S(1)}) custom-call(s32[5]{0:T(128)S(1)} %bitcast.59, s32[1]{0:T(128)S(6)} %copy.12.count.refs_1_, s32[1]{0:T(128)} %bitcast.core.refs_2_, f32[2,64,512]{2,1,0:T(8,128)S(1)} %bitcast.34, bf16[1,5,512,512]{3,2,1,0:T(8,128)(2,1)S(1)} %copy-done.1, ...), custom_call_target="tpu_custom_call" | custom-call | tf_op jit(solution)/shard_map/step/pallas_call | solution.py:231
  97.0 6.6 %all-gather.11 = f32[128,512]{1,0:T(8,128)S(1)} all-gather(f32[64,512]{1,0:T(8,128)S(1)} %get-tuple-element.44), channel_id=13, replica_groups={{8,17},{9,16},{10,19},{11,18},{12,21},{13,20},{14,23},{15,22},{24,33},{..., dimensions={0}, use_global_device_ids=true | all-gather | bytes 393216 | tf_op jit(solution)/shard_map/all_gather | solution.py:241
  103.5 3.8 %all-gather.12 = f32[128,512]{1,0:T(8,128)S(1)} all-gather(f32[64,512]{1,0:T(8,128)S(1)} %bitcast_add_fusion), channel_id=14, replica_groups=mesh['z'=16,'yhi'=2,'core'=2,'x'=4,'ylo'=2] {'core'}, dimensions={0}, use_global_device_ids=true | all-gather | bytes 393216 | tf_op jit(solution)/shard_map/all_gather | solution.py:243
  107.4 0.6 bitcast_multiply_fusion
  (14 shorter events, 0.2 us)
Async XLA Ops:
  0.0 18.7 %copy-start.5 = (f32[4,512]{1,0:T(4,128)S(1)}, f32[4,512]{1,0:T(4,128)}, u32[]{:S(2)}) copy-start(f32[4,512]{1,0:T(4,128)} %cotangent.1) | copy-start | bytes 24580
  0.7 1.7 %copy-start = (bf16[1,5,512,512]{3,2,1,0:T(8,128)(2,1)S(1)}, bf16[1,5,512,512]{3,2,1,0:T(8,128)(2,1)}, u32[]{:S(2)}) copy-start(bf16[1,5,512,512]{3,2,1,0:T(8,128)(2,1)} %refs_4_.11) | copy-start | bytes 7864324
  2.4 0.9 copy-start.2
  3.4 0.7 copy-start.4
  4.1 0.7 copy-start.6
  4.7 0.7 copy-start.8
  5.4 10.7 %copy-start.9 = (f32[6,4,512]{2,1,0:T(4,128)S(1)}, f32[6,4,512]{2,1,0:T(4,128)}, u32[]{:S(2)}) copy-start(f32[6,4,512]{2,1,0:T(4,128)} %param.10) | copy-start | bytes 147460
  5.4 17.7 %copy-start.3 = (f32[32,32]{1,0:T(8,128)S(1)}, f32[32,32]{1,0:T(8,128)}, u32[]{:S(2)}) copy-start(f32[32,32]{1,0:T(8,128)} %uptake_weight.1) | copy-start | bytes 12292
  5.4 17.8 %copy-start.10 = (f32[32,32]{1,0:T(8,128)S(1)}, f32[32,32]{1,0:T(8,128)}, u32[]{:S(2)}) copy-start(f32[32,32]{1,0:T(8,128)} %param.17) | copy-start | bytes 12292
  7.1 26.8 %copy-start.1 = (bf16[1,5,512,512]{3,2,1,0:T(8,128)(2,1)S(1)}, bf16[1,5,512,512]{3,2,1,0:T(8,128)(2,1)}, u32[]{:S(2)}) copy-start(bf16[1,5,512,512]{3,2,1,0:T(8,128)(2,1)} %refs_4_.11) | copy-start | bytes 7864324
  7.1 26.8 %copy-start.7 = (s32[1,5]{1,0:T(1,128)S(1)}, s32[1,5]{1,0:T(1,128)}, u32[]{:S(2)}) copy-start(s32[1,5]{1,0:T(1,128)} %param.14) | copy-start | bytes 64
  7.1 25.1 %collective-permute-start = (f32[512,512]{1,0:T(8,128)}, f32[512,512]{1,0:T(8,128)}, u32[]{:S(2)}, u32[]{:S(2)}) collective-permute-start(f32[512,512]{1,0:T(8,128)} %get-tuple-element.26), channel_id=1, source_target_pairs={{0,8},{8,0},{1,9},{9,1},{2,10},{10,2},{3,11},{11,3},{4,12},{12,4},... | collective-permute-start | bytes 3145736 | tf_op jit(solution)/shard_map/ppermute | solution.py:202
  19.6 12.6 %all-to-all-start = ((f32[8,32,512]{2,1,0:T(8,128)}), f32[8,32,512]{2,1,0:T(8,128)S(1)}, u32[]{:S(2)}, u32[]{:S(2)}) async-start(f32[8,32,512]{2,1,0:T(8,128)} %broadcast_in_dim.3), calls=%async_computation | async-start | bytes 1048576 | tf_op jit(solution)/shard_map/all_to_all | solution.py:206

commit v3 on v1

v3 whole, which is shorter than its diff:
```python
import jax
import jax.numpy as jnp
from jax import lax
from jax.experimental import pallas as pl
from jax.experimental.pallas import tpu as pltpu
from jax.sharding import Mesh, PartitionSpec as P


REGION = ("z", "yhi", "core")
TRACER = ("x", "ylo")
EVERY = REGION + TRACER
SPAN = 128
VMEM_LIMIT = 8 * 2**20


def device_at(sizes, chip, core, x, ylo):
    nq, nx, ny = sizes
    return (((chip % nq) * 2 + core) * nx + x) * ny + ylo


def neighbour_groups(sizes):
    nq, nx, ny = sizes
    return [
        [device_at(sizes, q, 1, x, yl), device_at(sizes, q + 1, 0, x, ny - 1 - yl)]
        for q in range(nq)
        for x in range(nx)
        for yl in range(ny)
    ]


def halves(value):
    high = value.astype(jnp.bfloat16)
    low = (value - high.astype(jnp.float32)).astype(jnp.bfloat16)
    return high, low


def dot(a, b):
    return lax.dot_general(a, b, (((1,), (0,)), ((), ())), preferred_element_type=jnp.float32)


def dot_split(a_high, a_low, b_high, b_low):
    rows = a_high.shape[0]
    both = dot(jnp.concatenate([a_high, a_low], axis=0), b_high)
    return both[:rows] + both[rows:] + dot(a_high, b_low)


def slot_at(offsets, distance):
    slots = offsets.shape[0]
    slot = jnp.int32(0)
    for k in range(slots):
        slot = slot + jnp.where(offsets[k] == distance, k, 0)
    return slot


def slot_live(offsets, count, distance):
    slots = offsets.shape[0]
    live = jnp.int32(0)
    for k in range(slots):
        live = live + jnp.where((offsets[k] == distance) & (k < count[0]), 1, 0)
    return live > 0


def away(core):
    return 2 * core[0] - 1


def lend_kernel(offsets, count, core, wet, tiles, inverse, lent, shared, buffer, arrival):
    distance = -2 * away(core)
    fetch = pltpu.make_async_copy(tiles.at[0, slot_at(offsets, distance)], buffer, arrival)
    fetch.start()
    columns, levels, _ = inverse.shape
    lane = lax.broadcasted_iota(jnp.int32, (levels, levels), 1)
    row = lax.broadcasted_iota(jnp.int32, (8, levels), 1)
    for c in range(columns):
        at = slice(c * levels, (c + 1) * levels)
        shared[0:levels, at] = jnp.where(lane < wet[c], inverse[c], 0.0)
        shared[levels : levels + 8, at] = jnp.where(row < wet[c], 1.0, 0.0)
    fetch.wait()
    live = slot_live(offsets, count, distance)
    lent[...] = jnp.where(live, buffer[...].astype(jnp.float32), 0.0)


def blocks_kernel(core, shared, borrowed, tile_out, block_high, block_low, wet_out):
    tile_out[...] = borrowed[...].astype(jnp.bfloat16)
    own = core[0]
    levels = shared.shape[1] - 8
    boxes = shared.shape[2]
    spans = boxes // SPAN
    same = (
        lax.broadcasted_iota(jnp.int32, (SPAN, SPAN), 0) // levels
        == lax.broadcasted_iota(jnp.int32, (SPAN, SPAN), 1) // levels
    )
    for which in range(2):
        side = own if which == 0 else 1 - own
        for s in range(spans):
            part = shared[side, 0:levels, s * SPAN : (s + 1) * SPAN]
            full = jnp.concatenate([part] * (SPAN // levels), axis=0)
            high, low = halves(jnp.where(same, full, 0.0))
            block_high[which * spans + s] = high
            block_low[which * spans + s] = low
        wet_out[which : which + 1, :] = shared[side, levels : levels + 1, :]


def gathered_kernel(gathered, uptake_weight, start, slopes):
    peers = gathered.shape[0]
    sections = slopes.shape[0]
    tracers = start.shape[0] // peers
    for t in range(peers):
        at = slice(t * tracers, (t + 1) * tracers)
        start[at, :] = gathered[t, 0:tracers, :]
        for n in range(sections):
            slopes[n, at, :] = gathered[t, (1 + n) * tracers : (2 + n) * tracers, :]
    weight_high, weight_low = halves(uptake_weight[...])
    for n in range(sections):
        state_high, state_low = halves(slopes[n])
        reach = jnp.tanh(dot_split(weight_high, weight_low, state_high, state_low))
        slopes[n] = 1.0 - reach * reach


def step_kernel(
    offsets, count, core, tracer, adjoint, tiles, borrowed, block_high, block_low, wet, slopes, uptake_t, release_t,
    send, keep, settled, rows,
    *, section, first, last,
):
    own = core[0]
    direction = away(core)
    boxes = tiles.shape[3]
    tracers = uptake_t.shape[0]
    spans = boxes // SPAN
    if first:
        pair = (adjoint[own], adjoint[1 - own])
    else:
        pair = (
            wet[0:1, :] * (adjoint[own, 0:tracers, :] + adjoint[1 - own, tracers:, :]),
            wet[1:2, :] * (adjoint[own, tracers:, :] + adjoint[1 - own, 0:tracers, :]),
        )
    for which in range(2):
        high, low = halves(pair[which])
        for s in range(spans):
            at = slice(s * SPAN, (s + 1) * SPAN)
            k = which * spans + s
            settled[which, :, at] = dot_split(high[:, at], low[:, at], block_high[k], block_low[k])
    own_high, own_low = halves(settled[0])
    other = settled[1].astype(jnp.bfloat16)

    def term(distance):
        product = dot(own_high, tiles[0, slot_at(offsets, distance)])
        return jnp.where(slot_live(offsets, count, distance), product, 0.0)

    def put(out, part, value, peer):
        if last:
            peers, few, _ = rows.shape
            for t in range(peers):
                rows[t] = value[t * few : (t + 1) * few]
            out[part * few : (part + 1) * few, :] = rows[peer]
        else:
            out[part * tracers : (part + 1) * tracers, :] = value

    put(send, 0, term(direction) + dot(other, borrowed[...]), tracer[1])
    put(send, 1, term(2 * direction), tracer[1])
    release_high, release_low = halves(release_t[...])
    pushed = slopes[section] * dot_split(release_high, release_low, own_high, own_low)
    pushed_high, pushed_low = halves(pushed)
    uptake_high, uptake_low = halves(uptake_t[...])
    put(keep, 0, term(0) + dot_split(uptake_high, uptake_low, pushed_high, pushed_low), tracer[0])
    put(keep, 1, term(-direction), tracer[0])


def local(
    cotangent,
    states,
    implicit_inverse,
    wet_levels,
    explicit_tiles,
    tile_offset,
    tile_count,
    uptake_weight,
    release_weight,
    *,
    sizes,
):
    tracers_here, boxes = cotangent.shape
    sections = states.shape[0]
    _, levels, _ = implicit_inverse.shape
    tracers = uptake_weight.shape[0]
    spans = boxes // SPAN
    peers = tracers // tracers_here
    f32, bf16 = jnp.float32, jnp.bfloat16
    shape = jax.ShapeDtypeStruct
    vmem = pl.BlockSpec(memory_space=pltpu.VMEM)
    smem = pl.BlockSpec(memory_space=pltpu.SMEM)
    core_index = lax.axis_index("core")
    core = core_index.astype(jnp.int32).reshape(1)
    here = lax.axis_index("x") * lax.axis_size("ylo")
    flip = lax.axis_index("ylo")
    tracer = jnp.stack([here + flip, here + lax.axis_size("ylo") - 1 - flip]).astype(jnp.int32)
    offsets = tile_offset.reshape(-1)
    groups = neighbour_groups(sizes)
    lean = pltpu.CompilerParams(vmem_limit_bytes=VMEM_LIMIT)

    outgoing = jnp.concatenate([cotangent, states.reshape(-1, boxes)], axis=0)
    copies = jnp.broadcast_to(outgoing, (peers, *outgoing.shape))
    gathered = lax.all_to_all(copies, TRACER, split_axis=0, concat_axis=0, tiled=True)
    lent, shared = pl.pallas_call(
        lend_kernel,
        in_specs=[smem] * 4 + [pl.BlockSpec(memory_space=pltpu.HBM), vmem],
        out_specs=[vmem] * 2,
        out_shape=[shape((boxes, boxes), f32), shape((levels + 8, boxes), f32)],
        scratch_shapes=[pltpu.VMEM((boxes, boxes), bf16), pltpu.SemaphoreType.DMA],
        compiler_params=lean,
        name="lend",
    )(offsets, tile_count, core, wet_levels, pltpu.with_memory_space_constraint(explicit_tiles, pltpu.HBM), implicit_inverse)
    borrowed = lax.ppermute(lent, "core", [(0, 1), (1, 0)])
    shared = lax.all_gather(shared, "core")
    borrowed, block_high, block_low, wet = pl.pallas_call(
        blocks_kernel,
        in_specs=[smem] + [vmem] * 2,
        out_specs=[vmem] * 4,
        out_shape=[
            shape((boxes, boxes), bf16),
            shape((2 * spans, SPAN, SPAN), bf16),
            shape((2 * spans, SPAN, SPAN), bf16),
            shape((2, boxes), f32),
        ],
        compiler_params=lean,
        name="blocks",
    )(core, shared, borrowed)
    start, slopes = pl.pallas_call(
        gathered_kernel,
        in_specs=[vmem] * 2,
        out_specs=[vmem] * 2,
        out_shape=[shape((tracers, boxes), f32), shape((sections, tracers, boxes), f32)],
        compiler_params=lean,
        name="gathered",
    )(gathered, uptake_weight)
    adjoint = lax.all_gather(start, "core")
    uptake_t, release_t = uptake_weight.T, release_weight.T
    for section in range(sections - 1, -1, -1):
        first, last = section == sections - 1, section == 0

        def step(*refs, section=section, first=first, last=last):
            step_kernel(*refs, section=section, first=first, last=last)

        exchanged = 2 * tracers_here if last else 2 * tracers
        send, keep = pl.pallas_call(
            step,
            in_specs=[smem] * 4 + [vmem] * 9,
            out_specs=[vmem] * 2,
            out_shape=[shape((exchanged, boxes), f32)] * 2,
            scratch_shapes=[pltpu.VMEM((2, tracers, boxes), f32), pltpu.VMEM((peers, tracers_here, boxes), f32)],
            compiler_params=lean,
        )(offsets, tile_count, core, tracer, adjoint, explicit_tiles, borrowed, block_high, block_low, wet,
          slopes, uptake_t, release_t)
        arrived = lax.all_gather(send, EVERY, axis_index_groups=groups)
        keep = keep + lax.dynamic_index_in_dim(arrived, core_index, 0, keepdims=False)
        adjoint = lax.all_gather(keep, "core")
    mine = lax.dynamic_index_in_dim(adjoint, core_index, 0, keepdims=False)[:tracers_here]
    theirs = lax.dynamic_index_in_dim(adjoint, 1 - core_index, 0, keepdims=False)[tracers_here:]
    return wet[0:1] * (mine + theirs)


def solution(mesh):
    regions, tracer_devices = mesh.devices.shape
    nq, nx, ny = regions // 2, tracer_devices // 2, 2
    fine = Mesh(mesh.devices.reshape(nq // 2, 2, 2, nx, ny), EVERY)
    placed = (
        P(TRACER, REGION),
        P(None, TRACER, REGION),
        P(REGION, None, None),
        P(REGION),
        P(REGION, None, None, None),
        P(REGION, None),
        P(REGION),
        P(),
        P(),
    )

    def body(*args):
        return local(*args, sizes=(nq, nx, ny))

    return jax.shard_map(body, mesh=fine, in_specs=placed, out_specs=P(TRACER, REGION), check_vma=False)
```

time: 131 us -> 106 us (0.81)
  Pallas kernels: 27.2 us -> 12.5 us
  other arithmetic: 6.17 us -> 0.78 us
  local copies, waits for them, and re-layouts: 6.51 us -> 3.3 us
  blocking collectives: 69.4 us -> 68 us
    pallas_call x8 -> x9, Pallas kernels: 27.2 us -> 12.5 us  [the longest x6 8.07 us: local(): pl.pallas_call(step, in_specs=[smem] * 4 + [vmem] * 9, out_specs=[vmem] *...]
    add x6, other arithmetic: 5.55 us -> 0.09 us  [local(): keep + lax.dynamic_index_in_dim(arrived, core_index, 0, keepdims=False)]
    all_gather x6, blocking collectives: 40.4 us -> 37.6 us  [local(): arrived = lax.all_gather(send, EVERY, axis_index_groups=groups)]
    all_gather x0 -> x1, blocking collectives: none -> 2.42 us  [local(): adjoint = lax.all_gather(start, 'core')]
    slice x2 -> x0, local copies, waits for them, and re-layouts: 1.77 us -> none  [the longest x1 1.76 us: local(): slopes[section:section + 1]]
    unnamed x16 -> x20, local copies, waits for them, and re-layouts: 3.15 us -> 2.42 us
  transfers between devices with their start and end apart: 2 -> 2, of which waited for: 1 -> 1; matrix products, arithmetic and copies ran while one was open for 2% -> 1% of each run, Pallas kernels for 0% -> 0%
where the time goes in v3:
time: 106 us; the launch traced here: 105 us
  blocking collectives  68 us (64%)
  Pallas kernels  12.5 us (12%)
  starting transfers between devices  12.5 us (12%)
  waiting for transfers between devices  7.34 us (7%)
  local copies, waits for them, and re-layouts  3.3 us (3%)
    all_gather x6, blocking collectives, local(): arrived = lax.all_gather(send, EVERY, axis_index_groups=groups)  37.6 us
    all_gather x6, blocking collectives, local(): adjoint = lax.all_gather(keep, 'core')  26.1 us
    ppermute x1, starting transfers between devices, local(): borrowed = lax.ppermute(lent, 'core', [(0, 1), (1, 0)])  9.01 us
    pallas_call x6, Pallas kernels, local(): pl.pallas_call(step, in_specs=[smem] * 4 + [vmem] * 9, out_specs=[vmem] *...  8.07 us
    all_to_all x1, waiting for transfers between devices, local(): lax.all_to_all(copies, TRACER, split_axis=0, concat_axis=0, tiled=True)  7.34 us
    all_to_all x1, starting transfers between devices, local(): lax.all_to_all(copies, TRACER, split_axis=0, concat_axis=0, tiled=True)  3.49 us
    pallas_call x1, Pallas kernels, local(): pl.pallas_call(lend_kernel, in_specs=[smem] * 4 + [pl.BlockSpec(memory_sp...  2.72 us
    unnamed x20, local copies, waits for them, and re-layouts  2.42 us
  transfers between devices with their start and end apart: 2, of which 1 were waited for; matrix products, arithmetic and copies ran while one was open for 1% of the time, Pallas kernels for 0%

profile of v3, /device:TPU:1, one launch (start us, length us, event | category | flops | bytes accessed | tf_op | source)
XLA Modules:
  0.0 105.3 jit_solution(9353321203716673028)
XLA Ops:
  0.0 0.0 copy-start.8
  0.7 0.0 copy-start.1
  0.7 0.9 copy-done.1
  1.6 0.0 copy-start.3
  1.6 0.7 copy-done.3
  2.3 0.0 copy-start.5
  2.3 0.7 copy-done.5
  2.9 0.0 copy-start.6
  2.9 2.7 %lend.1 = (f32[512,512]{1,0:T(8,128)}, f32[40,512]{1,0:T(8,128)S(1)}) custom-call(s32[5]{0:T(128)S(1)} %bitcast.56, s32[1]{0:T(128)S(6)} %copy.12.count.refs_1_, s32[1]{0:T(128)} %bitcast.core.refs_2_, s32[16]{0:T(128)S(1)} %copy-done.5, bf16[1,5,512,512]{3,2,1,0:T(8,128)(2,1)} %refs_5_.11, f32[16,32,32]{2,1,0:T(8,128)S(1)} %copy-done.1), custom_call_target="tpu_custom_call" | custom-call | tf_op jit(solution)/shard_map/lend/pallas_call | solution.py:204
  5.7 0.0 copy-start
  5.7 0.0 copy-start.4
  5.7 9.0 %collective-permute-start = (f32[512,512]{1,0:T(8,128)}, f32[512,512]{1,0:T(8,128)}, u32[]{:S(2)}, u32[]{:S(2)}) collective-permute-start(f32[512,512]{1,0:T(8,128)} %get-tuple-element.26), channel_id=1, source_target_pairs={{0,8},{8,0},{1,9},{9,1},{2,10},{10,2},{3,11},{11,3},{4,12},{12,4},... | collective-permute-start | bytes 3145736 | tf_op jit(solution)/shard_map/ppermute | solution.py:213
  14.7 0.0 copy-done.6
  14.7 0.0 copy-done.8
  14.8 0.9 broadcast_in_dim.3
  15.6 3.5 %all-to-all-start = ((f32[8,28,512]{2,1,0:T(8,128)}), f32[8,28,512]{2,1,0:T(8,128)S(1)}, u32[]{:S(2)}, u32[]{:S(2)}) async-start(f32[8,28,512]{2,1,0:T(8,128)} %broadcast_in_dim.3), calls=%async_computation | async-start | bytes 1048576 | tf_op jit(solution)/shard_map/all_to_all | solution.py:203
  19.1 0.0 copy-done.2
  19.1 0.1 copy.10
  19.2 0.0 copy-done.7
  19.2 0.1 copy.11
  19.3 1.9 %all-gather = f32[80,512]{1,0:T(8,128)S(1)} all-gather(f32[40,512]{1,0:T(8,128)S(1)} %get-tuple-element.25), channel_id=2, replica_groups=mesh['z'=16,'yhi'=2,'core'=2,'x'=4,'ylo'=2] {'core'}, dimensions={0}, use_global_device_ids=true | all-gather | bytes 245760 | tf_op jit(solution)/shard_map/all_gather | solution.py:214
  21.2 0.1 pad_add_fusion.refs_3_
  21.3 7.3 %all-to-all-done.gathered = f32[8,28,512]{2,1,0:T(8,128)S(1)} async-done(((f32[8,28,512]{2,1,0:T(8,128)}), f32[8,28,512]{2,1,0:T(8,128)S(1)}, u32[]{:S(2)}, u32[]{:S(2)}) %all-to-all-start) | async-done | bytes 458784 | tf_op jit(solution)/shard_map/all_to_all | solution.py:203
  28.6 0.3 gathered.1
  29.0 2.4 %all-gather.1 = f32[64,512]{1,0:T(8,128)S(1)} all-gather(f32[32,512]{1,0:T(8,128)S(1)} %get-tuple-element.28), channel_id=3, replica_groups=mesh['z'=16,'yhi'=2,'core'=2,'x'=4,'ylo'=2] {'core'}, dimensions={0}, use_global_device_ids=true | all-gather | bytes 196608 | tf_op jit(solution)/shard_map/all_gather | solution.py:236
  31.4 0.0 collective-permute-done.borrowed
  31.4 1.3 %blocks.1 = (bf16[512,512]{1,0:T(8,128)(2,1)S(1)}, bf16[8,128,128]{2,1,0:T(8,128)(2,1)S(1)}, bf16[8,128,128]{2,1,0:T(8,128)(2,1)S(1)}, f32[2,512]{1,0:T(2,128)S(1)}) custom-call(s32[1]{0:T(128)} %bitcast.core.refs_2_, f32[2,40,512]{2,1,0:T(8,128)S(1)} %bitcast.54, f32[512,512]{1,0:T(8,128)} %collective-permute-done.borrowed), custom_call_target="tpu_custom_call" | custom-call | tf_op jit(solution)/shard_map/blocks/pallas_call | solution.py:215
  32.8 0.0 copy-done
  32.8 0.0 copy-done.4
  32.8 1.3 %shard_map.91 = (f32[64,512]{1,0:T(8,128)S(1)}, f32[64,512]{1,0:T(8,128)S(1)}) custom-call(s32[5]{0:T(128)S(1)} %bitcast.57, s32[1]{0:T(128)S(6)} %copy.12.count.refs_1_, s32[1]{0:T(128)} %bitcast.core.refs_2_, s32[2]{0:T(128)S(1)} %pad_add_fusion.refs_3_, f32[2,32,512]{2,1,0:T(8,128)S(1)} %bitcast.55, bf16[1,5,512,512]{3,2,1,0:T(8,128)(2,1)S(1)} %copy-done, ...), custom_call_target="tpu_custom_call" | custom-call | tf_op jit(solution)/shard_map/pallas_call | solution.py:245
  34.1 6.3 %all-gather.2 = f32[128,512]{1,0:T(8,128)S(1)} all-gather(f32[64,512]{1,0:T(8,128)S(1)} %get-tuple-element.34), channel_id=4, replica_groups={{8,17},{9,16},{10,19},{11,18},{12,21},{13,20},{14,23},{15,22},{24,33},{..., dimensions={0}, use_global_device_ids=true | all-gather | bytes 393216 | tf_op jit(solution)/shard_map/all_gather | solution.py:254
  40.4 6.9 %all-gather.3 = f32[128,512]{1,0:T(8,128)S(1)} all-gather(f32[64,512]{1,0:T(8,128)S(1)} %bitcast_add_fusion.4), channel_id=5, replica_groups=mesh['z'=16,'yhi'=2,'core'=2,'x'=4,'ylo'=2] {'core'}, dimensions={0}, use_global_device_ids=true | all-gather | bytes 393216 | tf_op jit(solution)/shard_map/all_gather | solution.py:256
  47.3 1.3 %shard_map.92 = (f32[64,512]{1,0:T(8,128)S(1)}, f32[64,512]{1,0:T(8,128)S(1)}) custom-call(s32[5]{0:T(128)S(1)} %bitcast.58, s32[1]{0:T(128)S(6)} %copy.12.count.refs_1_, s32[1]{0:T(128)} %bitcast.core.refs_2_, s32[2]{0:T(128)S(1)} %pad_add_fusion.refs_3_, f32[2,64,512]{2,1,0:T(8,128)S(1)} %bitcast.38, bf16[1,5,512,512]{3,2,1,0:T(8,128)(2,1)S(1)} %copy-done, ...), custom_call_target="tpu_custom_call" | custom-call | tf_op jit(solution)/shard_map/pallas_call | solution.py:245
  48.6 6.6 %all-gather.4 = f32[128,512]{1,0:T(8,128)S(1)} all-gather(f32[64,512]{1,0:T(8,128)S(1)} %get-tuple-element.36), channel_id=6, replica_groups={{8,17},{9,16},{10,19},{11,18},{12,21},{13,20},{14,23},{15,22},{24,33},{..., dimensions={0}, use_global_device_ids=true | all-gather | bytes 393216 | tf_op jit(solution)/shard_map/all_gather | solution.py:254
  55.2 3.8 %all-gather.5 = f32[128,512]{1,0:T(8,128)S(1)} all-gather(f32[64,512]{1,0:T(8,128)S(1)} %bitcast_add_fusion.3), channel_id=7, replica_groups=mesh['z'=16,'yhi'=2,'core'=2,'x'=4,'ylo'=2] {'core'}, dimensions={0}, use_global_device_ids=true | all-gather | bytes 393216 | tf_op jit(solution)/shard_map/all_gather | solution.py:256
  59.0 1.3 %shard_map.93 = (f32[64,512]{1,0:T(8,128)S(1)}, f32[64,512]{1,0:T(8,128)S(1)}) custom-call(s32[5]{0:T(128)S(1)} %bitcast.59, s32[1]{0:T(128)S(6)} %copy.12.count.refs_1_, s32[1]{0:T(128)} %bitcast.core.refs_2_, s32[2]{0:T(128)S(1)} %pad_add_fusion.refs_3_, f32[2,64,512]{2,1,0:T(8,128)S(1)} %bitcast.39, bf16[1,5,512,512]{3,2,1,0:T(8,128)(2,1)S(1)} %copy-done, ...), custom_call_target="tpu_custom_call" | custom-call | tf_op jit(solution)/shard_map/pallas_call | solution.py:245
  60.4 6.6 %all-gather.6 = f32[128,512]{1,0:T(8,128)S(1)} all-gather(f32[64,512]{1,0:T(8,128)S(1)} %get-tuple-element.38), channel_id=8, replica_groups={{8,17},{9,16},{10,19},{11,18},{12,21},{13,20},{14,23},{15,22},{24,33},{..., dimensions={0}, use_global_device_ids=true | all-gather | bytes 393216 | tf_op jit(solution)/shard_map/all_gather | solution.py:254
  67.0 3.8 %all-gather.7 = f32[128,512]{1,0:T(8,128)S(1)} all-gather(f32[64,512]{1,0:T(8,128)S(1)} %bitcast_add_fusion.2), channel_id=9, replica_groups=mesh['z'=16,'yhi'=2,'core'=2,'x'=4,'ylo'=2] {'core'}, dimensions={0}, use_global_device_ids=true | all-gather | bytes 393216 | tf_op jit(solution)/shard_map/all_gather | solution.py:256
  70.8 1.3 %shard_map.94 = (f32[64,512]{1,0:T(8,128)S(1)}, f32[64,512]{1,0:T(8,128)S(1)}) custom-call(s32[5]{0:T(128)S(1)} %bitcast.60, s32[1]{0:T(128)S(6)} %copy.12.count.refs_1_, s32[1]{0:T(128)} %bitcast.core.refs_2_, s32[2]{0:T(128)S(1)} %pad_add_fusion.refs_3_, f32[2,64,512]{2,1,0:T(8,128)S(1)} %bitcast.40, bf16[1,5,512,512]{3,2,1,0:T(8,128)(2,1)S(1)} %copy-done, ...), custom_call_target="tpu_custom_call" | custom-call | tf_op jit(solution)/shard_map/pallas_call | solution.py:245
  72.1 6.6 %all-gather.8 = f32[128,512]{1,0:T(8,128)S(1)} all-gather(f32[64,512]{1,0:T(8,128)S(1)} %get-tuple-element.40), channel_id=10, replica_groups={{8,17},{9,16},{10,19},{11,18},{12,21},{13,20},{14,23},{15,22},{24,33},{..., dimensions={0}, use_global_device_ids=true | all-gather | bytes 393216 | tf_op jit(solution)/shard_map/all_gather | solution.py:254
  78.7 3.8 %all-gather.9 = f32[128,512]{1,0:T(8,128)S(1)} all-gather(f32[64,512]{1,0:T(8,128)S(1)} %bitcast_add_fusion.1), channel_id=11, replica_groups=mesh['z'=16,'yhi'=2,'core'=2,'x'=4,'ylo'=2] {'core'}, dimensions={0}, use_global_device_ids=true | all-gather | bytes 393216 | tf_op jit(solution)/shard_map/all_gather | solution.py:256
  82.5 1.3 %shard_map.95 = (f32[64,512]{1,0:T(8,128)S(1)}, f32[64,512]{1,0:T(8,128)S(1)}) custom-call(s32[5]{0:T(128)S(1)} %bitcast.61, s32[1]{0:T(128)S(6)} %copy.12.count.refs_1_, s32[1]{0:T(128)} %bitcast.core.refs_2_, s32[2]{0:T(128)S(1)} %pad_add_fusion.refs_3_, f32[2,64,512]{2,1,0:T(8,128)S(1)} %bitcast.41, bf16[1,5,512,512]{3,2,1,0:T(8,128)(2,1)S(1)} %copy-done, ...), custom_call_target="tpu_custom_call" | custom-call | tf_op jit(solution)/shard_map/pallas_call | solution.py:245
  83.9 6.6 %all-gather.10 = f32[128,512]{1,0:T(8,128)S(1)} all-gather(f32[64,512]{1,0:T(8,128)S(1)} %get-tuple-element.42), channel_id=12, replica_groups={{8,17},{9,16},{10,19},{11,18},{12,21},{13,20},{14,23},{15,22},{24,33},{..., dimensions={0}, use_global_device_ids=true | all-gather | bytes 393216 | tf_op jit(solution)/shard_map/all_gather | solution.py:254
  90.5 3.8 %all-gather.11 = f32[128,512]{1,0:T(8,128)S(1)} all-gather(f32[64,512]{1,0:T(8,128)S(1)} %bitcast_add_fusion), channel_id=13, replica_groups=mesh['z'=16,'yhi'=2,'core'=2,'x'=4,'ylo'=2] {'core'}, dimensions={0}, use_global_device_ids=true | all-gather | bytes 393216 | tf_op jit(solution)/shard_map/all_gather | solution.py:256
  94.3 1.4 %shard_map.96 = (f32[8,512]{1,0:T(8,128)S(1)}, f32[8,512]{1,0:T(8,128)S(1)}) custom-call(s32[5]{0:T(128)S(1)} %bitcast.62, s32[1]{0:T(128)S(6)} %copy.12.count.refs_1_, s32[1]{0:T(128)} %bitcast.core.refs_2_, s32[2]{0:T(128)S(1)} %pad_add_fusion.refs_3_, f32[2,64,512]{2,1,0:T(8,128)S(1)} %bitcast.37, bf16[1,5,512,512]{3,2,1,0:T(8,128)(2,1)S(1)} %copy-done, ...), custom_call_target="tpu_custom_call" | custom-call | tf_op jit(solution)/shard_map/pallas_call | solution.py:245
  95.6 5.1 %all-gather.12 = f32[16,512]{1,0:T(8,128)S(1)} all-gather(f32[8,512]{1,0:T(8,128)S(1)} %get-tuple-element.44), channel_id=14, replica_groups={{8,17},{9,16},{10,19},{11,18},{12,21},{13,20},{14,23},{15,22},{24,33},{..., dimensions={0}, use_global_device_ids=true | all-gather | bytes 49152 | tf_op jit(solution)/shard_map/all_gather | solution.py:254
  100.7 4.0 %all-gather.13 = f32[16,512]{1,0:T(8,128)S(1)} all-gather(f32[8,512]{1,0:T(8,128)S(1)} %bitcast_add_fusion.5), channel_id=15, replica_groups=mesh['z'=16,'yhi'=2,'core'=2,'x'=4,'ylo'=2] {'core'}, dimensions={0}, use_global_device_ids=true | all-gather | bytes 49152 | tf_op jit(solution)/shard_map/all_gather | solution.py:256
  104.7 0.6 fusion.1
  (11 shorter events, 0.1 us)
Async XLA Ops:
  0.0 14.7 %copy-start.8 = (f32[4,512]{1,0:T(4,128)S(1)}, f32[4,512]{1,0:T(4,128)}, u32[]{:S(2)}) copy-start(f32[4,512]{1,0:T(4,128)} %param.9) | copy-start | bytes 24580
  0.7 1.0 copy-start.1
  1.6 0.7 copy-start.3
  2.3 0.7 copy-start.5
  2.9 11.8 %copy-start.6 = (f32[6,4,512]{2,1,0:T(4,128)S(1)}, f32[6,4,512]{2,1,0:T(4,128)}, u32[]{:S(2)}) copy-start(f32[6,4,512]{2,1,0:T(4,128)} %param.10) | copy-start | bytes 147460
  2.9 16.2 %copy-start.2 = (f32[32,32]{1,0:T(8,128)S(1)}, f32[32,32]{1,0:T(8,128)}, u32[]{:S(2)}) copy-start(f32[32,32]{1,0:T(8,128)} %uptake_weight.1) | copy-start | bytes 12292
  2.9 16.3 %copy-start.7 = (f32[32,32]{1,0:T(8,128)S(1)}, f32[32,32]{1,0:T(8,128)}, u32[]{:S(2)}) copy-start(f32[32,32]{1,0:T(8,128)} %param.17) | copy-start | bytes 12292
  5.7 27.1 %copy-start = (bf16[1,5,512,512]{3,2,1,0:T(8,128)(2,1)S(1)}, bf16[1,5,512,512]{3,2,1,0:T(8,128)(2,1)}, u32[]{:S(2)}) copy-start(bf16[1,5,512,512]{3,2,1,0:T(8,128)(2,1)} %refs_5_.11) | copy-start | bytes 7864324
  5.7 27.1 %copy-start.4 = (s32[1,5]{1,0:T(1,128)S(1)}, s32[1,5]{1,0:T(1,128)}, u32[]{:S(2)}) copy-start(s32[1,5]{1,0:T(1,128)} %param.14) | copy-start | bytes 64
  5.7 25.7 %collective-permute-start = (f32[512,512]{1,0:T(8,128)}, f32[512,512]{1,0:T(8,128)}, u32[]{:S(2)}, u32[]{:S(2)}) collective-permute-start(f32[512,512]{1,0:T(8,128)} %get-tuple-element.26), channel_id=1, source_target_pairs={{0,8},{8,0},{1,9},{9,1},{2,10},{10,2},{3,11},{11,3},{4,12},{12,4},... | collective-permute-start | bytes 3145736 | tf_op jit(solution)/shard_map/ppermute | solution.py:213
  15.6 13.0 %all-to-all-start = ((f32[8,28,512]{2,1,0:T(8,128)}), f32[8,28,512]{2,1,0:T(8,128)S(1)}, u32[]{:S(2)}, u32[]{:S(2)}) async-start(f32[8,28,512]{2,1,0:T(8,128)} %broadcast_in_dim.3), calls=%async_computation | async-start | bytes 1048576 | tf_op jit(solution)/shard_map/all_to_all | solution.py:203

commit v4 on v3

v4 whole, which is shorter than its diff:
```python
import jax
import jax.numpy as jnp
from jax import lax
from jax.experimental import pallas as pl
from jax.experimental.pallas import tpu as pltpu
from jax.sharding import Mesh, PartitionSpec as P


REGION = ("z", "yhi", "core")
TRACER = ("x", "ylo")
EVERY = REGION + TRACER
SPAN = 128
VMEM_LIMIT = 8 * 2**20
OFFSETS_AT, COUNT_AT, CORE_AT, X_AT, WET_AT = 0, 5, 6, 7, 8


def neighbour_groups(sizes):
    nq, nx, ny = sizes

    def at(chip, core, x, ylo):
        return (((chip % nq) * 2 + core) * nx + x) * ny + ylo

    groups = []
    for q in range(nq):
        for x in range(nx):
            joined, alone = (1, 0) if q % 2 == 0 else (0, 1)
            groups.append([at(q, 1, x, joined), at(q + 1, 0, x, 1 - joined)])
            groups.append([at(q, 1, x, alone), at(q, 0, x, alone)])
    return groups


def halves(value):
    high = value.astype(jnp.bfloat16)
    low = (value - high.astype(jnp.float32)).astype(jnp.bfloat16)
    return high, low


def dot(a, b):
    return lax.dot_general(a, b, (((1,), (0,)), ((), ())), preferred_element_type=jnp.float32)


def dot_split(a_high, a_low, b_high, b_low):
    rows = a_high.shape[0]
    both = dot(jnp.concatenate([a_high, a_low], axis=0), b_high)
    return both[:rows] + both[rows:] + dot(a_high, b_low)


def slot_at(facts, slots, distance):
    slot = jnp.int32(0)
    for k in range(slots):
        slot = slot + jnp.where(facts[OFFSETS_AT + k] == distance, k, 0)
    return slot


def slot_live(facts, slots, distance):
    live = jnp.int32(0)
    for k in range(slots):
        live = live + jnp.where((facts[OFFSETS_AT + k] == distance) & (k < facts[COUNT_AT]), 1, 0)
    return live > 0


def away(facts):
    return 2 * facts[CORE_AT] - 1


def pack_kernel(cotangent, states, copies, buffer, fetched, sent):
    first = pltpu.make_async_copy(cotangent, buffer.at[0], fetched.at[0])
    rest = pltpu.make_async_copy(states, buffer.at[pl.ds(1, states.shape[0])], fetched.at[1])
    first.start()
    rest.start()
    first.wait()
    rest.wait()
    sends = [pltpu.make_async_copy(buffer, copies.at[t], sent.at[t]) for t in range(copies.shape[0])]
    for send in sends:
        send.start()
    for send in sends:
        send.wait()


def lend_kernel(facts, tiles, lent, buffer, arrival):
    slots = tiles.shape[1]
    distance = -2 * away(facts)
    fetch = pltpu.make_async_copy(tiles.at[0, slot_at(facts, slots, distance)], buffer, arrival)
    fetch.start()
    fetch.wait()
    lent[...] = jnp.where(slot_live(facts, slots, distance), buffer[...].astype(jnp.float32), 0.0)


def share_kernel(facts, inverse_hbm, shared, inverse, arrival):
    fetch = pltpu.make_async_copy(inverse_hbm, inverse, arrival)
    fetch.start()
    fetch.wait()
    columns, levels, _ = inverse.shape
    lane = lax.broadcasted_iota(jnp.int32, (levels, levels), 1)
    row = lax.broadcasted_iota(jnp.int32, (8, levels), 1)
    for c in range(columns):
        at = slice(c * levels, (c + 1) * levels)
        shared[0:levels, at] = jnp.where(lane < facts[WET_AT + c], inverse[c], 0.0)
        shared[levels : levels + 8, at] = jnp.where(row < facts[WET_AT + c], 1.0, 0.0)


def blocks_kernel(facts, shared, borrowed, tile_out, blocks, wet_out):
    own = facts[CORE_AT]
    levels = shared.shape[1] - 8
    boxes = shared.shape[2]
    spans = boxes // SPAN
    same = (
        lax.broadcasted_iota(jnp.int32, (SPAN, SPAN), 0) // levels
        == lax.broadcasted_iota(jnp.int32, (SPAN, SPAN), 1) // levels
    )
    for which in range(2):
        side = own if which == 0 else 1 - own
        for s in range(spans):
            part = shared[side, 0:levels, s * SPAN : (s + 1) * SPAN]
            full = jnp.concatenate([part] * (SPAN // levels), axis=0)
            high, low = halves(jnp.where(same, full, 0.0))
            blocks[0, which * spans + s] = high
            blocks[1, which * spans + s] = low
        wet_out[which : which + 1, :] = shared[side, levels : levels + 1, :]
    tile_out[...] = borrowed[...].astype(jnp.bfloat16)


def gathered_kernel(gathered, uptake_weight, start, slopes):
    peers, _, few, _ = gathered.shape
    for t in range(peers):
        at = slice(t * few, (t + 1) * few)
        start[at, :] = gathered[t, 0]
        for n in range(slopes.shape[0]):
            slopes[n, at, :] = gathered[t, 1 + n]
    weight_high, weight_low = halves(uptake_weight[...])
    for n in range(slopes.shape[0]):
        state_high, state_low = halves(slopes[n])
        reach = jnp.tanh(dot_split(weight_high, weight_low, state_high, state_low))
        slopes[n] = 1.0 - reach * reach


def step_kernel(
    facts, adjoint, tiles, borrowed, blocks, wet, slopes, uptake_t, release_t, send, keep, settled, rows,
    *, section, first, last,
):
    own = facts[CORE_AT]
    direction = away(facts)
    slots, boxes = tiles.shape[1], tiles.shape[3]
    tracers = uptake_t.shape[0]
    spans = boxes // SPAN
    if first:
        pair = (adjoint[own], adjoint[1 - own])
    else:
        pair = (
            wet[0:1, :] * (adjoint[own, 0:tracers, :] + adjoint[1 - own, tracers:, :]),
            wet[1:2, :] * (adjoint[own, tracers:, :] + adjoint[1 - own, 0:tracers, :]),
        )
    for which in range(2):
        high, low = halves(pair[which])
        for s in range(spans):
            at = slice(s * SPAN, (s + 1) * SPAN)
            k = which * spans + s
            settled[which, :, at] = dot_split(high[:, at], low[:, at], blocks[0, k], blocks[1, k])
    own_high, own_low = halves(settled[0])
    other = settled[1].astype(jnp.bfloat16)

    def term(distance):
        product = dot(own_high, tiles[0, slot_at(facts, slots, distance)])
        return jnp.where(slot_live(facts, slots, distance), product, 0.0)

    def put(out, part, value):
        few = out.shape[0] // 2
        if last:
            for x in range(rows.shape[0]):
                rows[x] = value[x * few : (x + 1) * few]
            value = rows[facts[X_AT]]
        out[part * few : (part + 1) * few, :] = value

    put(send, 0, term(direction) + dot(other, borrowed[...]))
    put(send, 1, term(2 * direction))
    release_high, release_low = halves(release_t[...])
    pushed = slopes[section] * dot_split(release_high, release_low, own_high, own_low)
    pushed_high, pushed_low = halves(pushed)
    uptake_high, uptake_low = halves(uptake_t[...])
    put(keep, 0, term(0) + dot_split(uptake_high, uptake_low, pushed_high, pushed_low))
    put(keep, 1, term(-direction))


def local(
    cotangent,
    states,
    implicit_inverse,
    wet_levels,
    explicit_tiles,
    tile_offset,
    tile_count,
    uptake_weight,
    release_weight,
    *,
    sizes,
):
    tracers_here, boxes = cotangent.shape
    sections = states.shape[0]
    columns, levels, _ = implicit_inverse.shape
    tracers = uptake_weight.shape[0]
    spans = boxes // SPAN
    peers = tracers // tracers_here
    f32, bf16 = jnp.float32, jnp.bfloat16
    shape = jax.ShapeDtypeStruct
    vmem = pl.BlockSpec(memory_space=pltpu.VMEM)
    smem = pl.BlockSpec(memory_space=pltpu.SMEM)
    hbm = pl.BlockSpec(memory_space=pltpu.HBM)
    lean = pltpu.CompilerParams(vmem_limit_bytes=VMEM_LIMIT)
    dma = pltpu.SemaphoreType.DMA
    core_index = lax.axis_index("core")
    x_index = lax.axis_index("x")
    ylo_index = lax.axis_index("ylo")
    ylo_size = lax.axis_size("ylo")
    joined = lax.axis_index("yhi") + ylo_index == 1
    groups = neighbour_groups(sizes)

    def in_hbm(array):
        return pltpu.with_memory_space_constraint(array, pltpu.HBM)

    copies = pl.pallas_call(
        pack_kernel,
        in_specs=[hbm] * 2,
        out_specs=hbm,
        out_shape=shape((peers, 1 + sections, tracers_here, boxes), f32),
        scratch_shapes=[pltpu.VMEM((1 + sections, tracers_here, boxes), f32), dma((2,)), dma((peers,))],
        compiler_params=lean,
        name="pack",
    )(in_hbm(cotangent), in_hbm(states))
    gathered = lax.all_to_all(copies, TRACER, split_axis=0, concat_axis=0, tiled=True)
    facts = jnp.concatenate(
        [tile_offset.reshape(-1), tile_count, jnp.stack([core_index, x_index]).astype(jnp.int32), wet_levels]
    )
    lent = pl.pallas_call(
        lend_kernel,
        in_specs=[smem, hbm],
        out_specs=vmem,
        out_shape=shape((boxes, boxes), f32),
        scratch_shapes=[pltpu.VMEM((boxes, boxes), bf16), dma],
        compiler_params=lean,
        name="lend",
    )(facts, in_hbm(explicit_tiles))
    borrowed = lax.ppermute(lent, "core", [(0, 1), (1, 0)])
    shared = pl.pallas_call(
        share_kernel,
        in_specs=[smem, hbm],
        out_specs=vmem,
        out_shape=shape((levels + 8, boxes), f32),
        scratch_shapes=[pltpu.VMEM((columns, levels, levels), f32), dma],
        compiler_params=lean,
        name="share",
    )(facts, in_hbm(implicit_inverse))
    shared = lax.all_gather(shared, "core")
    borrowed, blocks, wet = pl.pallas_call(
        blocks_kernel,
        in_specs=[smem] + [vmem] * 2,
        out_specs=[vmem] * 3,
        out_shape=[shape((boxes, boxes), bf16), shape((2, 2 * spans, SPAN, SPAN), bf16), shape((2, boxes), f32)],
        compiler_params=lean,
        name="blocks",
    )(facts, shared, borrowed)
    start, slopes = pl.pallas_call(
        gathered_kernel,
        in_specs=[vmem] * 2,
        out_specs=[vmem] * 2,
        out_shape=[shape((tracers, boxes), f32), shape((sections, tracers, boxes), f32)],
        compiler_params=lean,
        name="gathered",
    )(gathered, uptake_weight)
    adjoint = lax.all_gather(start, "core")
    uptake_t, release_t = uptake_weight.T, release_weight.T
    last_rows = ylo_size * tracers_here
    for section in range(sections - 1, -1, -1):
        first, last = section == sections - 1, section == 0

        def step(*refs, section=section, first=first, last=last):
            step_kernel(*refs, section=section, first=first, last=last)

        exchanged = 2 * last_rows if last else 2 * tracers
        send, keep = pl.pallas_call(
            step,
            in_specs=[smem] + [vmem] * 8,
            out_specs=[vmem] * 2,
            out_shape=[shape((exchanged, boxes), f32)] * 2,
            scratch_shapes=[
                pltpu.VMEM((2, tracers, boxes), f32),
                pltpu.VMEM((tracers // last_rows, last_rows, boxes), f32),
            ],
            compiler_params=lean,
        )(facts, adjoint, explicit_tiles, borrowed, blocks, wet, slopes, uptake_t, release_t)
        arrived = lax.all_gather(send, EVERY, axis_index_groups=groups)
        keep = keep + lax.dynamic_index_in_dim(arrived, core_index, 0, keepdims=False)
        adjoint = lax.all_gather(keep, "core")
    mine = lax.dynamic_index_in_dim(adjoint, core_index, 0, keepdims=False)[:last_rows]
    theirs = lax.dynamic_index_in_dim(adjoint, 1 - core_index, 0, keepdims=False)[last_rows:]
    result = (wet[0:1] * (mine + theirs)).reshape(ylo_size, tracers_here, boxes)
    passed = lax.dynamic_index_in_dim(result, 1 - ylo_index, 0, keepdims=False)
    passed = lax.dynamic_index_in_dim(lax.all_gather(passed, "ylo"), 1 - ylo_index, 0, keepdims=False)
    return jnp.where(joined, lax.dynamic_index_in_dim(result, ylo_index, 0, keepdims=False), passed)


def solution(mesh):
    regions, tracer_devices = mesh.devices.shape
    nq, nx, ny = regions // 2, tracer_devices // 2, 2
    fine = Mesh(mesh.devices.reshape(nq // 2, 2, 2, nx, ny), EVERY)
    placed = (
        P(TRACER, REGION),
        P(None, TRACER, REGION),
        P(REGION, None, None),
        P(REGION),
        P(REGION, None, None, None),
        P(REGION, None),
        P(REGION),
        P(),
        P(),
    )

    def body(*args):
        return local(*args, sizes=(nq, nx, ny))

    return jax.shard_map(body, mesh=fine, in_specs=placed, out_specs=P(TRACER, REGION), check_vma=False)
```

time: 106 us -> 100 us (0.943)
  blocking collectives: 68 us -> 63.6 us
  Pallas kernels: 12.5 us -> 15.7 us
  local copies, waits for them, and re-layouts: 3.3 us -> 0.93 us
  waiting for transfers between devices: 7.34 us -> 5.06 us
    all_gather x0 -> x1, blocking collectives: none -> 35.7 us  [local(): lax.all_gather(passed, 'ylo')]
    all_gather x6, blocking collectives: 37.6 us -> 11.8 us  [local(): arrived = lax.all_gather(send, EVERY, axis_index_groups=groups)]
    all_gather x6, blocking collectives: 26.1 us -> 11.8 us  [local(): adjoint = lax.all_gather(keep, 'core')]
    pallas_call x7 -> x9, Pallas kernels: 10.8 us -> 14 us  [the longest x6 8.02 us: local(): pl.pallas_call(step, in_specs=[smem] + [vmem] * 8, out_specs=[vmem] * 2,...]
    all_to_all x1, waiting for transfers between devices: 7.34 us -> 5.06 us  [local(): lax.all_to_all(copies, TRACER, split_axis=0, concat_axis=0, tiled=True)]
    unnamed x20 -> x8, local copies, waits for them, and re-layouts: 2.42 us -> 0.16 us
  transfers between devices with their start and end apart: 2 -> 2, of which waited for: 1 -> 1; matrix products, arithmetic and copies ran while one was open for 1% -> 0% of each run, Pallas kernels for 0% -> 4%
where the time goes in v4:
time: 100 us; the launch traced here: 99.3 us
  blocking collectives  63.6 us (64%)
  Pallas kernels  15.7 us (16%)
  starting transfers between devices  12.5 us (12%)
  waiting for transfers between devices  5.06 us (5%)
    all_gather x1, blocking collectives, local(): lax.all_gather(passed, 'ylo')  35.7 us
    all_gather x6, blocking collectives, local(): adjoint = lax.all_gather(keep, 'core')  11.8 us
    all_gather x6, blocking collectives, local(): arrived = lax.all_gather(send, EVERY, axis_index_groups=groups)  11.8 us
    ppermute x1, starting transfers between devices, local(): borrowed = lax.ppermute(lent, 'core', [(0, 1), (1, 0)])  9.01 us
    pallas_call x6, Pallas kernels, local(): pl.pallas_call(step, in_specs=[smem] + [vmem] * 8, out_specs=[vmem] * 2,...  8.02 us
    all_to_all x1, waiting for transfers between devices, local(): lax.all_to_all(copies, TRACER, split_axis=0, concat_axis=0, tiled=True)  5.06 us
    all_to_all x1, starting transfers between devices, local(): lax.all_to_all(copies, TRACER, split_axis=0, concat_axis=0, tiled=True)  3.48 us
    pallas_call x1, Pallas kernels, local(): pl.pallas_call(lend_kernel, in_specs=[smem, hbm], out_specs=vmem, out_sha...  2.65 us
  transfers between devices with their start and end apart: 2, of which 1 were waited for; matrix products, arithmetic and copies ran while one was open for 0% of the time, Pallas kernels for 4%

profile of v4, /device:TPU:1, one launch (start us, length us, event | category | flops | bytes accessed | tf_op | source)
XLA Modules:
  0.0 99.3 jit_solution(12311895861906882453)
XLA Ops:
  0.7 0.8 concatenate.3.facts.refs_0_
  1.4 0.0 copy-start.1
  1.4 0.0 copy-start.2
  1.4 2.7 %lend.1 = f32[512,512]{1,0:T(8,128)} custom-call(s32[24]{0:T(128)S(1)} %concatenate.3.facts.refs_0_, bf16[1,5,512,512]{3,2,1,0:T(8,128)(2,1)} %refs_2_.11), custom_call_target="tpu_custom_call" | custom-call | tf_op jit(solution)/shard_map/lend/pallas_call | solution.py:233
  4.1 0.0 copy-start
  4.1 9.0 %collective-permute-start = (f32[512,512]{1,0:T(8,128)}, f32[512,512]{1,0:T(8,128)}, u32[]{:S(2)}, u32[]{:S(2)}) collective-permute-start(f32[512,512]{1,0:T(8,128)} %lend.1), channel_id=1, source_target_pairs={{0,8},{8,0},{1,9},{9,1},{2,10},{10,2},{3,11},{11,3},{4,12},{12,4},... | collective-permute-start | bytes 3145736 | tf_op jit(solution)/shard_map/ppermute | solution.py:242
  13.1 1.7 %pack.1 = f32[8,7,4,512]{3,2,1,0:T(4,128)} custom-call(f32[4,512]{1,0:T(4,128)} %cotangent.1, f32[6,4,512]{2,1,0:T(4,128)} %states.1), custom_call_target="tpu_custom_call" | custom-call | tf_op jit(solution)/shard_map/pack/pallas_call | solution.py:220
  14.8 3.5 %all-to-all-start = ((f32[8,7,4,512]{3,2,1,0:T(4,128)}), f32[8,7,4,512]{3,2,1,0:T(4,128)S(1)}, u32[]{:S(2)}, u32[]{:S(2)}) async-start(f32[8,7,4,512]{3,2,1,0:T(4,128)} %pack.1), calls=%async_computation | async-start | bytes 917504 | tf_op jit(solution)/shard_map/all_to_all | solution.py:229
  18.3 1.6 %share.1 = f32[40,512]{1,0:T(8,128)S(1)} custom-call(s32[24]{0:T(128)S(1)} %concatenate.3.facts.refs_0_, f32[16,32,32]{2,1,0:T(8,128)} %inverse_hbm.1), custom_call_target="tpu_custom_call" | custom-call | tf_op jit(solution)/shard_map/share/pallas_call | solution.py:243
  19.9 0.0 copy-done.1
  19.9 0.1 copy.12
  20.0 0.0 copy-done.2
  20.0 0.1 copy.13
  20.1 1.9 %all-gather = f32[80,512]{1,0:T(8,128)S(1)} all-gather(f32[40,512]{1,0:T(8,128)S(1)} %share.1), channel_id=2, replica_groups=mesh['z'=16,'yhi'=2,'core'=2,'x'=4,'ylo'=2] {'core'}, dimensions={0}, use_global_device_ids=true | all-gather | bytes 245760 | tf_op jit(solution)/shard_map/all_gather | solution.py:252
  22.0 5.1 %all-to-all-done.gathered = f32[8,7,4,512]{3,2,1,0:T(4,128)S(1)} async-done(((f32[8,7,4,512]{3,2,1,0:T(4,128)}), f32[8,7,4,512]{3,2,1,0:T(4,128)S(1)}, u32[]{:S(2)}, u32[]{:S(2)}) %all-to-all-start) | async-done | bytes 458784 | tf_op jit(solution)/shard_map/all_to_all | solution.py:229
  27.0 0.3 gathered.1
  27.4 2.4 %all-gather.1 = f32[64,512]{1,0:T(8,128)S(1)} all-gather(f32[32,512]{1,0:T(8,128)S(1)} %get-tuple-element.23), channel_id=3, replica_groups=mesh['z'=16,'yhi'=2,'core'=2,'x'=4,'ylo'=2] {'core'}, dimensions={0}, use_global_device_ids=true | all-gather | bytes 196608 | tf_op jit(solution)/shard_map/all_gather | solution.py:269
  29.8 0.0 collective-permute-done.borrowed
  29.8 1.4 %blocks.1 = (bf16[512,512]{1,0:T(8,128)(2,1)S(1)}, bf16[2,8,128,128]{3,2,1,0:T(8,128)(2,1)S(1)}, f32[2,512]{1,0:T(2,128)S(1)}) custom-call(s32[24]{0:T(128)S(1)} %concatenate.3.facts.refs_0_, f32[2,40,512]{2,1,0:T(8,128)S(1)} %bitcast.51, f32[512,512]{1,0:T(8,128)} %collective-permute-done.borrowed), custom_call_target="tpu_custom_call" | custom-call | tf_op jit(solution)/shard_map/blocks/pallas_call | solution.py:253
  31.2 0.0 copy-done
  31.2 1.3 %shard_map.91 = (f32[64,512]{1,0:T(8,128)S(1)}, f32[64,512]{1,0:T(8,128)S(1)}) custom-call(s32[24]{0:T(128)S(1)} %concatenate.3.facts.refs_0_, f32[2,32,512]{2,1,0:T(8,128)S(1)} %bitcast.52, bf16[1,5,512,512]{3,2,1,0:T(8,128)(2,1)S(1)} %copy-done, bf16[512,512]{1,0:T(8,128)(2,1)S(1)} %get-tuple-element.24.refs_3_, ...), custom_call_target="tpu_custom_call" | custom-call | tf_op jit(solution)/shard_map/pallas_call | solution.py:279
  32.5 2.0 %all-gather.2 = f32[128,512]{1,0:T(8,128)S(1)} all-gather(f32[64,512]{1,0:T(8,128)S(1)} %get-tuple-element.28), channel_id=4, replica_groups={{9,16},{8,0},{11,18},{10,2},{13,20},{12,4},{15,22},{14,6},{24,33},{25,1..., dimensions={0}, use_global_device_ids=true | all-gather | bytes 393216 | tf_op jit(solution)/shard_map/all_gather | solution.py:290
  34.6 2.0 %all-gather.3 = f32[128,512]{1,0:T(8,128)S(1)} all-gather(f32[64,512]{1,0:T(8,128)S(1)} %bitcast_add_fusion.4), channel_id=5, replica_groups=mesh['z'=16,'yhi'=2,'core'=2,'x'=4,'ylo'=2] {'core'}, dimensions={0}, use_global_device_ids=true | all-gather | bytes 393216 | tf_op jit(solution)/shard_map/all_gather | solution.py:292
  36.5 1.3 %shard_map.92 = (f32[64,512]{1,0:T(8,128)S(1)}, f32[64,512]{1,0:T(8,128)S(1)}) custom-call(s32[24]{0:T(128)S(1)} %concatenate.3.facts.refs_0_, f32[2,64,512]{2,1,0:T(8,128)S(1)} %bitcast.35, bf16[1,5,512,512]{3,2,1,0:T(8,128)(2,1)S(1)} %copy-done, bf16[512,512]{1,0:T(8,128)(2,1)S(1)} %get-tuple-element.24.refs_3_, ...), custom_call_target="tpu_custom_call" | custom-call | tf_op jit(solution)/shard_map/pallas_call | solution.py:279
  37.9 2.0 %all-gather.4 = f32[128,512]{1,0:T(8,128)S(1)} all-gather(f32[64,512]{1,0:T(8,128)S(1)} %get-tuple-element.30), channel_id=6, replica_groups={{9,16},{8,0},{11,18},{10,2},{13,20},{12,4},{15,22},{14,6},{24,33},{25,1..., dimensions={0}, use_global_device_ids=true | all-gather | bytes 393216 | tf_op jit(solution)/shard_map/all_gather | solution.py:290
  39.9 2.0 %all-gather.5 = f32[128,512]{1,0:T(8,128)S(1)} all-gather(f32[64,512]{1,0:T(8,128)S(1)} %bitcast_add_fusion.3), channel_id=7, replica_groups=mesh['z'=16,'yhi'=2,'core'=2,'x'=4,'ylo'=2] {'core'}, dimensions={0}, use_global_device_ids=true | all-gather | bytes 393216 | tf_op jit(solution)/shard_map/all_gather | solution.py:292
  41.9 1.3 %shard_map.93 = (f32[64,512]{1,0:T(8,128)S(1)}, f32[64,512]{1,0:T(8,128)S(1)}) custom-call(s32[24]{0:T(128)S(1)} %concatenate.3.facts.refs_0_, f32[2,64,512]{2,1,0:T(8,128)S(1)} %bitcast.36, bf16[1,5,512,512]{3,2,1,0:T(8,128)(2,1)S(1)} %copy-done, bf16[512,512]{1,0:T(8,128)(2,1)S(1)} %get-tuple-element.24.refs_3_, ...), custom_call_target="tpu_custom_call" | custom-call | tf_op jit(solution)/shard_map/pallas_call | solution.py:279
  43.2 2.0 %all-gather.6 = f32[128,512]{1,0:T(8,128)S(1)} all-gather(f32[64,512]{1,0:T(8,128)S(1)} %get-tuple-element.32), channel_id=8, replica_groups={{9,16},{8,0},{11,18},{10,2},{13,20},{12,4},{15,22},{14,6},{24,33},{25,1..., dimensions={0}, use_global_device_ids=true | all-gather | bytes 393216 | tf_op jit(solution)/shard_map/all_gather | solution.py:290
  45.2 2.0 %all-gather.7 = f32[128,512]{1,0:T(8,128)S(1)} all-gather(f32[64,512]{1,0:T(8,128)S(1)} %bitcast_add_fusion.2), channel_id=9, replica_groups=mesh['z'=16,'yhi'=2,'core'=2,'x'=4,'ylo'=2] {'core'}, dimensions={0}, use_global_device_ids=true | all-gather | bytes 393216 | tf_op jit(solution)/shard_map/all_gather | solution.py:292
  47.2 1.3 %shard_map.94 = (f32[64,512]{1,0:T(8,128)S(1)}, f32[64,512]{1,0:T(8,128)S(1)}) custom-call(s32[24]{0:T(128)S(1)} %concatenate.3.facts.refs_0_, f32[2,64,512]{2,1,0:T(8,128)S(1)} %bitcast.37, bf16[1,5,512,512]{3,2,1,0:T(8,128)(2,1)S(1)} %copy-done, bf16[512,512]{1,0:T(8,128)(2,1)S(1)} %get-tuple-element.24.refs_3_, ...), custom_call_target="tpu_custom_call" | custom-call | tf_op jit(solution)/shard_map/pallas_call | solution.py:279
  48.6 2.0 %all-gather.8 = f32[128,512]{1,0:T(8,128)S(1)} all-gather(f32[64,512]{1,0:T(8,128)S(1)} %get-tuple-element.34), channel_id=10, replica_groups={{9,16},{8,0},{11,18},{10,2},{13,20},{12,4},{15,22},{14,6},{24,33},{25,1..., dimensions={0}, use_global_device_ids=true | all-gather | bytes 393216 | tf_op jit(solution)/shard_map/all_gather | solution.py:290
  50.6 2.0 %all-gather.9 = f32[128,512]{1,0:T(8,128)S(1)} all-gather(f32[64,512]{1,0:T(8,128)S(1)} %bitcast_add_fusion.1), channel_id=11, replica_groups=mesh['z'=16,'yhi'=2,'core'=2,'x'=4,'ylo'=2] {'core'}, dimensions={0}, use_global_device_ids=true | all-gather | bytes 393216 | tf_op jit(solution)/shard_map/all_gather | solution.py:292
  52.6 1.3 %shard_map.95 = (f32[64,512]{1,0:T(8,128)S(1)}, f32[64,512]{1,0:T(8,128)S(1)}) custom-call(s32[24]{0:T(128)S(1)} %concatenate.3.facts.refs_0_, f32[2,64,512]{2,1,0:T(8,128)S(1)} %bitcast.38, bf16[1,5,512,512]{3,2,1,0:T(8,128)(2,1)S(1)} %copy-done, bf16[512,512]{1,0:T(8,128)(2,1)S(1)} %get-tuple-element.24.refs_3_, ...), custom_call_target="tpu_custom_call" | custom-call | tf_op jit(solution)/shard_map/pallas_call | solution.py:279
  53.9 2.0 %all-gather.10 = f32[128,512]{1,0:T(8,128)S(1)} all-gather(f32[64,512]{1,0:T(8,128)S(1)} %get-tuple-element.36), channel_id=12, replica_groups={{9,16},{8,0},{11,18},{10,2},{13,20},{12,4},{15,22},{14,6},{24,33},{25,1..., dimensions={0}, use_global_device_ids=true | all-gather | bytes 393216 | tf_op jit(solution)/shard_map/all_gather | solution.py:290
  55.9 2.0 %all-gather.11 = f32[128,512]{1,0:T(8,128)S(1)} all-gather(f32[64,512]{1,0:T(8,128)S(1)} %bitcast_add_fusion), channel_id=13, replica_groups=mesh['z'=16,'yhi'=2,'core'=2,'x'=4,'ylo'=2] {'core'}, dimensions={0}, use_global_device_ids=true | all-gather | bytes 393216 | tf_op jit(solution)/shard_map/all_gather | solution.py:292
  57.9 1.3 %shard_map.96 = (f32[16,512]{1,0:T(8,128)S(1)}, f32[16,512]{1,0:T(8,128)S(1)}) custom-call(s32[24]{0:T(128)S(1)} %concatenate.3.facts.refs_0_, f32[2,64,512]{2,1,0:T(8,128)S(1)} %bitcast.34, bf16[1,5,512,512]{3,2,1,0:T(8,128)(2,1)S(1)} %copy-done, bf16[512,512]{1,0:T(8,128)(2,1)S(1)} %get-tuple-element.24.refs_3_, ...), custom_call_target="tpu_custom_call" | custom-call | tf_op jit(solution)/shard_map/pallas_call | solution.py:279
  59.3 1.9 %all-gather.12 = f32[32,512]{1,0:T(8,128)S(1)} all-gather(f32[16,512]{1,0:T(8,128)S(1)} %get-tuple-element.38), channel_id=14, replica_groups={{9,16},{8,0},{11,18},{10,2},{13,20},{12,4},{15,22},{14,6},{24,33},{25,1..., dimensions={0}, use_global_device_ids=true | all-gather | bytes 98304 | tf_op jit(solution)/shard_map/all_gather | solution.py:290
  61.1 1.9 %all-gather.13 = f32[32,512]{1,0:T(8,128)S(1)} all-gather(f32[16,512]{1,0:T(8,128)S(1)} %bitcast_add_fusion.5), channel_id=15, replica_groups=mesh['z'=16,'yhi'=2,'core'=2,'x'=4,'ylo'=2] {'core'}, dimensions={0}, use_global_device_ids=true | all-gather | bytes 98304 | tf_op jit(solution)/shard_map/all_gather | solution.py:292
  63.0 35.7 %all_gather.116 = f32[2,4,512]{2,1,0:T(4,128)S(1)} all-gather(f32[1,4,512]{2,1,0:T(4,128)S(1)} %constant_dynamic-slice_fusion), channel_id=1, replica_groups=mesh['z'=16,'yhi'=2,'core'=2,'x'=4,'ylo'=2] {'ylo'}, dimensions={0}, use_global_device_ids=true | all-gather | bytes 24576 | tf_op jit(solution)/shard_map/all_gather | solution.py:297
  98.7 0.6 select_bitcast_fusion
  (11 shorter events, 0.1 us)
Async XLA Ops:
  1.4 18.5 %copy-start.1 = (f32[32,32]{1,0:T(8,128)S(1)}, f32[32,32]{1,0:T(8,128)}, u32[]{:S(2)}) copy-start(f32[32,32]{1,0:T(8,128)} %uptake_weight.1) | copy-start | bytes 12292
  1.4 18.6 %copy-start.2 = (f32[32,32]{1,0:T(8,128)S(1)}, f32[32,32]{1,0:T(8,128)}, u32[]{:S(2)}) copy-start(f32[32,32]{1,0:T(8,128)} %param.17) | copy-start | bytes 12292
  4.1 27.1 %copy-start = (bf16[1,5,512,512]{3,2,1,0:T(8,128)(2,1)S(1)}, bf16[1,5,512,512]{3,2,1,0:T(8,128)(2,1)}, u32[]{:S(2)}) copy-start(bf16[1,5,512,512]{3,2,1,0:T(8,128)(2,1)} %refs_2_.11) | copy-start | bytes 7864324
  4.1 25.7 %collective-permute-start = (f32[512,512]{1,0:T(8,128)}, f32[512,512]{1,0:T(8,128)}, u32[]{:S(2)}, u32[]{:S(2)}) collective-permute-start(f32[512,512]{1,0:T(8,128)} %lend.1), channel_id=1, source_target_pairs={{0,8},{8,0},{1,9},{9,1},{2,10},{10,2},{3,11},{11,3},{4,12},{12,4},... | collective-permute-start | bytes 3145736 | tf_op jit(solution)/shard_map/ppermute | solution.py:242
  14.8 12.3 %all-to-all-start = ((f32[8,7,4,512]{3,2,1,0:T(4,128)}), f32[8,7,4,512]{3,2,1,0:T(4,128)S(1)}, u32[]{:S(2)}, u32[]{:S(2)}) async-start(f32[8,7,4,512]{3,2,1,0:T(4,128)} %pack.1), calls=%async_computation | async-start | bytes 917504 | tf_op jit(solution)/shard_map/all_to_all | solution.py:229

commit v5 on v4

--- a/solution.py
+++ b/solution.py
@@ -11,7 +11,7 @@
 EVERY = REGION + TRACER
 SPAN = 128
 VMEM_LIMIT = 8 * 2**20
-OFFSETS_AT, COUNT_AT, CORE_AT, X_AT, WET_AT = 0, 5, 6, 7, 8
+OFFSETS_AT, COUNT_AT, CORE_AT, TRACER_AT, NEIGHBOUR_AT, WET_AT = 0, 5, 6, 7, 8, 9
 
 
 def neighbour_groups(sizes):
@@ -29,6 +29,20 @@
     return groups
 
 
+def final_groups(sizes):
+    nq, nx, ny = sizes
+
+    def at(chip, core, x, ylo):
+        return (((chip % nq) * 2 + core) * nx + x) * ny + ylo
+
+    groups = []
+    for q in range(nq):
+        for x in range(nx):
+            j = 1 if q % 2 == 0 else 0
+            groups.append([at(q, 1, x, j), at(q + 1, 0, x, 1 - j), at(q, 1, x, 1 - j), at(q + 1, 0, x, j)])
+    return groups
+
+
 def halves(value):
     high = value.astype(jnp.bfloat16)
     low = (value - high.astype(jnp.float32)).astype(jnp.bfloat16)
@@ -63,18 +77,15 @@
     return 2 * facts[CORE_AT] - 1
 
 
-def pack_kernel(cotangent, states, copies, buffer, fetched, sent):
+def pack_kernel(cotangent, states, copies, buffer, fetched):
     first = pltpu.make_async_copy(cotangent, buffer.at[0], fetched.at[0])
     rest = pltpu.make_async_copy(states, buffer.at[pl.ds(1, states.shape[0])], fetched.at[1])
     first.start()
     rest.start()
     first.wait()
     rest.wait()
-    sends = [pltpu.make_async_copy(buffer, copies.at[t], sent.at[t]) for t in range(copies.shape[0])]
-    for send in sends:
-        send.start()
-    for send in sends:
-        send.wait()
+    for t in range(copies.shape[0]):
+        copies[t] = buffer[...]
 
 
 def lend_kernel(facts, tiles, lent, buffer, arrival):
@@ -99,7 +110,18 @@
         shared[levels : levels + 8, at] = jnp.where(row < facts[WET_AT + c], 1.0, 0.0)
 
 
-def blocks_kernel(facts, shared, borrowed, tile_out, blocks, wet_out):
+def gathered_kernel(facts, gathered, shared, uptake_weight, start, slopes, blocks, wet_out):
+    peers, _, few, _ = gathered.shape
+    for t in range(peers):
+        at = slice(t * few, (t + 1) * few)
+        start[at, :] = gathered[t, 0]
+        for n in range(slopes.shape[0]):
+            slopes[n, at, :] = gathered[t, 1 + n]
+    weight_high, weight_low = halves(uptake_weight[...])
+    for n in range(slopes.shape[0]):
+        state_high, state_low = halves(slopes[n])
+        reach = jnp.tanh(dot_split(weight_high, weight_low, state_high, state_low))
+        slopes[n] = 1.0 - reach * reach
     own = facts[CORE_AT]
     levels = shared.shape[1] - 8
     boxes = shared.shape[2]
@@ -111,32 +133,16 @@
     for which in range(2):
         side = own if which == 0 else 1 - own
         for s in range(spans):
-            part = shared[side, 0:levels, s * SPAN : (s + 1) * SPAN]
-            full = jnp.concatenate([part] * (SPAN // levels), axis=0)
-            high, low = halves(jnp.where(same, full, 0.0))
-            blocks[0, which * spans + s] = high
-            blocks[1, which * spans + s] = low
+            high, low = halves(shared[side, 0:levels, s * SPAN : (s + 1) * SPAN])
+            full_high = jnp.concatenate([high] * (SPAN // levels), axis=0)
+            full_low = jnp.concatenate([low] * (SPAN // levels), axis=0)
+            blocks[0, which * spans + s] = jnp.where(same, full_high, jnp.zeros_like(full_high))
+            blocks[1, which * spans + s] = jnp.where(same, full_low, jnp.zeros_like(full_low))
         wet_out[which : which + 1, :] = shared[side, levels : levels + 1, :]
-    tile_out[...] = borrowed[...].astype(jnp.bfloat16)
-
-
-def gathered_kernel(gathered, uptake_weight, start, slopes):
-    peers, _, few, _ = gathered.shape
-    for t in range(peers):
-        at = slice(t * few, (t + 1) * few)
-        start[at, :] = gathered[t, 0]
-        for n in range(slopes.shape[0]):
-            slopes[n, at, :] = gathered[t, 1 + n]
-    weight_high, weight_low = halves(uptake_weight[...])
-    for n in range(slopes.shape[0]):
-        state_high, state_low = halves(slopes[n])
-        reach = jnp.tanh(dot_split(weight_high, weight_low, state_high, state_low))
-        slopes[n] = 1.0 - reach * reach
 
 
 def step_kernel(
-    facts, adjoint, tiles, borrowed, blocks, wet, slopes, uptake_t, release_t, send, keep, settled, rows,
-    *, section, first, last,
+    facts, adjoint, tiles, borrowed, blocks, wet, slopes, uptake_t, release_t, *outputs, section, first, last,
 ):
     own = facts[CORE_AT]
     direction = away(facts)
@@ -144,12 +150,19 @@
     tracers = uptake_t.shape[0]
     spans = boxes // SPAN
     if first:
+        send, keep, tile_out, settled = outputs
         pair = (adjoint[own], adjoint[1 - own])
+        tile_out[...] = borrowed[...].astype(jnp.bfloat16)
+        borrowed = tile_out
     else:
         pair = (
             wet[0:1, :] * (adjoint[own, 0:tracers, :] + adjoint[1 - own, tracers:, :]),
             wet[1:2, :] * (adjoint[own, tracers:, :] + adjoint[1 - own, 0:tracers, :]),
         )
+        if last:
+            parcels, settled, send, keep = outputs
+        else:
+            send, keep, settled = outputs
     for which in range(2):
         high, low = halves(pair[which])
         for s in range(spans):
@@ -164,12 +177,12 @@
         return jnp.where(slot_live(facts, slots, distance), product, 0.0)
 
     def put(out, part, value):
-        few = out.shape[0] // 2
         if last:
-            for x in range(rows.shape[0]):
-                rows[x] = value[x * few : (x + 1) * few]
-            value = rows[facts[X_AT]]
-        out[part * few : (part + 1) * few, :] = value
+            few = out.shape[2]
+            for t in range(tracers // few):
+                out[t, part] = value[t * few : (t + 1) * few]
+        else:
+            out[part * tracers : (part + 1) * tracers, :] = value
 
     put(send, 0, term(direction) + dot(other, borrowed[...]))
     put(send, 1, term(2 * direction))
@@ -179,6 +192,13 @@
     uptake_high, uptake_low = halves(uptake_t[...])
     put(keep, 0, term(0) + dot_split(uptake_high, uptake_low, pushed_high, pushed_low))
     put(keep, 1, term(-direction))
+    if last:
+        here, there = facts[TRACER_AT], facts[NEIGHBOUR_AT]
+        upper = own == 1
+        parcels[0] = jnp.where(upper, keep[here], send[there])
+        parcels[1] = jnp.where(upper, send[there], keep[here])
+        parcels[2] = jnp.where(upper, keep[there], send[here])
+        parcels[3] = jnp.where(upper, send[here], keep[there])
 
 
 def local(
@@ -208,10 +228,9 @@
     lean = pltpu.CompilerParams(vmem_limit_bytes=VMEM_LIMIT)
     dma = pltpu.SemaphoreType.DMA
     core_index = lax.axis_index("core")
-    x_index = lax.axis_index("x")
-    ylo_index = lax.axis_index("ylo")
-    ylo_size = lax.axis_size("ylo")
-    joined = lax.axis_index("yhi") + ylo_index == 1
+    ylo_index, ylo_size = lax.axis_index("ylo"), lax.axis_size("ylo")
+    tracer_here = lax.axis_index("x") * ylo_size + ylo_index
+    neighbour = tracer_here + 1 - 2 * ylo_index
     groups = neighbour_groups(sizes)
 
     def in_hbm(array):
@@ -220,15 +239,15 @@
     copies = pl.pallas_call(
         pack_kernel,
         in_specs=[hbm] * 2,
-        out_specs=hbm,
+        out_specs=vmem,
         out_shape=shape((peers, 1 + sections, tracers_here, boxes), f32),
-        scratch_shapes=[pltpu.VMEM((1 + sections, tracers_here, boxes), f32), dma((2,)), dma((peers,))],
+        scratch_shapes=[pltpu.VMEM((1 + sections, tracers_here, boxes), f32), dma((2,))],
         compiler_params=lean,
         name="pack",
     )(in_hbm(cotangent), in_hbm(states))
     gathered = lax.all_to_all(copies, TRACER, split_axis=0, concat_axis=0, tiled=True)
     facts = jnp.concatenate(
-        [tile_offset.reshape(-1), tile_count, jnp.stack([core_index, x_index]).astype(jnp.int32), wet_levels]
+        [tile_offset.reshape(-1), tile_count, jnp.stack([core_index, tracer_here, neighbour]).astype(jnp.int32), wet_levels]
     )
     lent = pl.pallas_call(
         lend_kernel,
@@ -250,52 +269,54 @@
         name="share",
     )(facts, in_hbm(implicit_inverse))
     shared = lax.all_gather(shared, "core")
-    borrowed, blocks, wet = pl.pallas_call(
-        blocks_kernel,
-        in_specs=[smem] + [vmem] * 2,
-        out_specs=[vmem] * 3,
-        out_shape=[shape((boxes, boxes), bf16), shape((2, 2 * spans, SPAN, SPAN), bf16), shape((2, boxes), f32)],
-        compiler_params=lean,
-        name="blocks",
-    )(facts, shared, borrowed)
-    start, slopes = pl.pallas_call(
+    start, slopes, blocks, wet = pl.pallas_call(
         gathered_kernel,
-        in_specs=[vmem] * 2,
-        out_specs=[vmem] * 2,
-        out_shape=[shape((tracers, boxes), f32), shape((sections, tracers, boxes), f32)],
+        in_specs=[smem] + [vmem] * 3,
+        out_specs=[vmem] * 4,
+        out_shape=[
+            shape((tracers, boxes), f32),
+            shape((sections, tracers, boxes), f32),
+            shape((2, 2 * spans, SPAN, SPAN), bf16),
+            shape((2, boxes), f32),
+        ],
         compiler_params=lean,
         name="gathered",
-    )(gathered, uptake_weight)
+    )(facts, gathered, shared, uptake_weight)
     adjoint = lax.all_gather(start, "core")
     uptake_t, release_t = uptake_weight.T, release_weight.T
-    last_rows = ylo_size * tracers_here
     for section in range(sections - 1, -1, -1):
         first, last = section == sections - 1, section == 0
 
         def step(*refs, section=section, first=first, last=last):
             step_kernel(*refs, section=section, first=first, last=last)
 
-        exchanged = 2 * last_rows if last else 2 * tracers
-        send, keep = pl.pallas_call(
+        pieces = pltpu.VMEM((peers, 2, tracers_here, boxes), f32)
+        if last:
+            out_shape = [shape((4, 2, tracers_here, boxes), f32)]
+        else:
+            out_shape = [shape((2 * tracers, boxes), f32)] * 2 + [shape((boxes, boxes), bf16)] * first
+        results = pl.pallas_call(
             step,
             in_specs=[smem] + [vmem] * 8,
-            out_specs=[vmem] * 2,
-            out_shape=[shape((exchanged, boxes), f32)] * 2,
-            scratch_shapes=[
-                pltpu.VMEM((2, tracers, boxes), f32),
-                pltpu.VMEM((tracers // last_rows, last_rows, boxes), f32),
-            ],
+            out_specs=[vmem] * len(out_shape),
+            out_shape=out_shape,
+            scratch_shapes=[pltpu.VMEM((2, tracers, boxes), f32)] + [pieces] * (2 * last),
             compiler_params=lean,
         )(facts, adjoint, explicit_tiles, borrowed, blocks, wet, slopes, uptake_t, release_t)
-        arrived = lax.all_gather(send, EVERY, axis_index_groups=groups)
-        keep = keep + lax.dynamic_index_in_dim(arrived, core_index, 0, keepdims=False)
+        if last:
+            parcels = lax.all_to_all(
+                results[0], EVERY, split_axis=0, concat_axis=0, tiled=True, axis_index_groups=final_groups(sizes)
+            )
+            keep = parcels[0] + parcels[1]
+        else:
+            if first:
+                borrowed = results[2]
+            arrived = lax.all_gather(results[0], EVERY, axis_index_groups=groups)
+            keep = results[1] + lax.dynamic_index_in_dim(arrived, core_index, 0, keepdims=False)
         adjoint = lax.all_gather(keep, "core")
-    mine = lax.dynamic_index_in_dim(adjoint, core_index, 0, keepdims=False)[:last_rows]
-    theirs = lax.dynamic_index_in_dim(adjoint, 1 - core_index, 0, keepdims=False)[last_rows:]
-    result = (wet[0:1] * (mine + theirs)).reshape(ylo_size, tracers_here, boxes)
-    passed = lax.dynamic_index_in_dim(result, 1 - ylo_index, 0, keepdims=False)
-    passed = lax.dynamic_index_in_dim(lax.all_gather(passed, "ylo"), 1 - ylo_index, 0, keepdims=False)
-    return jnp.where(joined, lax.dynamic_index_in_dim(result, ylo_index, 0, keepdims=False), passed)
+    mine = lax.dynamic_index_in_dim(adjoint, core_index, 0, keepdims=False)[0]
+    theirs = lax.dynamic_index_in_dim(adjoint, 1 - core_index, 0, keepdims=False)[1]
+    return wet[0:1] * (mine + theirs)
 
 
 def solution(mesh):

time: 100 us -> 102 us (1.020)
  blocking collectives: 63.6 us -> 27.7 us
  starting transfers between devices: 12.5 us -> 45.1 us
  waiting for transfers between devices: 5.06 us -> 9.66 us
    all_gather x7 -> x5, blocking collectives: 47.5 us -> 9.94 us  [local(): arrived = lax.all_gather(results[0], EVERY, axis_index_groups=groups)]
    all_to_all x0 -> x1, starting transfers between devices: none -> 32.9 us  [local(): lax.all_to_all(results[0], EVERY, split_axis=0, concat_axis=0, tiled=True...]
    all_to_all x0 -> x1, waiting for transfers between devices: none -> 4.6 us  [local(): lax.all_to_all(results[0], EVERY, split_axis=0, concat_axis=0, tiled=True...]
    all_gather x6, blocking collectives: 11.8 us -> 13.4 us  [local(): adjoint = lax.all_gather(keep, 'core')]
    pallas_call x9 -> x8, Pallas kernels: 11.4 us -> 11.9 us  [the longest x6 9.35 us: local(): pl.pallas_call(step, in_specs=[smem] + [vmem] * 8, out_specs=[vmem] * len...]
  transfers between devices with their start and end apart: 2 -> 3, of which waited for: 1 -> 2; matrix products, arithmetic and copies ran while one was open for 0% -> 0% of each run, Pallas kernels for 4% -> 4%
where the time goes in v5:
time: 102 us; the launch traced here: 101 us
  starting transfers between devices  45.1 us (44%)
  blocking collectives  27.7 us (27%)
  Pallas kernels  16.4 us (16%)
  waiting for transfers between devices  9.66 us (9%)
    all_to_all x1, starting transfers between devices, local(): lax.all_to_all(results[0], EVERY, split_axis=0, concat_axis=0, tiled=True...  32.9 us
    all_gather x6, blocking collectives, local(): adjoint = lax.all_gather(keep, 'core')  13.4 us
    all_gather x5, blocking collectives, local(): arrived = lax.all_gather(results[0], EVERY, axis_index_groups=groups)  9.94 us
    pallas_call x6, Pallas kernels, local(): pl.pallas_call(step, in_specs=[smem] + [vmem] * 8, out_specs=[vmem] * len...  9.35 us
    ppermute x1, starting transfers between devices, local(): borrowed = lax.ppermute(lent, 'core', [(0, 1), (1, 0)])  8.75 us
    all_to_all x1, waiting for transfers between devices, local(): lax.all_to_all(copies, TRACER, split_axis=0, concat_axis=0, tiled=True)  5.06 us
    all_to_all x1, waiting for transfers between devices, local(): lax.all_to_all(results[0], EVERY, split_axis=0, concat_axis=0, tiled=True...  4.6 us
    all_to_all x1, starting transfers between devices, local(): lax.all_to_all(copies, TRACER, split_axis=0, concat_axis=0, tiled=True)  3.48 us
  transfers between devices with their start and end apart: 3, of which 2 were waited for; matrix products, arithmetic and copies ran while one was open for 0% of the time, Pallas kernels for 4%

profile of v5, /device:TPU:1, one launch (start us, length us, event | category | flops | bytes accessed | tf_op | source)
XLA Modules:
  0.0 101.2 jit_solution(15134516594138008937)
XLA Ops:
  0.7 0.8 concatenate.3.facts.refs_0_
  1.4 0.0 copy-start.1
  1.4 0.0 copy-start.2
  1.4 0.0 copy-start
  1.4 2.9 %lend.1 = f32[512,512]{1,0:T(8,128)} custom-call(s32[25]{0:T(128)S(1)} %concatenate.3.facts.refs_0_, bf16[1,5,512,512]{3,2,1,0:T(8,128)(2,1)} %refs_2_.11), custom_call_target="tpu_custom_call" | custom-call | tf_op jit(solution)/shard_map/lend/pallas_call | solution.py:252
  4.3 8.7 %collective-permute-start = (f32[512,512]{1,0:T(8,128)}, f32[512,512]{1,0:T(8,128)}, u32[]{:S(2)}, u32[]{:S(2)}) collective-permute-start(f32[512,512]{1,0:T(8,128)} %lend.1), channel_id=1, source_target_pairs={{0,8},{8,0},{1,9},{9,1},{2,10},{10,2},{3,11},{11,3},{4,12},{12,4},... | collective-permute-start | bytes 3145736 | tf_op jit(solution)/shard_map/ppermute | solution.py:261
  13.1 1.6 %pack.1 = f32[8,7,4,512]{3,2,1,0:T(4,128)} custom-call(f32[4,512]{1,0:T(4,128)} %cotangent.1, f32[6,4,512]{2,1,0:T(4,128)} %states.1), custom_call_target="tpu_custom_call" | custom-call | tf_op jit(solution)/shard_map/pack/pallas_call | solution.py:239
  14.7 3.5 %all-to-all-start = ((f32[8,7,4,512]{3,2,1,0:T(4,128)}), f32[8,7,4,512]{3,2,1,0:T(4,128)S(1)}, u32[]{:S(2)}, u32[]{:S(2)}) async-start(f32[8,7,4,512]{3,2,1,0:T(4,128)} %pack.1), calls=%async_computation | async-start | bytes 917504 | tf_op jit(solution)/shard_map/all_to_all | solution.py:248
  18.2 1.6 %share.1 = f32[40,512]{1,0:T(8,128)S(1)} custom-call(s32[25]{0:T(128)S(1)} %concatenate.3.facts.refs_0_, f32[16,32,32]{2,1,0:T(8,128)} %inverse_hbm.1), custom_call_target="tpu_custom_call" | custom-call | tf_op jit(solution)/shard_map/share/pallas_call | solution.py:262
  19.9 0.0 copy-done.1
  19.9 0.1 copy.12
  19.9 0.0 copy-done.2
  19.9 0.1 copy.13
  20.0 1.9 %all-gather = f32[80,512]{1,0:T(8,128)S(1)} all-gather(f32[40,512]{1,0:T(8,128)S(1)} %share.1), channel_id=2, replica_groups=mesh['z'=16,'yhi'=2,'core'=2,'x'=4,'ylo'=2] {'core'}, dimensions={0}, use_global_device_ids=true | all-gather | bytes 245760 | tf_op jit(solution)/shard_map/all_gather | solution.py:271
  21.9 5.1 %all-to-all-done.gathered = f32[8,7,4,512]{3,2,1,0:T(4,128)S(1)} async-done(((f32[8,7,4,512]{3,2,1,0:T(4,128)}), f32[8,7,4,512]{3,2,1,0:T(4,128)S(1)}, u32[]{:S(2)}, u32[]{:S(2)}) %all-to-all-start) | async-done | bytes 458784 | tf_op jit(solution)/shard_map/all_to_all | solution.py:248
  27.0 0.9 gathered.1
  27.9 2.4 %all-gather.1 = f32[64,512]{1,0:T(8,128)S(1)} all-gather(f32[32,512]{1,0:T(8,128)S(1)} %get-tuple-element.21), channel_id=3, replica_groups=mesh['z'=16,'yhi'=2,'core'=2,'x'=4,'ylo'=2] {'core'}, dimensions={0}, use_global_device_ids=true | all-gather | bytes 196608 | tf_op jit(solution)/shard_map/all_gather | solution.py:285
  30.3 0.0 collective-permute-done.refs_3_
  30.3 0.0 copy-done
  30.3 2.0 %shard_map.91 = (f32[64,512]{1,0:T(8,128)S(1)}, f32[64,512]{1,0:T(8,128)S(1)}, bf16[512,512]{1,0:T(8,128)(2,1)S(1)}) custom-call(s32[25]{0:T(128)S(1)} %concatenate.3.facts.refs_0_, f32[2,32,512]{2,1,0:T(8,128)S(1)} %bitcast.51, bf16[1,5,512,512]{3,2,1,0:T(8,128)(2,1)S(1)} %copy-done, f32[512,512]{1,0:T(8,128)} %collective-permute-done.refs_3_, ...), custom_call_target="tpu_custom_call" | custom-call | tf_op jit(solution)/shard_map/pallas_call | solution.py:298
  32.4 2.0 %all-gather.2 = f32[128,512]{1,0:T(8,128)S(1)} all-gather(f32[64,512]{1,0:T(8,128)S(1)} %get-tuple-element.25), channel_id=4, replica_groups={{9,16},{8,0},{11,18},{10,2},{13,20},{12,4},{15,22},{14,6},{24,33},{25,1..., dimensions={0}, use_global_device_ids=true | all-gather | bytes 393216 | tf_op jit(solution)/shard_map/all_gather | solution.py:314
  34.4 2.0 %all-gather.3 = f32[128,512]{1,0:T(8,128)S(1)} all-gather(f32[64,512]{1,0:T(8,128)S(1)} %bitcast_add_fusion.4), channel_id=5, replica_groups=mesh['z'=16,'yhi'=2,'core'=2,'x'=4,'ylo'=2] {'core'}, dimensions={0}, use_global_device_ids=true | all-gather | bytes 393216 | tf_op jit(solution)/shard_map/all_gather | solution.py:316
  36.4 1.3 %shard_map.92 = (f32[64,512]{1,0:T(8,128)S(1)}, f32[64,512]{1,0:T(8,128)S(1)}) custom-call(s32[25]{0:T(128)S(1)} %concatenate.3.facts.refs_0_, f32[2,64,512]{2,1,0:T(8,128)S(1)} %bitcast.34, bf16[1,5,512,512]{3,2,1,0:T(8,128)(2,1)S(1)} %copy-done, bf16[512,512]{1,0:T(8,128)(2,1)S(1)} %get-tuple-element.26.refs_3_, ...), custom_call_target="tpu_custom_call" | custom-call | tf_op jit(solution)/shard_map/pallas_call | solution.py:298
  37.7 2.0 %all-gather.4 = f32[128,512]{1,0:T(8,128)S(1)} all-gather(f32[64,512]{1,0:T(8,128)S(1)} %get-tuple-element.28), channel_id=6, replica_groups={{9,16},{8,0},{11,18},{10,2},{13,20},{12,4},{15,22},{14,6},{24,33},{25,1..., dimensions={0}, use_global_device_ids=true | all-gather | bytes 393216 | tf_op jit(solution)/shard_map/all_gather | solution.py:314
  39.7 2.0 %all-gather.5 = f32[128,512]{1,0:T(8,128)S(1)} all-gather(f32[64,512]{1,0:T(8,128)S(1)} %bitcast_add_fusion.3), channel_id=7, replica_groups=mesh['z'=16,'yhi'=2,'core'=2,'x'=4,'ylo'=2] {'core'}, dimensions={0}, use_global_device_ids=true | all-gather | bytes 393216 | tf_op jit(solution)/shard_map/all_gather | solution.py:316
  41.7 1.3 %shard_map.93 = (f32[64,512]{1,0:T(8,128)S(1)}, f32[64,512]{1,0:T(8,128)S(1)}) custom-call(s32[25]{0:T(128)S(1)} %concatenate.3.facts.refs_0_, f32[2,64,512]{2,1,0:T(8,128)S(1)} %bitcast.35, bf16[1,5,512,512]{3,2,1,0:T(8,128)(2,1)S(1)} %copy-done, bf16[512,512]{1,0:T(8,128)(2,1)S(1)} %get-tuple-element.26.refs_3_, ...), custom_call_target="tpu_custom_call" | custom-call | tf_op jit(solution)/shard_map/pallas_call | solution.py:298
  43.1 2.0 %all-gather.6 = f32[128,512]{1,0:T(8,128)S(1)} all-gather(f32[64,512]{1,0:T(8,128)S(1)} %get-tuple-element.30), channel_id=8, replica_groups={{9,16},{8,0},{11,18},{10,2},{13,20},{12,4},{15,22},{14,6},{24,33},{25,1..., dimensions={0}, use_global_device_ids=true | all-gather | bytes 393216 | tf_op jit(solution)/shard_map/all_gather | solution.py:314
  45.1 2.0 %all-gather.7 = f32[128,512]{1,0:T(8,128)S(1)} all-gather(f32[64,512]{1,0:T(8,128)S(1)} %bitcast_add_fusion.2), channel_id=9, replica_groups=mesh['z'=16,'yhi'=2,'core'=2,'x'=4,'ylo'=2] {'core'}, dimensions={0}, use_global_device_ids=true | all-gather | bytes 393216 | tf_op jit(solution)/shard_map/all_gather | solution.py:316
  47.1 1.3 %shard_map.94 = (f32[64,512]{1,0:T(8,128)S(1)}, f32[64,512]{1,0:T(8,128)S(1)}) custom-call(s32[25]{0:T(128)S(1)} %concatenate.3.facts.refs_0_, f32[2,64,512]{2,1,0:T(8,128)S(1)} %bitcast.36, bf16[1,5,512,512]{3,2,1,0:T(8,128)(2,1)S(1)} %copy-done, bf16[512,512]{1,0:T(8,128)(2,1)S(1)} %get-tuple-element.26.refs_3_, ...), custom_call_target="tpu_custom_call" | custom-call | tf_op jit(solution)/shard_map/pallas_call | solution.py:298
  48.4 2.0 %all-gather.8 = f32[128,512]{1,0:T(8,128)S(1)} all-gather(f32[64,512]{1,0:T(8,128)S(1)} %get-tuple-element.32), channel_id=10, replica_groups={{9,16},{8,0},{11,18},{10,2},{13,20},{12,4},{15,22},{14,6},{24,33},{25,1..., dimensions={0}, use_global_device_ids=true | all-gather | bytes 393216 | tf_op jit(solution)/shard_map/all_gather | solution.py:314
  50.4 2.0 %all-gather.9 = f32[128,512]{1,0:T(8,128)S(1)} all-gather(f32[64,512]{1,0:T(8,128)S(1)} %bitcast_add_fusion.1), channel_id=11, replica_groups=mesh['z'=16,'yhi'=2,'core'=2,'x'=4,'ylo'=2] {'core'}, dimensions={0}, use_global_device_ids=true | all-gather | bytes 393216 | tf_op jit(solution)/shard_map/all_gather | solution.py:316
  52.4 1.3 %shard_map.95 = (f32[64,512]{1,0:T(8,128)S(1)}, f32[64,512]{1,0:T(8,128)S(1)}) custom-call(s32[25]{0:T(128)S(1)} %concatenate.3.facts.refs_0_, f32[2,64,512]{2,1,0:T(8,128)S(1)} %bitcast.37, bf16[1,5,512,512]{3,2,1,0:T(8,128)(2,1)S(1)} %copy-done, bf16[512,512]{1,0:T(8,128)(2,1)S(1)} %get-tuple-element.26.refs_3_, ...), custom_call_target="tpu_custom_call" | custom-call | tf_op jit(solution)/shard_map/pallas_call | solution.py:298
  53.7 2.0 %all-gather.10 = f32[128,512]{1,0:T(8,128)S(1)} all-gather(f32[64,512]{1,0:T(8,128)S(1)} %get-tuple-element.34), channel_id=12, replica_groups={{9,16},{8,0},{11,18},{10,2},{13,20},{12,4},{15,22},{14,6},{24,33},{25,1..., dimensions={0}, use_global_device_ids=true | all-gather | bytes 393216 | tf_op jit(solution)/shard_map/all_gather | solution.py:314
  55.7 2.0 %all-gather.11 = f32[128,512]{1,0:T(8,128)S(1)} all-gather(f32[64,512]{1,0:T(8,128)S(1)} %bitcast_add_fusion), channel_id=13, replica_groups=mesh['z'=16,'yhi'=2,'core'=2,'x'=4,'ylo'=2] {'core'}, dimensions={0}, use_global_device_ids=true | all-gather | bytes 393216 | tf_op jit(solution)/shard_map/all_gather | solution.py:316
  57.7 2.0 %shard_map.96 = f32[4,2,4,512]{3,2,1,0:T(4,128)} custom-call(s32[25]{0:T(128)S(1)} %concatenate.3.facts.refs_0_, f32[2,64,512]{2,1,0:T(8,128)S(1)} %bitcast.33, bf16[1,5,512,512]{3,2,1,0:T(8,128)(2,1)S(1)} %copy-done, bf16[512,512]{1,0:T(8,128)(2,1)S(1)} %get-tuple-element.26.refs_3_, bf16[2,8,128,128]{3,2,1,0:T(8,128)(2,1)S(1)} %get-tuple-element.22.refs_4_, ...), custom_call_target="tpu_custom_call" | custom-call | tf_op jit(solution)/shard_map/pallas_call | solution.py:298
  59.7 32.9 %all-to-all-start.1 = ((f32[4,2,4,512]{3,2,1,0:T(4,128)}), f32[4,2,4,512]{3,2,1,0:T(4,128)S(1)}, u32[]{:S(2)}, u32[]{:S(2)}) async-start(f32[4,2,4,512]{3,2,1,0:T(4,128)} %shard_map.96), calls=%async_computation.1 | async-start | bytes 131072 | tf_op jit(solution)/shard_map/all_to_all | solution.py:307
  92.6 4.6 %all-to-all-done.1 = f32[4,2,4,512]{3,2,1,0:T(4,128)S(1)} async-done(((f32[4,2,4,512]{3,2,1,0:T(4,128)}), f32[4,2,4,512]{3,2,1,0:T(4,128)S(1)}, u32[]{:S(2)}, u32[]{:S(2)}) %all-to-all-start.1) | async-done | bytes 65568 | tf_op jit(solution)/shard_map/all_to_all | solution.py:307
  97.2 3.4 %all_gather.100 = f32[2,2,4,512]{3,2,1,0:T(4,128)S(1)} all-gather(f32[1,2,4,512]{3,2,1,0:T(4,128)S(1)} %slice_add_fusion), channel_id=1, replica_groups=mesh['z'=16,'yhi'=2,'core'=2,'x'=4,'ylo'=2] {'core'}, dimensions={0}, use_global_device_ids=true | all-gather | bytes 49152 | tf_op jit(solution)/shard_map/all_gather | solution.py:316
  100.6 0.6 fusion.1
  (7 shorter events, 0.1 us)
Async XLA Ops:
  1.4 18.5 %copy-start.1 = (f32[32,32]{1,0:T(8,128)S(1)}, f32[32,32]{1,0:T(8,128)}, u32[]{:S(2)}) copy-start(f32[32,32]{1,0:T(8,128)} %uptake_weight.1) | copy-start | bytes 12292
  1.4 18.5 %copy-start.2 = (f32[32,32]{1,0:T(8,128)S(1)}, f32[32,32]{1,0:T(8,128)}, u32[]{:S(2)}) copy-start(f32[32,32]{1,0:T(8,128)} %param.17) | copy-start | bytes 12292
  1.4 28.9 %copy-start = (bf16[1,5,512,512]{3,2,1,0:T(8,128)(2,1)S(1)}, bf16[1,5,512,512]{3,2,1,0:T(8,128)(2,1)}, u32[]{:S(2)}) copy-start(bf16[1,5,512,512]{3,2,1,0:T(8,128)(2,1)} %refs_2_.11) | copy-start | bytes 7864324
  4.3 26.0 %collective-permute-start = (f32[512,512]{1,0:T(8,128)}, f32[512,512]{1,0:T(8,128)}, u32[]{:S(2)}, u32[]{:S(2)}) collective-permute-start(f32[512,512]{1,0:T(8,128)} %lend.1), channel_id=1, source_target_pairs={{0,8},{8,0},{1,9},{9,1},{2,10},{10,2},{3,11},{11,3},{4,12},{12,4},... | collective-permute-start | bytes 3145736 | tf_op jit(solution)/shard_map/ppermute | solution.py:261
  14.7 12.3 %all-to-all-start = ((f32[8,7,4,512]{3,2,1,0:T(4,128)}), f32[8,7,4,512]{3,2,1,0:T(4,128)S(1)}, u32[]{:S(2)}, u32[]{:S(2)}) async-start(f32[8,7,4,512]{3,2,1,0:T(4,128)} %pack.1), calls=%async_computation | async-start | bytes 917504 | tf_op jit(solution)/shard_map/all_to_all | solution.py:248
  59.7 37.5 %all-to-all-start.1 = ((f32[4,2,4,512]{3,2,1,0:T(4,128)}), f32[4,2,4,512]{3,2,1,0:T(4,128)S(1)}, u32[]{:S(2)}, u32[]{:S(2)}) async-start(f32[4,2,4,512]{3,2,1,0:T(4,128)} %shard_map.96), calls=%async_computation.1 | async-start | bytes 131072 | tf_op jit(solution)/shard_map/all_to_all | solution.py:307

commit v6 on v4

--- a/solution.py
+++ b/solution.py
@@ -9,9 +9,9 @@
 REGION = ("z", "yhi", "core")
 TRACER = ("x", "ylo")
 EVERY = REGION + TRACER
-SPAN = 128
+SPAN = 256
 VMEM_LIMIT = 8 * 2**20
-OFFSETS_AT, COUNT_AT, CORE_AT, X_AT, WET_AT = 0, 5, 6, 7, 8
+COUNT_AT, CORE_AT, X_AT = 5, 6, 7
 
 
 def neighbour_groups(sizes):
@@ -45,61 +45,74 @@
     return both[:rows] + both[rows:] + dot(a_high, b_low)
 
 
-def slot_at(facts, slots, distance):
+def slot_at(offsets, slots, distance):
     slot = jnp.int32(0)
     for k in range(slots):
-        slot = slot + jnp.where(facts[OFFSETS_AT + k] == distance, k, 0)
+        slot = slot + jnp.where(offsets[k] == distance, k, 0)
     return slot
 
 
-def slot_live(facts, slots, distance):
+def slot_live(offsets, count, slots, distance):
     live = jnp.int32(0)
     for k in range(slots):
-        live = live + jnp.where((facts[OFFSETS_AT + k] == distance) & (k < facts[COUNT_AT]), 1, 0)
+        live = live + jnp.where((offsets[k] == distance) & (k < count), 1, 0)
     return live > 0
 
 
-def away(facts):
-    return 2 * facts[CORE_AT] - 1
-
-
-def pack_kernel(cotangent, states, copies, buffer, fetched, sent):
+def pack_kernel(cotangent, states, copies, buffer, fetched):
     first = pltpu.make_async_copy(cotangent, buffer.at[0], fetched.at[0])
     rest = pltpu.make_async_copy(states, buffer.at[pl.ds(1, states.shape[0])], fetched.at[1])
     first.start()
     rest.start()
     first.wait()
     rest.wait()
-    sends = [pltpu.make_async_copy(buffer, copies.at[t], sent.at[t]) for t in range(copies.shape[0])]
-    for send in sends:
-        send.start()
-    for send in sends:
-        send.wait()
-
-
-def lend_kernel(facts, tiles, lent, buffer, arrival):
+    for t in range(copies.shape[0]):
+        copies[t] = buffer[...]
+
+
+def lend_kernel(core, count, offsets_hbm, wet_hbm, tiles, inverse_hbm, lent, shared, offsets, wet, buffer, inverse, arrival):
+    fetches = [
+        pltpu.make_async_copy(source, target, arrival.at[n])
+        for n, (source, target) in enumerate(
+            [(offsets_hbm, offsets), (wet_hbm, wet), (inverse_hbm, inverse)]
+        )
+    ]
+    for fetch in fetches:
+        fetch.start()
+    fetches[0].wait()
     slots = tiles.shape[1]
-    distance = -2 * away(facts)
-    fetch = pltpu.make_async_copy(tiles.at[0, slot_at(facts, slots, distance)], buffer, arrival)
-    fetch.start()
-    fetch.wait()
-    lent[...] = jnp.where(slot_live(facts, slots, distance), buffer[...].astype(jnp.float32), 0.0)
-
-
-def share_kernel(facts, inverse_hbm, shared, inverse, arrival):
-    fetch = pltpu.make_async_copy(inverse_hbm, inverse, arrival)
-    fetch.start()
-    fetch.wait()
+    distance = -2 * (2 * core[0] - 1)
+    tile = pltpu.make_async_copy(tiles.at[0, slot_at(offsets.at[0], slots, distance)], buffer, arrival.at[3])
+    tile.start()
+    for fetch in fetches[1:]:
+        fetch.wait()
     columns, levels, _ = inverse.shape
     lane = lax.broadcasted_iota(jnp.int32, (levels, levels), 1)
     row = lax.broadcasted_iota(jnp.int32, (8, levels), 1)
     for c in range(columns):
         at = slice(c * levels, (c + 1) * levels)
-        shared[0:levels, at] = jnp.where(lane < facts[WET_AT + c], inverse[c], 0.0)
-        shared[levels : levels + 8, at] = jnp.where(row < facts[WET_AT + c], 1.0, 0.0)
-
-
-def blocks_kernel(facts, shared, borrowed, tile_out, blocks, wet_out):
+        shared[0:levels, at] = jnp.where(lane < wet[c], inverse[c], 0.0)
+        shared[levels : levels + 8, at] = jnp.where(row < wet[c], 1.0, 0.0)
+    tile.wait()
+    lent[...] = jnp.where(slot_live(offsets.at[0], count[0], slots, distance), buffer[...].astype(jnp.float32), 0.0)
+
+
+def round_kernel(borrowed, tile_out):
+    tile_out[...] = borrowed[...].astype(jnp.bfloat16)
+
+
+def gathered_kernel(facts, gathered, shared, uptake_weight, start, slopes, blocks, wet_out):
+    peers, _, few, _ = gathered.shape
+    for t in range(peers):
+        at = slice(t * few, (t + 1) * few)
+        start[at, :] = gathered[t, 0]
+        for n in range(slopes.shape[0]):
+            slopes[n, at, :] = gathered[t, 1 + n]
+    weight_high, weight_low = halves(uptake_weight[...])
+    for n in range(slopes.shape[0]):
+        state_high, state_low = halves(slopes[n])
+        reach = jnp.tanh(dot_split(weight_high, weight_low, state_high, state_low))
+        slopes[n] = 1.0 - reach * reach
     own = facts[CORE_AT]
     levels = shared.shape[1] - 8
     boxes = shared.shape[2]
@@ -111,27 +124,12 @@
     for which in range(2):
         side = own if which == 0 else 1 - own
         for s in range(spans):
-            part = shared[side, 0:levels, s * SPAN : (s + 1) * SPAN]
-            full = jnp.concatenate([part] * (SPAN // levels), axis=0)
-            high, low = halves(jnp.where(same, full, 0.0))
-            blocks[0, which * spans + s] = high
-            blocks[1, which * spans + s] = low
+            high, low = halves(shared[side, 0:levels, s * SPAN : (s + 1) * SPAN])
+            full_high = jnp.concatenate([high] * (SPAN // levels), axis=0)
+            full_low = jnp.concatenate([low] * (SPAN // levels), axis=0)
+            blocks[0, which * spans + s] = jnp.where(same, full_high, jnp.zeros_like(full_high))
+            blocks[1, which * spans + s] = jnp.where(same, full_low, jnp.zeros_like(full_low))
         wet_out[which : which + 1, :] = shared[side, levels : levels + 1, :]
-    tile_out[...] = borrowed[...].astype(jnp.bfloat16)
-
-
-def gathered_kernel(gathered, uptake_weight, start, slopes):
-    peers, _, few, _ = gathered.shape
-    for t in range(peers):
-        at = slice(t * few, (t + 1) * few)
-        start[at, :] = gathered[t, 0]
-        for n in range(slopes.shape[0]):
-            slopes[n, at, :] = gathered[t, 1 + n]
-    weight_high, weight_low = halves(uptake_weight[...])
-    for n in range(slopes.shape[0]):
-        state_high, state_low = halves(slopes[n])
-        reach = jnp.tanh(dot_split(weight_high, weight_low, state_high, state_low))
-        slopes[n] = 1.0 - reach * reach
 
 
 def step_kernel(
@@ -139,7 +137,7 @@
     *, section, first, last,
 ):
     own = facts[CORE_AT]
-    direction = away(facts)
+    direction = 2 * own - 1
     slots, boxes = tiles.shape[1], tiles.shape[3]
     tracers = uptake_t.shape[0]
     spans = boxes // SPAN
@@ -161,7 +159,7 @@
 
     def term(distance):
         product = dot(own_high, tiles[0, slot_at(facts, slots, distance)])
-        return jnp.where(slot_live(facts, slots, distance), product, 0.0)
+        return jnp.where(slot_live(facts, facts[COUNT_AT], slots, distance), product, 0.0)
 
     def put(out, part, value):
         few = out.shape[0] // 2
@@ -208,9 +206,9 @@
     lean = pltpu.CompilerParams(vmem_limit_bytes=VMEM_LIMIT)
     dma = pltpu.SemaphoreType.DMA
     core_index = lax.axis_index("core")
-    x_index = lax.axis_index("x")
-    ylo_index = lax.axis_index("ylo")
-    ylo_size = lax.axis_size("ylo")
+    core = core_index.astype(jnp.int32).reshape(1)
+    x_index = lax.axis_index("x").astype(jnp.int32).reshape(1)
+    ylo_index, ylo_size = lax.axis_index("ylo"), lax.axis_size("ylo")
     joined = lax.axis_index("yhi") + ylo_index == 1
     groups = neighbour_groups(sizes)
 
@@ -220,52 +218,52 @@
     copies = pl.pallas_call(
         pack_kernel,
         in_specs=[hbm] * 2,
-        out_specs=hbm,
+        out_specs=vmem,
         out_shape=shape((peers, 1 + sections, tracers_here, boxes), f32),
-        scratch_shapes=[pltpu.VMEM((1 + sections, tracers_here, boxes), f32), dma((2,)), dma((peers,))],
+        scratch_shapes=[pltpu.VMEM((1 + sections, tracers_here, boxes), f32), dma((2,))],
         compiler_params=lean,
         name="pack",
     )(in_hbm(cotangent), in_hbm(states))
     gathered = lax.all_to_all(copies, TRACER, split_axis=0, concat_axis=0, tiled=True)
-    facts = jnp.concatenate(
-        [tile_offset.reshape(-1), tile_count, jnp.stack([core_index, x_index]).astype(jnp.int32), wet_levels]
-    )
-    lent = pl.pallas_call(
+    facts = jnp.concatenate([tile_offset.reshape(-1), tile_count, core, x_index])
+    lent, shared = pl.pallas_call(
         lend_kernel,
-        in_specs=[smem, hbm],
-        out_specs=vmem,
-        out_shape=shape((boxes, boxes), f32),
-        scratch_shapes=[pltpu.VMEM((boxes, boxes), bf16), dma],
+        in_specs=[smem] * 2 + [hbm] * 4,
+        out_specs=[vmem] * 2,
+        out_shape=[shape((boxes, boxes), f32), shape((levels + 8, boxes), f32)],
+        scratch_shapes=[
+            pltpu.SMEM(tile_offset.shape, jnp.int32),
+            pltpu.SMEM((columns,), jnp.int32),
+            pltpu.VMEM((boxes, boxes), bf16),
+            pltpu.VMEM((columns, levels, levels), f32),
+            dma((4,)),
+        ],
         compiler_params=lean,
         name="lend",
-    )(facts, in_hbm(explicit_tiles))
+    )(core, tile_count, *map(in_hbm, (tile_offset, wet_levels, explicit_tiles, implicit_inverse)))
     borrowed = lax.ppermute(lent, "core", [(0, 1), (1, 0)])
-    shared = pl.pallas_call(
-        share_kernel,
-        in_specs=[smem, hbm],
+    shared = lax.all_gather(shared, "core")
+    borrowed = pl.pallas_call(
+        round_kernel,
+        in_specs=[vmem],
         out_specs=vmem,
-        out_shape=shape((levels + 8, boxes), f32),
-        scratch_shapes=[pltpu.VMEM((columns, levels, levels), f32), dma],
+        out_shape=shape((boxes, boxes), bf16),
         compiler_params=lean,
-        name="share",
-    )(facts, in_hbm(implicit_inverse))
-    shared = lax.all_gather(shared, "core")
-    borrowed, blocks, wet = pl.pallas_call(
-        blocks_kernel,
-        in_specs=[smem] + [vmem] * 2,
-        out_specs=[vmem] * 3,
-        out_shape=[shape((boxes, boxes), bf16), shape((2, 2 * spans, SPAN, SPAN), bf16), shape((2, boxes), f32)],
-        compiler_params=lean,
-        name="blocks",
-    )(facts, shared, borrowed)
-    start, slopes = pl.pallas_call(
+        name="round",
+    )(borrowed)
+    start, slopes, blocks, wet = pl.pallas_call(
         gathered_kernel,
-        in_specs=[vmem] * 2,
-        out_specs=[vmem] * 2,
-        out_shape=[shape((tracers, boxes), f32), shape((sections, tracers, boxes), f32)],
+        in_specs=[smem] + [vmem] * 3,
+        out_specs=[vmem] * 4,
+        out_shape=[
+            shape((tracers, boxes), f32),
+            shape((sections, tracers, boxes), f32),
+            shape((2, 2 * spans, SPAN, SPAN), bf16),
+            shape((2, boxes), f32),
+        ],
         compiler_params=lean,
         name="gathered",
-    )(gathered, uptake_weight)
+    )(facts, gathered, shared, uptake_weight)
     adjoint = lax.all_gather(start, "core")
     uptake_t, release_t = uptake_weight.T, release_weight.T
     last_rows = ylo_size * tracers_here

time: 100 us -> 100 us (level)
  waiting for transfers between devices: 5.06 us -> 6.61 us
    all_to_all x1, waiting for transfers between devices: 5.06 us -> 6.61 us  [local(): lax.all_to_all(copies, TRACER, split_axis=0, concat_axis=0, tiled=True)]
    pallas_call x5 -> x4, Pallas kernels: 7.65 us -> 6.68 us  [the longest x1 2.83 us: local(): pl.pallas_call(lend_kernel, in_specs=[smem] * 2 + [hbm] * 4, out_specs=[v...]
  transfers between devices with their start and end apart: 2 -> 2, of which waited for: 1 -> 1; matrix products, arithmetic and copies ran while one was open for 0% -> 0% of each run, Pallas kernels for 4% -> 3%
where the time goes in v6:
time: 100 us; the launch traced here: 99.3 us
  blocking collectives  63.6 us (64%)
  Pallas kernels  14.8 us (15%)
  starting transfers between devices  12.5 us (12%)
  waiting for transfers between devices  6.61 us (7%)
    all_gather x1, blocking collectives, local(): lax.all_gather(passed, 'ylo')  35.7 us
    all_gather x6, blocking collectives, local(): adjoint = lax.all_gather(keep, 'core')  11.8 us
    all_gather x6, blocking collectives, local(): arrived = lax.all_gather(send, EVERY, axis_index_groups=groups)  11.8 us
    ppermute x1, starting transfers between devices, local(): borrowed = lax.ppermute(lent, 'core', [(0, 1), (1, 0)])  9 us
    pallas_call x6, Pallas kernels, local(): pl.pallas_call(step, in_specs=[smem] + [vmem] * 8, out_specs=[vmem] * 2,...  8.12 us
    all_to_all x1, waiting for transfers between devices, local(): lax.all_to_all(copies, TRACER, split_axis=0, concat_axis=0, tiled=True)  6.61 us
    all_to_all x1, starting transfers between devices, local(): lax.all_to_all(copies, TRACER, split_axis=0, concat_axis=0, tiled=True)  3.48 us
    pallas_call x1, Pallas kernels, local(): pl.pallas_call(lend_kernel, in_specs=[smem] * 2 + [hbm] * 4, out_specs=[v...  2.83 us
  transfers between devices with their start and end apart: 2, of which 1 were waited for; matrix products, arithmetic and copies ran while one was open for 0% of the time, Pallas kernels for 3%

profile of v6, /device:TPU:1, one launch (start us, length us, event | category | flops | bytes accessed | tf_op | source)
XLA Modules:
  0.0 99.3 jit_solution(11295784167915232062)
XLA Ops:
  0.0 0.0 copy-start.3
  0.0 0.0 copy-start.1
  0.0 0.0 copy-start.2
  0.7 2.8 %lend.1 = (f32[512,512]{1,0:T(8,128)}, f32[40,512]{1,0:T(8,128)S(1)}) custom-call(s32[1]{0:T(128)} %bitcast.1.core, s32[1]{0:T(128)S(6)} %copy.14.count, s32[1,5]{1,0:T(1,128)} %offsets_hbm.1, s32[16]{0:T(128)} %wet_hbm.1, bf16[1,5,512,512]{3,2,1,0:T(8,128)(2,1)} %refs_2_.11, f32[16,32,32]{2,1,0:T(8,128)} %inverse_hbm.1), custom_call_target="tpu_custom_call" | custom-call | tf_op jit(solution)/shard_map/lend/pallas_call | solution.py:229
  3.5 0.0 copy-start
  3.5 9.0 %collective-permute-start = (f32[512,512]{1,0:T(8,128)}, f32[512,512]{1,0:T(8,128)}, u32[]{:S(2)}, u32[]{:S(2)}) collective-permute-start(f32[512,512]{1,0:T(8,128)} %get-tuple-element.26), channel_id=1, source_target_pairs={{0,8},{8,0},{1,9},{9,1},{2,10},{10,2},{3,11},{11,3},{4,12},{12,4},... | collective-permute-start | bytes 3145736 | tf_op jit(solution)/shard_map/ppermute | solution.py:244
  12.6 1.6 %pack.1 = f32[8,7,4,512]{3,2,1,0:T(4,128)} custom-call(f32[4,512]{1,0:T(4,128)} %cotangent.1, f32[6,4,512]{2,1,0:T(4,128)} %states.1), custom_call_target="tpu_custom_call" | custom-call | tf_op jit(solution)/shard_map/pack/pallas_call | solution.py:218
  14.2 3.5 %all-to-all-start = ((f32[8,7,4,512]{3,2,1,0:T(4,128)}), f32[8,7,4,512]{3,2,1,0:T(4,128)S(1)}, u32[]{:S(2)}, u32[]{:S(2)}) async-start(f32[8,7,4,512]{3,2,1,0:T(4,128)} %pack.1), calls=%async_computation | async-start | bytes 917504 | tf_op jit(solution)/shard_map/all_to_all | solution.py:227
  17.7 0.0 copy-done.1
  17.7 0.1 copy.12
  17.8 0.0 copy-done.2
  17.8 0.1 copy.13
  17.8 1.9 %all-gather = f32[80,512]{1,0:T(8,128)S(1)} all-gather(f32[40,512]{1,0:T(8,128)S(1)} %get-tuple-element.23), channel_id=2, replica_groups=mesh['z'=16,'yhi'=2,'core'=2,'x'=4,'ylo'=2] {'core'}, dimensions={0}, use_global_device_ids=true | all-gather | bytes 245760 | tf_op jit(solution)/shard_map/all_gather | solution.py:245
  19.8 0.0 copy-done.3
  19.8 0.1 pad_add_fusion.facts.refs_0_
  19.8 6.6 %all-to-all-done.gathered = f32[8,7,4,512]{3,2,1,0:T(4,128)S(1)} async-done(((f32[8,7,4,512]{3,2,1,0:T(4,128)}), f32[8,7,4,512]{3,2,1,0:T(4,128)S(1)}, u32[]{:S(2)}, u32[]{:S(2)}) %all-to-all-start) | async-done | bytes 458784 | tf_op jit(solution)/shard_map/all_to_all | solution.py:227
  26.5 0.9 gathered.1
  27.4 2.4 %all-gather.1 = f32[64,512]{1,0:T(8,128)S(1)} all-gather(f32[32,512]{1,0:T(8,128)S(1)} %get-tuple-element.25), channel_id=3, replica_groups=mesh['z'=16,'yhi'=2,'core'=2,'x'=4,'ylo'=2] {'core'}, dimensions={0}, use_global_device_ids=true | all-gather | bytes 196608 | tf_op jit(solution)/shard_map/all_gather | solution.py:267
  29.8 0.0 collective-permute-done.borrowed
  29.8 1.3 %round.1.refs_3_ = bf16[512,512]{1,0:T(8,128)(2,1)S(1)} custom-call(f32[512,512]{1,0:T(8,128)} %collective-permute-done.borrowed), custom_call_target="tpu_custom_call" | custom-call | tf_op jit(solution)/shard_map/round/pallas_call | solution.py:246
  31.1 0.0 copy-done
  31.1 1.4 %shard_map.91 = (f32[64,512]{1,0:T(8,128)S(1)}, f32[64,512]{1,0:T(8,128)S(1)}) custom-call(s32[8]{0:T(128)S(1)} %pad_add_fusion.facts.refs_0_, f32[2,32,512]{2,1,0:T(8,128)S(1)} %bitcast.52, bf16[1,5,512,512]{3,2,1,0:T(8,128)(2,1)S(1)} %copy-done, bf16[512,512]{1,0:T(8,128)(2,1)S(1)} %round.1.refs_3_, ...), custom_call_target="tpu_custom_call" | custom-call | tf_op jit(solution)/shard_map/pallas_call | solution.py:277
  32.5 2.0 %all-gather.2 = f32[128,512]{1,0:T(8,128)S(1)} all-gather(f32[64,512]{1,0:T(8,128)S(1)} %get-tuple-element.30), channel_id=4, replica_groups={{9,16},{8,0},{11,18},{10,2},{13,20},{12,4},{15,22},{14,6},{24,33},{25,1..., dimensions={0}, use_global_device_ids=true | all-gather | bytes 393216 | tf_op jit(solution)/shard_map/all_gather | solution.py:288
  34.5 2.0 %all-gather.3 = f32[128,512]{1,0:T(8,128)S(1)} all-gather(f32[64,512]{1,0:T(8,128)S(1)} %bitcast_add_fusion.4), channel_id=5, replica_groups=mesh['z'=16,'yhi'=2,'core'=2,'x'=4,'ylo'=2] {'core'}, dimensions={0}, use_global_device_ids=true | all-gather | bytes 393216 | tf_op jit(solution)/shard_map/all_gather | solution.py:290
  36.5 1.4 %shard_map.92 = (f32[64,512]{1,0:T(8,128)S(1)}, f32[64,512]{1,0:T(8,128)S(1)}) custom-call(s32[8]{0:T(128)S(1)} %pad_add_fusion.facts.refs_0_, f32[2,64,512]{2,1,0:T(8,128)S(1)} %bitcast.35, bf16[1,5,512,512]{3,2,1,0:T(8,128)(2,1)S(1)} %copy-done, bf16[512,512]{1,0:T(8,128)(2,1)S(1)} %round.1.refs_3_, ...), custom_call_target="tpu_custom_call" | custom-call | tf_op jit(solution)/shard_map/pallas_call | solution.py:277
  37.8 2.0 %all-gather.4 = f32[128,512]{1,0:T(8,128)S(1)} all-gather(f32[64,512]{1,0:T(8,128)S(1)} %get-tuple-element.32), channel_id=6, replica_groups={{9,16},{8,0},{11,18},{10,2},{13,20},{12,4},{15,22},{14,6},{24,33},{25,1..., dimensions={0}, use_global_device_ids=true | all-gather | bytes 393216 | tf_op jit(solution)/shard_map/all_gather | solution.py:288
  39.9 2.0 %all-gather.5 = f32[128,512]{1,0:T(8,128)S(1)} all-gather(f32[64,512]{1,0:T(8,128)S(1)} %bitcast_add_fusion.3), channel_id=7, replica_groups=mesh['z'=16,'yhi'=2,'core'=2,'x'=4,'ylo'=2] {'core'}, dimensions={0}, use_global_device_ids=true | all-gather | bytes 393216 | tf_op jit(solution)/shard_map/all_gather | solution.py:290
  41.9 1.4 %shard_map.93 = (f32[64,512]{1,0:T(8,128)S(1)}, f32[64,512]{1,0:T(8,128)S(1)}) custom-call(s32[8]{0:T(128)S(1)} %pad_add_fusion.facts.refs_0_, f32[2,64,512]{2,1,0:T(8,128)S(1)} %bitcast.36, bf16[1,5,512,512]{3,2,1,0:T(8,128)(2,1)S(1)} %copy-done, bf16[512,512]{1,0:T(8,128)(2,1)S(1)} %round.1.refs_3_, ...), custom_call_target="tpu_custom_call" | custom-call | tf_op jit(solution)/shard_map/pallas_call | solution.py:277
  43.2 2.0 %all-gather.6 = f32[128,512]{1,0:T(8,128)S(1)} all-gather(f32[64,512]{1,0:T(8,128)S(1)} %get-tuple-element.34), channel_id=8, replica_groups={{9,16},{8,0},{11,18},{10,2},{13,20},{12,4},{15,22},{14,6},{24,33},{25,1..., dimensions={0}, use_global_device_ids=true | all-gather | bytes 393216 | tf_op jit(solution)/shard_map/all_gather | solution.py:288
  45.2 2.0 %all-gather.7 = f32[128,512]{1,0:T(8,128)S(1)} all-gather(f32[64,512]{1,0:T(8,128)S(1)} %bitcast_add_fusion.2), channel_id=9, replica_groups=mesh['z'=16,'yhi'=2,'core'=2,'x'=4,'ylo'=2] {'core'}, dimensions={0}, use_global_device_ids=true | all-gather | bytes 393216 | tf_op jit(solution)/shard_map/all_gather | solution.py:290
  47.2 1.4 %shard_map.94 = (f32[64,512]{1,0:T(8,128)S(1)}, f32[64,512]{1,0:T(8,128)S(1)}) custom-call(s32[8]{0:T(128)S(1)} %pad_add_fusion.facts.refs_0_, f32[2,64,512]{2,1,0:T(8,128)S(1)} %bitcast.37, bf16[1,5,512,512]{3,2,1,0:T(8,128)(2,1)S(1)} %copy-done, bf16[512,512]{1,0:T(8,128)(2,1)S(1)} %round.1.refs_3_, ...), custom_call_target="tpu_custom_call" | custom-call | tf_op jit(solution)/shard_map/pallas_call | solution.py:277
  48.6 2.0 %all-gather.8 = f32[128,512]{1,0:T(8,128)S(1)} all-gather(f32[64,512]{1,0:T(8,128)S(1)} %get-tuple-element.36), channel_id=10, replica_groups={{9,16},{8,0},{11,18},{10,2},{13,20},{12,4},{15,22},{14,6},{24,33},{25,1..., dimensions={0}, use_global_device_ids=true | all-gather | bytes 393216 | tf_op jit(solution)/shard_map/all_gather | solution.py:288
  50.6 2.0 %all-gather.9 = f32[128,512]{1,0:T(8,128)S(1)} all-gather(f32[64,512]{1,0:T(8,128)S(1)} %bitcast_add_fusion.1), channel_id=11, replica_groups=mesh['z'=16,'yhi'=2,'core'=2,'x'=4,'ylo'=2] {'core'}, dimensions={0}, use_global_device_ids=true | all-gather | bytes 393216 | tf_op jit(solution)/shard_map/all_gather | solution.py:290
  52.6 1.4 %shard_map.95 = (f32[64,512]{1,0:T(8,128)S(1)}, f32[64,512]{1,0:T(8,128)S(1)}) custom-call(s32[8]{0:T(128)S(1)} %pad_add_fusion.facts.refs_0_, f32[2,64,512]{2,1,0:T(8,128)S(1)} %bitcast.38, bf16[1,5,512,512]{3,2,1,0:T(8,128)(2,1)S(1)} %copy-done, bf16[512,512]{1,0:T(8,128)(2,1)S(1)} %round.1.refs_3_, ...), custom_call_target="tpu_custom_call" | custom-call | tf_op jit(solution)/shard_map/pallas_call | solution.py:277
  53.9 2.0 %all-gather.10 = f32[128,512]{1,0:T(8,128)S(1)} all-gather(f32[64,512]{1,0:T(8,128)S(1)} %get-tuple-element.38), channel_id=12, replica_groups={{9,16},{8,0},{11,18},{10,2},{13,20},{12,4},{15,22},{14,6},{24,33},{25,1..., dimensions={0}, use_global_device_ids=true | all-gather | bytes 393216 | tf_op jit(solution)/shard_map/all_gather | solution.py:288
  55.9 2.0 %all-gather.11 = f32[128,512]{1,0:T(8,128)S(1)} all-gather(f32[64,512]{1,0:T(8,128)S(1)} %bitcast_add_fusion), channel_id=13, replica_groups=mesh['z'=16,'yhi'=2,'core'=2,'x'=4,'ylo'=2] {'core'}, dimensions={0}, use_global_device_ids=true | all-gather | bytes 393216 | tf_op jit(solution)/shard_map/all_gather | solution.py:290
  57.9 1.4 %shard_map.96 = (f32[16,512]{1,0:T(8,128)S(1)}, f32[16,512]{1,0:T(8,128)S(1)}) custom-call(s32[8]{0:T(128)S(1)} %pad_add_fusion.facts.refs_0_, f32[2,64,512]{2,1,0:T(8,128)S(1)} %bitcast.34, bf16[1,5,512,512]{3,2,1,0:T(8,128)(2,1)S(1)} %copy-done, bf16[512,512]{1,0:T(8,128)(2,1)S(1)} %round.1.refs_3_, ...), custom_call_target="tpu_custom_call" | custom-call | tf_op jit(solution)/shard_map/pallas_call | solution.py:277
  59.3 1.9 %all-gather.12 = f32[32,512]{1,0:T(8,128)S(1)} all-gather(f32[16,512]{1,0:T(8,128)S(1)} %get-tuple-element.40), channel_id=14, replica_groups={{9,16},{8,0},{11,18},{10,2},{13,20},{12,4},{15,22},{14,6},{24,33},{25,1..., dimensions={0}, use_global_device_ids=true | all-gather | bytes 98304 | tf_op jit(solution)/shard_map/all_gather | solution.py:288
  61.1 1.9 %all-gather.13 = f32[32,512]{1,0:T(8,128)S(1)} all-gather(f32[16,512]{1,0:T(8,128)S(1)} %bitcast_add_fusion.5), channel_id=15, replica_groups=mesh['z'=16,'yhi'=2,'core'=2,'x'=4,'ylo'=2] {'core'}, dimensions={0}, use_global_device_ids=true | all-gather | bytes 98304 | tf_op jit(solution)/shard_map/all_gather | solution.py:290
  63.0 35.7 %all_gather.116 = f32[2,4,512]{2,1,0:T(4,128)S(1)} all-gather(f32[1,4,512]{2,1,0:T(4,128)S(1)} %constant_dynamic-slice_fusion), channel_id=1, replica_groups=mesh['z'=16,'yhi'=2,'core'=2,'x'=4,'ylo'=2] {'ylo'}, dimensions={0}, use_global_device_ids=true | all-gather | bytes 24576 | tf_op jit(solution)/shard_map/all_gather | solution.py:295
  98.7 0.6 select_bitcast_fusion
  (11 shorter events, 0.1 us)
Async XLA Ops:
  0.0 19.8 %copy-start.3 = (s32[1,5]{1,0:T(1,128)S(1)}, s32[1,5]{1,0:T(1,128)}, u32[]{:S(2)}) copy-start(s32[1,5]{1,0:T(1,128)} %offsets_hbm.1) | copy-start | bytes 64
  0.0 17.7 %copy-start.1 = (f32[32,32]{1,0:T(8,128)S(1)}, f32[32,32]{1,0:T(8,128)}, u32[]{:S(2)}) copy-start(f32[32,32]{1,0:T(8,128)} %uptake_weight.1) | copy-start | bytes 12292
  0.0 17.8 %copy-start.2 = (f32[32,32]{1,0:T(8,128)S(1)}, f32[32,32]{1,0:T(8,128)}, u32[]{:S(2)}) copy-start(f32[32,32]{1,0:T(8,128)} %param.17) | copy-start | bytes 12292
  3.5 27.6 %copy-start = (bf16[1,5,512,512]{3,2,1,0:T(8,128)(2,1)S(1)}, bf16[1,5,512,512]{3,2,1,0:T(8,128)(2,1)}, u32[]{:S(2)}) copy-start(bf16[1,5,512,512]{3,2,1,0:T(8,128)(2,1)} %refs_2_.11) | copy-start | bytes 7864324
  3.5 26.3 %collective-permute-start = (f32[512,512]{1,0:T(8,128)}, f32[512,512]{1,0:T(8,128)}, u32[]{:S(2)}, u32[]{:S(2)}) collective-permute-start(f32[512,512]{1,0:T(8,128)} %get-tuple-element.26), channel_id=1, source_target_pairs={{0,8},{8,0},{1,9},{9,1},{2,10},{10,2},{3,11},{11,3},{4,12},{12,4},... | collective-permute-start | bytes 3145736 | tf_op jit(solution)/shard_map/ppermute | solution.py:244
  14.2 12.3 %all-to-all-start = ((f32[8,7,4,512]{3,2,1,0:T(4,128)}), f32[8,7,4,512]{3,2,1,0:T(4,128)S(1)}, u32[]{:S(2)}, u32[]{:S(2)}) async-start(f32[8,7,4,512]{3,2,1,0:T(4,128)} %pack.1), calls=%async_computation | async-start | bytes 917504 | tf_op jit(solution)/shard_map/all_to_all | solution.py:227

commit v7 on v6

v7 whole, which is shorter than its diff:
```python
import jax
import jax.numpy as jnp
from jax import lax
from jax.experimental import pallas as pl
from jax.experimental.pallas import tpu as pltpu
from jax.sharding import Mesh, PartitionSpec as P


REGION = ("z", "yhi", "core")
TRACER = ("x", "ylo")
EVERY = REGION + TRACER
SPAN = 256
VMEM_LIMIT = 8 * 2**20
COUNT_AT, CORE_AT = 5, 6


def neighbour_groups(sizes):
    nq, nx, ny = sizes

    def at(chip, core, x, ylo):
        return (((chip % nq) * 2 + core) * nx + x) * ny + ylo

    groups = []
    for q in range(nq):
        for x in range(nx):
            joined, alone = (1, 0) if q % 2 == 0 else (0, 1)
            groups.append([at(q, 1, x, joined), at(q + 1, 0, x, 1 - joined)])
            groups.append([at(q, 1, x, alone), at(q, 0, x, alone)])
    return groups


def halves(value):
    high = value.astype(jnp.bfloat16)
    low = (value - high.astype(jnp.float32)).astype(jnp.bfloat16)
    return high, low


def dot(a, b):
    return lax.dot_general(a, b, (((1,), (0,)), ((), ())), preferred_element_type=jnp.float32)


def dot_split(a_high, a_low, b_high, b_low):
    rows = a_high.shape[0]
    both = dot(jnp.concatenate([a_high, a_low], axis=0), b_high)
    return both[:rows] + both[rows:] + dot(a_high, b_low)


def slot_at(offsets, slots, distance):
    slot = jnp.int32(0)
    for k in range(slots):
        slot = slot + jnp.where(offsets[k] == distance, k, 0)
    return slot


def slot_live(offsets, slots, distance):
    live = jnp.int32(0)
    for k in range(slots):
        live = live + jnp.where((offsets[k] == distance) & (k < offsets[COUNT_AT]), 1, 0)
    return live > 0


def pack_kernel(cotangent, states, copies, buffer, fetched):
    first = pltpu.make_async_copy(cotangent, buffer.at[0], fetched.at[0])
    rest = pltpu.make_async_copy(states, buffer.at[pl.ds(1, states.shape[0])], fetched.at[1])
    first.start()
    rest.start()
    first.wait()
    rest.wait()
    for t in range(copies.shape[0]):
        copies[t] = buffer[...]


def lend_kernel(facts, tiles, lent, buffer, arrival):
    slots = tiles.shape[1]
    distance = 2 - 4 * facts[CORE_AT]
    fetch = pltpu.make_async_copy(tiles.at[0, slot_at(facts, slots, distance)], buffer, arrival)
    fetch.start()
    fetch.wait()
    lent[...] = jnp.where(slot_live(facts, slots, distance), buffer[...].astype(jnp.float32), 0.0)


def arrange_kernel(facts, wet, tiles, inverse, ordered, shared, upper, arrival):
    slots = tiles.shape[1]
    direction = 2 * facts[CORE_AT] - 1
    uses = (direction, 2 * direction, 0, -direction)
    fetches = [
        pltpu.make_async_copy(tiles.at[0, slot_at(facts, slots, distance)], ordered.at[n], arrival.at[n])
        for n, distance in enumerate(uses)
    ]
    for fetch in fetches:
        fetch.start()
    columns, levels, _ = inverse.shape
    lane = lax.broadcasted_iota(jnp.int32, (levels, levels), 1)
    row = lax.broadcasted_iota(jnp.int32, (8, levels), 1)
    for c in range(columns):
        at = slice(c * levels, (c + 1) * levels)
        shared[0:levels, at] = jnp.where(lane < wet[c], inverse[c], 0.0)
        shared[levels : levels + 8, at] = jnp.where(row < wet[c], 1.0, 0.0)
    upper[...] = jnp.full(upper.shape, facts[CORE_AT], jnp.int32).astype(jnp.float32)
    for fetch in fetches:
        fetch.wait()
    for n, distance in enumerate(uses):

        @pl.when(jnp.logical_not(slot_live(facts, slots, distance)))
        def _():
            ordered[n] = jnp.zeros(ordered.shape[1:], ordered.dtype)


def round_kernel(borrowed, tile_out):
    tile_out[...] = borrowed[...].astype(jnp.bfloat16)


def gathered_kernel(gathered, shared, uptake_weight, start, slopes):
    peers, _, few, _ = gathered.shape
    tracers = uptake_weight.shape[0]
    start[tracers:, :] = shared[...]
    for t in range(peers):
        at = slice(t * few, (t + 1) * few)
        start[at, :] = gathered[t, 0]
        for n in range(slopes.shape[0]):
            slopes[n, at, :] = gathered[t, 1 + n]
    weight_high, weight_low = halves(uptake_weight[...])
    for n in range(slopes.shape[0]):
        state_high, state_low = halves(slopes[n])
        reach = jnp.tanh(dot_split(weight_high, weight_low, state_high, state_low))
        slopes[n] = 1.0 - reach * reach


def lay_out_blocks(adjoint, tracers, levels, blocks, wet):
    spans = adjoint.shape[2] // SPAN
    same = (
        lax.broadcasted_iota(jnp.int32, (SPAN, SPAN), 0) // levels
        == lax.broadcasted_iota(jnp.int32, (SPAN, SPAN), 1) // levels
    )
    for side in range(2):
        for s in range(spans):
            high, low = halves(adjoint[side, tracers : tracers + levels, s * SPAN : (s + 1) * SPAN])
            full_high = jnp.concatenate([high] * (SPAN // levels), axis=0)
            full_low = jnp.concatenate([low] * (SPAN // levels), axis=0)
            blocks[0, side * spans + s] = jnp.where(same, full_high, jnp.zeros_like(full_high))
            blocks[1, side * spans + s] = jnp.where(same, full_low, jnp.zeros_like(full_low))
        wet[side : side + 1, :] = adjoint[side, tracers + levels : tracers + levels + 1, :]


def step_kernel(adjoint, ordered, borrowed, upper, slopes, uptake_t, release_t, *rest, section, levels, first):
    tracers = uptake_t.shape[0]
    if first:
        send, keep, blocks, wet, settled = rest
        lay_out_blocks(adjoint, tracers, levels, blocks, wet)
        pair = (adjoint[0, 0:tracers, :], adjoint[1, 0:tracers, :])
    else:
        blocks, wet, send, keep, settled = rest
        pair = (
            wet[0:1, :] * (adjoint[0, 0:tracers, :] + adjoint[1, tracers:, :]),
            wet[1:2, :] * (adjoint[1, 0:tracers, :] + adjoint[0, tracers:, :]),
        )
    spans = adjoint.shape[2] // SPAN
    for side in range(2):
        high, low = halves(pair[side])
        for s in range(spans):
            at = slice(s * SPAN, (s + 1) * SPAN)
            k = side * spans + s
            settled[side, :, at] = dot_split(high[:, at], low[:, at], blocks[0, k], blocks[1, k])
    is_upper = upper[0:1, :] > 0.5
    own_high, own_low = halves(jnp.where(is_upper, settled[1], settled[0]))
    other = jnp.where(is_upper, settled[0], settled[1]).astype(jnp.bfloat16)
    send[0:tracers, :] = dot(own_high, ordered[0]) + dot(other, borrowed[...])
    send[tracers:, :] = dot(own_high, ordered[1])
    release_high, release_low = halves(release_t[...])
    pushed = slopes[section] * dot_split(release_high, release_low, own_high, own_low)
    pushed_high, pushed_low = halves(pushed)
    uptake_high, uptake_low = halves(uptake_t[...])
    keep[0:tracers, :] = dot(own_high, ordered[2]) + dot_split(uptake_high, uptake_low, pushed_high, pushed_low)
    keep[tracers:, :] = dot(own_high, ordered[3])


def local(
    cotangent,
    states,
    implicit_inverse,
    wet_levels,
    explicit_tiles,
    tile_offset,
    tile_count,
    uptake_weight,
    release_weight,
    *,
    sizes,
):
    tracers_here, boxes = cotangent.shape
    sections = states.shape[0]
    _, levels, _ = implicit_inverse.shape
    tracers = uptake_weight.shape[0]
    spans = boxes // SPAN
    peers = tracers // tracers_here
    f32, bf16 = jnp.float32, jnp.bfloat16
    shape = jax.ShapeDtypeStruct
    vmem = pl.BlockSpec(memory_space=pltpu.VMEM)
    smem = pl.BlockSpec(memory_space=pltpu.SMEM)
    hbm = pl.BlockSpec(memory_space=pltpu.HBM)
    lean = pltpu.CompilerParams(vmem_limit_bytes=VMEM_LIMIT)
    dma = pltpu.SemaphoreType.DMA
    core_index = lax.axis_index("core")
    core = core_index.astype(jnp.int32).reshape(1)
    ylo_index, ylo_size = lax.axis_index("ylo"), lax.axis_size("ylo")
    joined = lax.axis_index("yhi") + ylo_index == 1
    groups = neighbour_groups(sizes)

    def in_hbm(array):
        return pltpu.with_memory_space_constraint(array, pltpu.HBM)

    copies = pl.pallas_call(
        pack_kernel,
        in_specs=[hbm] * 2,
        out_specs=vmem,
        out_shape=shape((peers, 1 + sections, tracers_here, boxes), f32),
        scratch_shapes=[pltpu.VMEM((1 + sections, tracers_here, boxes), f32), dma((2,))],
        compiler_params=lean,
        name="pack",
    )(in_hbm(cotangent), in_hbm(states))
    gathered = lax.all_to_all(copies, TRACER, split_axis=0, concat_axis=0, tiled=True)
    facts = jnp.concatenate([tile_offset.reshape(-1), tile_count, core])
    lent = pl.pallas_call(
        lend_kernel,
        in_specs=[smem, hbm],
        out_specs=vmem,
        out_shape=shape((boxes, boxes), f32),
        scratch_shapes=[pltpu.VMEM((boxes, boxes), bf16), dma],
        compiler_params=lean,
        name="lend",
    )(facts, in_hbm(explicit_tiles))
    borrowed = lax.ppermute(lent, "core", [(0, 1), (1, 0)])
    ordered, shared, upper = pl.pallas_call(
        arrange_kernel,
        in_specs=[smem] * 2 + [hbm, vmem],
        out_specs=[vmem] * 3,
        out_shape=[
            shape((4, boxes, boxes), bf16),
            shape((levels + 8, boxes), f32),
            shape((8, boxes), f32),
        ],
        scratch_shapes=[dma((4,))],
        compiler_params=lean,
        name="arrange",
    )(facts, wet_levels, in_hbm(explicit_tiles), implicit_inverse)
    borrowed = pl.pallas_call(
        round_kernel,
        in_specs=[vmem],
        out_specs=vmem,
        out_shape=shape((boxes, boxes), bf16),
        compiler_params=lean,
        name="round",
    )(borrowed)
    start, slopes = pl.pallas_call(
        gathered_kernel,
        in_specs=[vmem] * 3,
        out_specs=[vmem] * 2,
        out_shape=[shape((tracers + levels + 8, boxes), f32), shape((sections, tracers, boxes), f32)],
        compiler_params=lean,
        name="gathered",
    )(gathered, shared, uptake_weight)
    adjoint = lax.all_gather(start, "core")
    uptake_t, release_t = uptake_weight.T, release_weight.T
    kept_shapes = [shape((2, 2 * spans, SPAN, SPAN), bf16), shape((2, boxes), f32)]
    kept = []
    for section in range(sections - 1, -1, -1):
        first = section == sections - 1

        def step(*refs, section=section, first=first):
            step_kernel(*refs, section=section, levels=levels, first=first)

        out_shape = [shape((2 * tracers, boxes), f32)] * 2 + kept_shapes * first
        send, keep, *made = pl.pallas_call(
            step,
            in_specs=[vmem] * (7 + len(kept)),
            out_specs=[vmem] * len(out_shape),
            out_shape=out_shape,
            scratch_shapes=[pltpu.VMEM((2, tracers, boxes), f32)],
            compiler_params=lean,
        )(adjoint, ordered, borrowed, upper, slopes, uptake_t, release_t, *kept)
        kept = made or kept
        if section == 0:
            rows = ylo_size * tracers_here
            at = (0, lax.axis_index("x") * rows, 0)
            send, keep = (
                lax.dynamic_slice(part.reshape(2, tracers, boxes), at, (2, rows, boxes)).reshape(2 * rows, boxes)
                for part in (send, keep)
            )
        arrived = lax.all_gather(send, EVERY, axis_index_groups=groups)
        keep = keep + lax.dynamic_index_in_dim(arrived, core_index, 0, keepdims=False)
        adjoint = lax.all_gather(keep, "core")
    mine = lax.dynamic_index_in_dim(adjoint, core_index, 0, keepdims=False)[:rows]
    theirs = lax.dynamic_index_in_dim(adjoint, 1 - core_index, 0, keepdims=False)[rows:]
    wet = lax.dynamic_index_in_dim(kept[1], core_index, 0, keepdims=True)
    result = (wet * (mine + theirs)).reshape(ylo_size, tracers_here, boxes)
    passed = lax.dynamic_index_in_dim(result, 1 - ylo_index, 0, keepdims=False)
    passed = lax.dynamic_index_in_dim(lax.all_gather(passed, "ylo"), 1 - ylo_index, 0, keepdims=False)
    return jnp.where(joined, lax.dynamic_index_in_dim(result, ylo_index, 0, keepdims=False), passed)


def solution(mesh):
    regions, tracer_devices = mesh.devices.shape
    nq, nx, ny = regions // 2, tracer_devices // 2, 2
    fine = Mesh(mesh.devices.reshape(nq // 2, 2, 2, nx, ny), EVERY)
    placed = (
        P(TRACER, REGION),
        P(None, TRACER, REGION),
        P(REGION, None, None),
        P(REGION),
        P(REGION, None, None, None),
        P(REGION, None),
        P(REGION),
        P(),
        P(),
    )

    def body(*args):
        return local(*args, sizes=(nq, nx, ny))

    return jax.shard_map(body, mesh=fine, in_specs=placed, out_specs=P(TRACER, REGION), check_vma=False)
```

time: 100 us -> 97.6 us (0.976)
  blocking collectives: 63.6 us -> 61.8 us
    all_gather x1 -> x0, blocking collectives: 1.92 us -> none  [local(): shared = lax.all_gather(shared, 'core')]
    pallas_call x8 -> x9, Pallas kernels: 11.9 us -> 11.1 us  [the longest x6 5.85 us: local(): pl.pallas_call(step, in_specs=[vmem] * (7 + len(kept)), out_specs=[vmem]...]
  transfers between devices with their start and end apart: 2 -> 2, of which waited for: 1 -> 1; matrix products, arithmetic and copies ran while one was open for 0% -> 0% of each run, Pallas kernels for 3% -> 4%
where the time goes in v7:
time: 97.6 us; the launch traced here: 96.9 us
  blocking collectives  61.8 us (63%)
  Pallas kernels  14 us (14%)
  starting transfers between devices  12.2 us (12%)
  waiting for transfers between devices  6.33 us (6%)
  other arithmetic  1.44 us (1%)
    all_gather x1, blocking collectives, local(): lax.all_gather(passed, 'ylo')  35.7 us
    all_gather x6, blocking collectives, local(): arrived = lax.all_gather(send, EVERY, axis_index_groups=groups)  11.8 us
    all_gather x6, blocking collectives, local(): adjoint = lax.all_gather(keep, 'core')  11.8 us
    ppermute x1, starting transfers between devices, local(): borrowed = lax.ppermute(lent, 'core', [(0, 1), (1, 0)])  8.74 us
    all_to_all x1, waiting for transfers between devices, local(): lax.all_to_all(copies, TRACER, split_axis=0, concat_axis=0, tiled=True)  6.32 us
    pallas_call x6, Pallas kernels, local(): pl.pallas_call(step, in_specs=[vmem] * (7 + len(kept)), out_specs=[vmem]...  5.85 us
    all_to_all x1, starting transfers between devices, local(): lax.all_to_all(copies, TRACER, split_axis=0, concat_axis=0, tiled=True)  3.48 us
    pallas_call x1, Pallas kernels, local(): pl.pallas_call(lend_kernel, in_specs=[smem, hbm], out_specs=vmem, out_sha...  2.66 us
  transfers between devices with their start and end apart: 2, of which 1 were waited for; matrix products, arithmetic and copies ran while one was open for 0% of the time, Pallas kernels for 4%

profile of v7, /device:TPU:1, one launch (start us, length us, event | category | flops | bytes accessed | tf_op | source)
XLA Modules:
  0.0 96.9 jit_solution(5302124013386749873)
XLA Ops:
  0.0 0.0 copy-start.3
  0.0 0.0 copy-start.1
  0.0 0.0 copy-start
  0.0 0.0 copy-start.2
  0.7 0.7 pad_add_fusion.facts
  1.4 2.7 %lend.1 = f32[512,512]{1,0:T(8,128)} custom-call(s32[7]{0:T(128)S(1)} %pad_add_fusion.facts, bf16[1,5,512,512]{3,2,1,0:T(8,128)(2,1)} %tiles.3), custom_call_target="tpu_custom_call" | custom-call | tf_op jit(solution)/shard_map/lend/pallas_call | solution.py:223
  4.1 8.7 %collective-permute-start = (f32[512,512]{1,0:T(8,128)}, f32[512,512]{1,0:T(8,128)}, u32[]{:S(2)}, u32[]{:S(2)}) collective-permute-start(f32[512,512]{1,0:T(8,128)} %lend.1), channel_id=1, source_target_pairs={{0,8},{8,0},{1,9},{9,1},{2,10},{10,2},{3,11},{11,3},{4,12},{12,4},... | collective-permute-start | bytes 3145736 | tf_op jit(solution)/shard_map/ppermute | solution.py:232
  12.9 1.6 %pack.1 = f32[8,7,4,512]{3,2,1,0:T(4,128)} custom-call(f32[4,512]{1,0:T(4,128)} %cotangent.1, f32[6,4,512]{2,1,0:T(4,128)} %states.1), custom_call_target="tpu_custom_call" | custom-call | tf_op jit(solution)/shard_map/pack/pallas_call | solution.py:212
  14.5 3.5 %all-to-all-start = ((f32[8,7,4,512]{3,2,1,0:T(4,128)}), f32[8,7,4,512]{3,2,1,0:T(4,128)S(1)}, u32[]{:S(2)}, u32[]{:S(2)}) async-start(f32[8,7,4,512]{3,2,1,0:T(4,128)} %pack.1), calls=%async_computation | async-start | bytes 917504 | tf_op jit(solution)/shard_map/all_to_all | solution.py:221
  18.0 0.0 copy-done.3
  18.0 0.1 copy.13
  18.1 0.0 copy-done.1
  18.1 0.1 copy.12
  18.2 0.0 copy-done
  18.2 0.0 copy-done.2
  18.2 2.3 %arrange.1 = (bf16[4,512,512]{2,1,0:T(8,128)(2,1)S(1)}, f32[40,512]{1,0:T(8,128)S(1)}, f32[8,512]{1,0:T(8,128)S(1)}) custom-call(s32[7]{0:T(128)S(1)} %pad_add_fusion.facts, s32[16]{0:T(128)S(1)} %copy-done.2, bf16[1,5,512,512]{3,2,1,0:T(8,128)(2,1)} %tiles.3, f32[16,32,32]{2,1,0:T(8,128)S(1)} %copy-done), custom_call_target="tpu_custom_call" | custom-call | tf_op jit(solution)/shard_map/arrange/pallas_call | solution.py:233
  20.4 6.3 %all-to-all-done.gathered = f32[8,7,4,512]{3,2,1,0:T(4,128)S(1)} async-done(((f32[8,7,4,512]{3,2,1,0:T(4,128)}), f32[8,7,4,512]{3,2,1,0:T(4,128)S(1)}, u32[]{:S(2)}, u32[]{:S(2)}) %all-to-all-start) | async-done | bytes 458784 | tf_op jit(solution)/shard_map/all_to_all | solution.py:221
  26.8 0.3 gathered.1
  27.1 2.5 %all-gather = f32[144,512]{1,0:T(8,128)S(1)} all-gather(f32[72,512]{1,0:T(8,128)S(1)} %get-tuple-element.25), channel_id=2, replica_groups=mesh['z'=16,'yhi'=2,'core'=2,'x'=4,'ylo'=2] {'core'}, dimensions={0}, use_global_device_ids=true | all-gather | bytes 442368 | tf_op jit(solution)/shard_map/all_gather | solution.py:262
  29.6 0.0 collective-permute-done.borrowed
  29.6 1.3 %round.1.refs_2_ = bf16[512,512]{1,0:T(8,128)(2,1)S(1)} custom-call(f32[512,512]{1,0:T(8,128)} %collective-permute-done.borrowed), custom_call_target="tpu_custom_call" | custom-call | tf_op jit(solution)/shard_map/round/pallas_call | solution.py:246
  30.9 1.0 %shard_map.91 = (f32[64,512]{1,0:T(8,128)S(1)}, f32[64,512]{1,0:T(8,128)S(1)}, bf16[2,4,256,256]{3,2,1,0:T(8,128)(2,1)S(1)}, f32[2,512]{1,0:T(2,128)S(1)}) custom-call(f32[2,72,512]{2,1,0:T(8,128)S(1)} %bitcast.34, bf16[4,512,512]{2,1,0:T(8,128)(2,1)S(1)} %get-tuple-element.26.refs_1_, bf16[512,512]{1,0:T(8,128)(2,1)S(1)} %round.1.refs_2_, ...), custom_call_target="tpu_custom_call" | custom-call | tf_op jit(solution)/shard_map/pallas_call | solution.py:273
  31.9 2.0 %all-gather.1 = f32[128,512]{1,0:T(8,128)S(1)} all-gather(f32[64,512]{1,0:T(8,128)S(1)} %get-tuple-element.31), channel_id=3, replica_groups={{9,16},{8,0},{11,18},{10,2},{13,20},{12,4},{15,22},{14,6},{24,33},{25,1..., dimensions={0}, use_global_device_ids=true | all-gather | bytes 393216 | tf_op jit(solution)/shard_map/all_gather | solution.py:289
  33.9 2.0 %all-gather.2 = f32[128,512]{1,0:T(8,128)S(1)} all-gather(f32[64,512]{1,0:T(8,128)S(1)} %bitcast_add_fusion.4), channel_id=4, replica_groups=mesh['z'=16,'yhi'=2,'core'=2,'x'=4,'ylo'=2] {'core'}, dimensions={0}, use_global_device_ids=true | all-gather | bytes 393216 | tf_op jit(solution)/shard_map/all_gather | solution.py:291
  35.9 1.0 %shard_map.92 = (f32[64,512]{1,0:T(8,128)S(1)}, f32[64,512]{1,0:T(8,128)S(1)}) custom-call(f32[2,64,512]{2,1,0:T(8,128)S(1)} %bitcast.36, bf16[4,512,512]{2,1,0:T(8,128)(2,1)S(1)} %get-tuple-element.26.refs_1_, bf16[512,512]{1,0:T(8,128)(2,1)S(1)} %round.1.refs_2_, f32[8,512]{1,0:T(8,128)S(1)} %get-tuple-element.27.refs_3_, ...), custom_call_target="tpu_custom_call" | custom-call | tf_op jit(solution)/shard_map/pallas_call | solution.py:273
  36.9 2.0 %all-gather.3 = f32[128,512]{1,0:T(8,128)S(1)} all-gather(f32[64,512]{1,0:T(8,128)S(1)} %get-tuple-element.34), channel_id=5, replica_groups={{9,16},{8,0},{11,18},{10,2},{13,20},{12,4},{15,22},{14,6},{24,33},{25,1..., dimensions={0}, use_global_device_ids=true | all-gather | bytes 393216 | tf_op jit(solution)/shard_map/all_gather | solution.py:289
  38.9 2.0 %all-gather.4 = f32[128,512]{1,0:T(8,128)S(1)} all-gather(f32[64,512]{1,0:T(8,128)S(1)} %bitcast_add_fusion.3), channel_id=6, replica_groups=mesh['z'=16,'yhi'=2,'core'=2,'x'=4,'ylo'=2] {'core'}, dimensions={0}, use_global_device_ids=true | all-gather | bytes 393216 | tf_op jit(solution)/shard_map/all_gather | solution.py:291
  40.9 1.0 %shard_map.93 = (f32[64,512]{1,0:T(8,128)S(1)}, f32[64,512]{1,0:T(8,128)S(1)}) custom-call(f32[2,64,512]{2,1,0:T(8,128)S(1)} %bitcast.37, bf16[4,512,512]{2,1,0:T(8,128)(2,1)S(1)} %get-tuple-element.26.refs_1_, bf16[512,512]{1,0:T(8,128)(2,1)S(1)} %round.1.refs_2_, f32[8,512]{1,0:T(8,128)S(1)} %get-tuple-element.27.refs_3_, ...), custom_call_target="tpu_custom_call" | custom-call | tf_op jit(solution)/shard_map/pallas_call | solution.py:273
  41.9 2.0 %all-gather.5 = f32[128,512]{1,0:T(8,128)S(1)} all-gather(f32[64,512]{1,0:T(8,128)S(1)} %get-tuple-element.36), channel_id=7, replica_groups={{9,16},{8,0},{11,18},{10,2},{13,20},{12,4},{15,22},{14,6},{24,33},{25,1..., dimensions={0}, use_global_device_ids=true | all-gather | bytes 393216 | tf_op jit(solution)/shard_map/all_gather | solution.py:289
  43.9 2.0 %all-gather.6 = f32[128,512]{1,0:T(8,128)S(1)} all-gather(f32[64,512]{1,0:T(8,128)S(1)} %bitcast_add_fusion.2), channel_id=8, replica_groups=mesh['z'=16,'yhi'=2,'core'=2,'x'=4,'ylo'=2] {'core'}, dimensions={0}, use_global_device_ids=true | all-gather | bytes 393216 | tf_op jit(solution)/shard_map/all_gather | solution.py:291
  45.9 1.0 %shard_map.94 = (f32[64,512]{1,0:T(8,128)S(1)}, f32[64,512]{1,0:T(8,128)S(1)}) custom-call(f32[2,64,512]{2,1,0:T(8,128)S(1)} %bitcast.38, bf16[4,512,512]{2,1,0:T(8,128)(2,1)S(1)} %get-tuple-element.26.refs_1_, bf16[512,512]{1,0:T(8,128)(2,1)S(1)} %round.1.refs_2_, f32[8,512]{1,0:T(8,128)S(1)} %get-tuple-element.27.refs_3_, ...), custom_call_target="tpu_custom_call" | custom-call | tf_op jit(solution)/shard_map/pallas_call | solution.py:273
  46.8 2.0 %all-gather.7 = f32[128,512]{1,0:T(8,128)S(1)} all-gather(f32[64,512]{1,0:T(8,128)S(1)} %get-tuple-element.38), channel_id=9, replica_groups={{9,16},{8,0},{11,18},{10,2},{13,20},{12,4},{15,22},{14,6},{24,33},{25,1..., dimensions={0}, use_global_device_ids=true | all-gather | bytes 393216 | tf_op jit(solution)/shard_map/all_gather | solution.py:289
  48.9 2.0 %all-gather.8 = f32[128,512]{1,0:T(8,128)S(1)} all-gather(f32[64,512]{1,0:T(8,128)S(1)} %bitcast_add_fusion.1), channel_id=10, replica_groups=mesh['z'=16,'yhi'=2,'core'=2,'x'=4,'ylo'=2] {'core'}, dimensions={0}, use_global_device_ids=true | all-gather | bytes 393216 | tf_op jit(solution)/shard_map/all_gather | solution.py:291
  50.9 1.0 %shard_map.95 = (f32[64,512]{1,0:T(8,128)S(1)}, f32[64,512]{1,0:T(8,128)S(1)}) custom-call(f32[2,64,512]{2,1,0:T(8,128)S(1)} %bitcast.39, bf16[4,512,512]{2,1,0:T(8,128)(2,1)S(1)} %get-tuple-element.26.refs_1_, bf16[512,512]{1,0:T(8,128)(2,1)S(1)} %round.1.refs_2_, f32[8,512]{1,0:T(8,128)S(1)} %get-tuple-element.27.refs_3_, ...), custom_call_target="tpu_custom_call" | custom-call | tf_op jit(solution)/shard_map/pallas_call | solution.py:273
  51.8 2.0 %all-gather.9 = f32[128,512]{1,0:T(8,128)S(1)} all-gather(f32[64,512]{1,0:T(8,128)S(1)} %get-tuple-element.40), channel_id=11, replica_groups={{9,16},{8,0},{11,18},{10,2},{13,20},{12,4},{15,22},{14,6},{24,33},{25,1..., dimensions={0}, use_global_device_ids=true | all-gather | bytes 393216 | tf_op jit(solution)/shard_map/all_gather | solution.py:289
  53.8 2.0 %all-gather.10 = f32[128,512]{1,0:T(8,128)S(1)} all-gather(f32[64,512]{1,0:T(8,128)S(1)} %bitcast_add_fusion), channel_id=12, replica_groups=mesh['z'=16,'yhi'=2,'core'=2,'x'=4,'ylo'=2] {'core'}, dimensions={0}, use_global_device_ids=true | all-gather | bytes 393216 | tf_op jit(solution)/shard_map/all_gather | solution.py:291
  55.8 1.0 %shard_map.96 = (f32[64,512]{1,0:T(8,128)S(1)}, f32[64,512]{1,0:T(8,128)S(1)}) custom-call(f32[2,64,512]{2,1,0:T(8,128)S(1)} %bitcast.35, bf16[4,512,512]{2,1,0:T(8,128)(2,1)S(1)} %get-tuple-element.26.refs_1_, bf16[512,512]{1,0:T(8,128)(2,1)S(1)} %round.1.refs_2_, f32[8,512]{1,0:T(8,128)S(1)} %get-tuple-element.27.refs_3_, ...), custom_call_target="tpu_custom_call" | custom-call | tf_op jit(solution)/shard_map/pallas_call | solution.py:273
  56.8 1.9 %all_gather.99 = f32[2,16,512]{2,1,0:T(8,128)S(1)} all-gather(f32[1,16,512]{2,1,0:T(8,128)S(1)} %dynamic-slice_bitcast_fusion), channel_id=1, replica_groups={{9,16},{8,0},{11,18},{10,2},{13,20},{12,4},{15,22},{14,6},{24,33},{25,1..., dimensions={0}, use_global_device_ids=true | all-gather | bytes 98304 | tf_op jit(solution)/shard_map/all_gather | solution.py:289
  58.7 1.8 %all_gather.100 = f32[2,16,512]{2,1,0:T(8,128)S(1)} all-gather(f32[1,16,512]{2,1,0:T(8,128)S(1)} %bitcast_add_fusion.5), channel_id=1, replica_groups=mesh['z'=16,'yhi'=2,'core'=2,'x'=4,'ylo'=2] {'core'}, dimensions={0}, use_global_device_ids=true | all-gather | bytes 98304 | tf_op jit(solution)/shard_map/all_gather | solution.py:291
  60.6 35.7 %all_gather.101 = f32[2,4,512]{2,1,0:T(4,128)S(1)} all-gather(f32[1,4,512]{2,1,0:T(4,128)S(1)} %constant_dynamic-slice_fusion), channel_id=1, replica_groups=mesh['z'=16,'yhi'=2,'core'=2,'x'=4,'ylo'=2] {'ylo'}, dimensions={0}, use_global_device_ids=true | all-gather | bytes 24576 | tf_op jit(solution)/shard_map/all_gather | solution.py:297
  96.3 0.6 select_bitcast_fusion
  (12 shorter events, 0.1 us)
Async XLA Ops:
  0.0 18.0 %copy-start.3 = (f32[32,32]{1,0:T(8,128)S(1)}, f32[32,32]{1,0:T(8,128)}, u32[]{:S(2)}) copy-start(f32[32,32]{1,0:T(8,128)} %param.17) | copy-start | bytes 12292
  0.0 18.1 %copy-start.1 = (f32[32,32]{1,0:T(8,128)S(1)}, f32[32,32]{1,0:T(8,128)}, u32[]{:S(2)}) copy-start(f32[32,32]{1,0:T(8,128)} %uptake_weight.1) | copy-start | bytes 12292
  0.0 18.2 %copy-start = (f32[16,32,32]{2,1,0:T(8,128)S(1)}, f32[16,32,32]{2,1,0:T(8,128)}, u32[]{:S(2)}) copy-start(f32[16,32,32]{2,1,0:T(8,128)} %inverse.1) | copy-start | bytes 196612
  0.0 18.2 %copy-start.2 = (s32[16]{0:T(128)S(1)}, s32[16]{0:T(128)}, u32[]{:S(2)}) copy-start(s32[16]{0:T(128)} %wet.1) | copy-start | bytes 196
  4.1 25.5 %collective-permute-start = (f32[512,512]{1,0:T(8,128)}, f32[512,512]{1,0:T(8,128)}, u32[]{:S(2)}, u32[]{:S(2)}) collective-permute-start(f32[512,512]{1,0:T(8,128)} %lend.1), channel_id=1, source_target_pairs={{0,8},{8,0},{1,9},{9,1},{2,10},{10,2},{3,11},{11,3},{4,12},{12,4},... | collective-permute-start | bytes 3145736 | tf_op jit(solution)/shard_map/ppermute | solution.py:232
  14.5 12.3 %all-to-all-start = ((f32[8,7,4,512]{3,2,1,0:T(4,128)}), f32[8,7,4,512]{3,2,1,0:T(4,128)S(1)}, u32[]{:S(2)}, u32[]{:S(2)}) async-start(f32[8,7,4,512]{3,2,1,0:T(4,128)} %pack.1), calls=%async_computation | async-start | bytes 917504 | tf_op jit(solution)/shard_map/all_to_all | solution.py:221

commit v8 on v7

--- a/solution.py
+++ b/solution.py
@@ -59,36 +59,22 @@
     return live > 0
 
 
-def pack_kernel(cotangent, states, copies, buffer, fetched):
-    first = pltpu.make_async_copy(cotangent, buffer.at[0], fetched.at[0])
-    rest = pltpu.make_async_copy(states, buffer.at[pl.ds(1, states.shape[0])], fetched.at[1])
-    first.start()
-    rest.start()
-    first.wait()
-    rest.wait()
+def open_kernel(cotangent, states, inverse_hbm, wet_hbm, copies, shared, buffer, inverse, wet, arrival):
+    pairs = [
+        (cotangent, buffer.at[0]),
+        (states, buffer.at[pl.ds(1, states.shape[0])]),
+        (wet_hbm, wet),
+        (inverse_hbm, inverse),
+    ]
+    fetches = [pltpu.make_async_copy(source, target, arrival.at[n]) for n, (source, target) in enumerate(pairs)]
+    for fetch in fetches:
+        fetch.start()
+    for fetch in fetches[:2]:
+        fetch.wait()
     for t in range(copies.shape[0]):
         copies[t] = buffer[...]
-
-
-def lend_kernel(facts, tiles, lent, buffer, arrival):
-    slots = tiles.shape[1]
-    distance = 2 - 4 * facts[CORE_AT]
-    fetch = pltpu.make_async_copy(tiles.at[0, slot_at(facts, slots, distance)], buffer, arrival)
-    fetch.start()
-    fetch.wait()
-    lent[...] = jnp.where(slot_live(facts, slots, distance), buffer[...].astype(jnp.float32), 0.0)
-
-
-def arrange_kernel(facts, wet, tiles, inverse, ordered, shared, upper, arrival):
-    slots = tiles.shape[1]
-    direction = 2 * facts[CORE_AT] - 1
-    uses = (direction, 2 * direction, 0, -direction)
-    fetches = [
-        pltpu.make_async_copy(tiles.at[0, slot_at(facts, slots, distance)], ordered.at[n], arrival.at[n])
-        for n, distance in enumerate(uses)
-    ]
-    for fetch in fetches:
-        fetch.start()
+    for fetch in fetches[2:]:
+        fetch.wait()
     columns, levels, _ = inverse.shape
     lane = lax.broadcasted_iota(jnp.int32, (levels, levels), 1)
     row = lax.broadcasted_iota(jnp.int32, (8, levels), 1)
@@ -96,10 +82,26 @@
         at = slice(c * levels, (c + 1) * levels)
         shared[0:levels, at] = jnp.where(lane < wet[c], inverse[c], 0.0)
         shared[levels : levels + 8, at] = jnp.where(row < wet[c], 1.0, 0.0)
-    upper[...] = jnp.full(upper.shape, facts[CORE_AT], jnp.int32).astype(jnp.float32)
+
+
+def lend_kernel(facts, tiles, lent, ordered, upper, buffer, arrival):
+    slots = tiles.shape[1]
+    core = facts[CORE_AT]
+    direction = 2 * core - 1
+    uses = (-2 * direction, direction, 2 * direction, 0, -direction)
+    fetches = [
+        pltpu.make_async_copy(
+            tiles.at[0, slot_at(facts, slots, distance)], ordered.at[n - 1] if n else buffer, arrival.at[n]
+        )
+        for n, distance in enumerate(uses)
+    ]
     for fetch in fetches:
-        fetch.wait()
-    for n, distance in enumerate(uses):
+        fetch.start()
+    upper[...] = jnp.full(upper.shape, core, jnp.int32).astype(jnp.float32)
+    fetches[0].wait()
+    lent[...] = jnp.where(slot_live(facts, slots, uses[0]), buffer[...].astype(jnp.float32), 0.0)
+    for n, distance in enumerate(uses[1:]):
+        fetches[n + 1].wait()
 
         @pl.when(jnp.logical_not(slot_live(facts, slots, distance)))
         def _():
@@ -209,40 +211,35 @@
     def in_hbm(array):
         return pltpu.with_memory_space_constraint(array, pltpu.HBM)
 
-    copies = pl.pallas_call(
-        pack_kernel,
-        in_specs=[hbm] * 2,
-        out_specs=vmem,
-        out_shape=shape((peers, 1 + sections, tracers_here, boxes), f32),
-        scratch_shapes=[pltpu.VMEM((1 + sections, tracers_here, boxes), f32), dma((2,))],
+    copies, shared = pl.pallas_call(
+        open_kernel,
+        in_specs=[hbm] * 4,
+        out_specs=[vmem] * 2,
+        out_shape=[
+            shape((peers, 1 + sections, tracers_here, boxes), f32),
+            shape((levels + 8, boxes), f32),
+        ],
+        scratch_shapes=[
+            pltpu.VMEM((1 + sections, tracers_here, boxes), f32),
+            pltpu.VMEM(implicit_inverse.shape, f32),
+            pltpu.SMEM(wet_levels.shape, jnp.int32),
+            dma((4,)),
+        ],
         compiler_params=lean,
-        name="pack",
-    )(in_hbm(cotangent), in_hbm(states))
+        name="open",
+    )(*map(in_hbm, (cotangent, states, implicit_inverse, wet_levels)))
     gathered = lax.all_to_all(copies, TRACER, split_axis=0, concat_axis=0, tiled=True)
     facts = jnp.concatenate([tile_offset.reshape(-1), tile_count, core])
-    lent = pl.pallas_call(
+    lent, ordered, upper = pl.pallas_call(
         lend_kernel,
         in_specs=[smem, hbm],
-        out_specs=vmem,
-        out_shape=shape((boxes, boxes), f32),
-        scratch_shapes=[pltpu.VMEM((boxes, boxes), bf16), dma],
+        out_specs=[vmem] * 3,
+        out_shape=[shape((boxes, boxes), f32), shape((4, boxes, boxes), bf16), shape((8, boxes), f32)],
+        scratch_shapes=[pltpu.VMEM((boxes, boxes), bf16), dma((5,))],
         compiler_params=lean,
         name="lend",
     )(facts, in_hbm(explicit_tiles))
     borrowed = lax.ppermute(lent, "core", [(0, 1), (1, 0)])
-    ordered, shared, upper = pl.pallas_call(
-        arrange_kernel,
-        in_specs=[smem] * 2 + [hbm, vmem],
-        out_specs=[vmem] * 3,
-        out_shape=[
-            shape((4, boxes, boxes), bf16),
-            shape((levels + 8, boxes), f32),
-            shape((8, boxes), f32),
-        ],
-        scratch_shapes=[dma((4,))],
-        compiler_params=lean,
-        name="arrange",
-    )(facts, wet_levels, in_hbm(explicit_tiles), implicit_inverse)
     borrowed = pl.pallas_call(
         round_kernel,
         in_specs=[vmem],

time: 97.6 us -> 98.3 us (level)
  waiting for transfers between devices: 6.33 us -> 8.62 us
  Pallas kernels: 14 us -> 12.6 us
    all_to_all x1, waiting for transfers between devices: 6.32 us -> 8.61 us  [local(): lax.all_to_all(copies, TRACER, split_axis=0, concat_axis=0, tiled=True)]
    pallas_call x3 -> x2, Pallas kernels: 6.56 us -> 5.09 us  [the longest x1 3.24 us: local(): pl.pallas_call(lend_kernel, in_specs=[smem, hbm], out_specs=[vmem] * 3, o...]
  transfers between devices with their start and end apart: 2 -> 2, of which waited for: 1 -> 1; matrix products, arithmetic and copies ran while one was open for 0% -> 0% of each run, Pallas kernels for 4% -> 2%
where the time goes in v8:
time: 98.3 us; the launch traced here: 97.6 us
  blocking collectives  61.8 us (63%)
  Pallas kernels  12.6 us (13%)
  starting transfers between devices  12.3 us (13%)
  waiting for transfers between devices  8.62 us (9%)
  other arithmetic  1.44 us (1%)
    all_gather x1, blocking collectives, local(): lax.all_gather(passed, 'ylo')  35.6 us
    all_gather x6, blocking collectives, local(): arrived = lax.all_gather(send, EVERY, axis_index_groups=groups)  11.8 us
    all_gather x6, blocking collectives, local(): adjoint = lax.all_gather(keep, 'core')  11.8 us
    ppermute x1, starting transfers between devices, local(): borrowed = lax.ppermute(lent, 'core', [(0, 1), (1, 0)])  8.78 us
    all_to_all x1, waiting for transfers between devices, local(): lax.all_to_all(copies, TRACER, split_axis=0, concat_axis=0, tiled=True)  8.61 us
    pallas_call x6, Pallas kernels, local(): pl.pallas_call(step, in_specs=[vmem] * (7 + len(kept)), out_specs=[vmem]...  5.85 us
    all_to_all x1, starting transfers between devices, local(): lax.all_to_all(copies, TRACER, split_axis=0, concat_axis=0, tiled=True)  3.48 us
    pallas_call x1, Pallas kernels, local(): pl.pallas_call(lend_kernel, in_specs=[smem, hbm], out_specs=[vmem] * 3, o...  3.24 us
  transfers between devices with their start and end apart: 2, of which 1 were waited for; matrix products, arithmetic and copies ran while one was open for 0% of the time, Pallas kernels for 2%

profile of v8, /device:TPU:1, one launch (start us, length us, event | category | flops | bytes accessed | tf_op | source)
XLA Modules:
  0.0 97.6 jit_solution(11379931395544445441)
XLA Ops:
  0.0 0.0 copy-start
  0.0 0.0 copy-start.1
  0.7 0.7 pad_add_fusion.facts
  1.4 3.2 %lend.1 = (f32[512,512]{1,0:T(8,128)}, bf16[4,512,512]{2,1,0:T(8,128)(2,1)S(1)}, f32[8,512]{1,0:T(8,128)S(1)}) custom-call(s32[7]{0:T(128)S(1)} %pad_add_fusion.facts, bf16[1,5,512,512]{3,2,1,0:T(8,128)(2,1)} %tiles.1), custom_call_target="tpu_custom_call" | custom-call | tf_op jit(solution)/shard_map/lend/pallas_call | solution.py:233
  4.7 8.8 %collective-permute-start = (f32[512,512]{1,0:T(8,128)}, f32[512,512]{1,0:T(8,128)}, u32[]{:S(2)}, u32[]{:S(2)}) collective-permute-start(f32[512,512]{1,0:T(8,128)} %get-tuple-element.30), channel_id=1, source_target_pairs={{0,8},{8,0},{1,9},{9,1},{2,10},{10,2},{3,11},{11,3},{4,12},{12,4},... | collective-permute-start | bytes 3145736 | tf_op jit(solution)/shard_map/ppermute | solution.py:242
  13.4 1.9 %open.1 = (f32[8,7,4,512]{3,2,1,0:T(4,128)}, f32[40,512]{1,0:T(8,128)S(1)}) custom-call(f32[4,512]{1,0:T(4,128)} %cotangent.1, f32[6,4,512]{2,1,0:T(4,128)} %states.1, f32[16,32,32]{2,1,0:T(8,128)} %inverse_hbm.1, s32[16]{0:T(128)} %wet_hbm.1), custom_call_target="tpu_custom_call" | custom-call | tf_op jit(solution)/shard_map/open/pallas_call | solution.py:214
  15.3 3.5 %all-to-all-start = ((f32[8,7,4,512]{3,2,1,0:T(4,128)}), f32[8,7,4,512]{3,2,1,0:T(4,128)S(1)}, u32[]{:S(2)}, u32[]{:S(2)}) async-start(f32[8,7,4,512]{3,2,1,0:T(4,128)} %get-tuple-element.26), calls=%async_computation | async-start | bytes 917504 | tf_op jit(solution)/shard_map/all_to_all | solution.py:231
  18.8 0.0 copy-done
  18.8 0.1 copy.12
  18.9 0.0 copy-done.1
  18.9 0.1 copy.13
  19.0 8.6 %all-to-all-done.gathered = f32[8,7,4,512]{3,2,1,0:T(4,128)S(1)} async-done(((f32[8,7,4,512]{3,2,1,0:T(4,128)}), f32[8,7,4,512]{3,2,1,0:T(4,128)S(1)}, u32[]{:S(2)}, u32[]{:S(2)}) %all-to-all-start) | async-done | bytes 458784 | tf_op jit(solution)/shard_map/all_to_all | solution.py:231
  27.6 0.3 gathered.1
  27.9 2.5 %all-gather = f32[144,512]{1,0:T(8,128)S(1)} all-gather(f32[72,512]{1,0:T(8,128)S(1)} %get-tuple-element.28), channel_id=2, replica_groups=mesh['z'=16,'yhi'=2,'core'=2,'x'=4,'ylo'=2] {'core'}, dimensions={0}, use_global_device_ids=true | all-gather | bytes 442368 | tf_op jit(solution)/shard_map/all_gather | solution.py:259
  30.4 0.0 collective-permute-done.borrowed
  30.4 1.3 %round.1.refs_2_ = bf16[512,512]{1,0:T(8,128)(2,1)S(1)} custom-call(f32[512,512]{1,0:T(8,128)} %collective-permute-done.borrowed), custom_call_target="tpu_custom_call" | custom-call | tf_op jit(solution)/shard_map/round/pallas_call | solution.py:243
  31.7 1.0 %shard_map.91 = (f32[64,512]{1,0:T(8,128)S(1)}, f32[64,512]{1,0:T(8,128)S(1)}, bf16[2,4,256,256]{3,2,1,0:T(8,128)(2,1)S(1)}, f32[2,512]{1,0:T(2,128)S(1)}) custom-call(f32[2,72,512]{2,1,0:T(8,128)S(1)} %bitcast.34, bf16[4,512,512]{2,1,0:T(8,128)(2,1)S(1)} %get-tuple-element.29.refs_1_, bf16[512,512]{1,0:T(8,128)(2,1)S(1)} %round.1.refs_2_, ...), custom_call_target="tpu_custom_call" | custom-call | tf_op jit(solution)/shard_map/pallas_call | solution.py:270
  32.7 2.0 %all-gather.1 = f32[128,512]{1,0:T(8,128)S(1)} all-gather(f32[64,512]{1,0:T(8,128)S(1)} %get-tuple-element.35), channel_id=3, replica_groups={{9,16},{8,0},{11,18},{10,2},{13,20},{12,4},{15,22},{14,6},{24,33},{25,1..., dimensions={0}, use_global_device_ids=true | all-gather | bytes 393216 | tf_op jit(solution)/shard_map/all_gather | solution.py:286
  34.7 2.0 %all-gather.2 = f32[128,512]{1,0:T(8,128)S(1)} all-gather(f32[64,512]{1,0:T(8,128)S(1)} %bitcast_add_fusion.4), channel_id=4, replica_groups=mesh['z'=16,'yhi'=2,'core'=2,'x'=4,'ylo'=2] {'core'}, dimensions={0}, use_global_device_ids=true | all-gather | bytes 393216 | tf_op jit(solution)/shard_map/all_gather | solution.py:288
  36.7 1.0 shard_map.92
  37.7 2.0 %all-gather.3 = f32[128,512]{1,0:T(8,128)S(1)} all-gather(f32[64,512]{1,0:T(8,128)S(1)} %get-tuple-element.38), channel_id=5, replica_groups={{9,16},{8,0},{11,18},{10,2},{13,20},{12,4},{15,22},{14,6},{24,33},{25,1..., dimensions={0}, use_global_device_ids=true | all-gather | bytes 393216 | tf_op jit(solution)/shard_map/all_gather | solution.py:286
  39.7 2.0 %all-gather.4 = f32[128,512]{1,0:T(8,128)S(1)} all-gather(f32[64,512]{1,0:T(8,128)S(1)} %bitcast_add_fusion.3), channel_id=6, replica_groups=mesh['z'=16,'yhi'=2,'core'=2,'x'=4,'ylo'=2] {'core'}, dimensions={0}, use_global_device_ids=true | all-gather | bytes 393216 | tf_op jit(solution)/shard_map/all_gather | solution.py:288
  41.7 1.0 shard_map.93
  42.7 2.0 %all-gather.5 = f32[128,512]{1,0:T(8,128)S(1)} all-gather(f32[64,512]{1,0:T(8,128)S(1)} %get-tuple-element.40), channel_id=7, replica_groups={{9,16},{8,0},{11,18},{10,2},{13,20},{12,4},{15,22},{14,6},{24,33},{25,1..., dimensions={0}, use_global_device_ids=true | all-gather | bytes 393216 | tf_op jit(solution)/shard_map/all_gather | solution.py:286
  44.7 2.0 %all-gather.6 = f32[128,512]{1,0:T(8,128)S(1)} all-gather(f32[64,512]{1,0:T(8,128)S(1)} %bitcast_add_fusion.2), channel_id=8, replica_groups=mesh['z'=16,'yhi'=2,'core'=2,'x'=4,'ylo'=2] {'core'}, dimensions={0}, use_global_device_ids=true | all-gather | bytes 393216 | tf_op jit(solution)/shard_map/all_gather | solution.py:288
  46.7 1.0 shard_map.94
  47.6 2.0 %all-gather.7 = f32[128,512]{1,0:T(8,128)S(1)} all-gather(f32[64,512]{1,0:T(8,128)S(1)} %get-tuple-element.42), channel_id=9, replica_groups={{9,16},{8,0},{11,18},{10,2},{13,20},{12,4},{15,22},{14,6},{24,33},{25,1..., dimensions={0}, use_global_device_ids=true | all-gather | bytes 393216 | tf_op jit(solution)/shard_map/all_gather | solution.py:286
  49.7 2.0 %all-gather.8 = f32[128,512]{1,0:T(8,128)S(1)} all-gather(f32[64,512]{1,0:T(8,128)S(1)} %bitcast_add_fusion.1), channel_id=10, replica_groups=mesh['z'=16,'yhi'=2,'core'=2,'x'=4,'ylo'=2] {'core'}, dimensions={0}, use_global_device_ids=true | all-gather | bytes 393216 | tf_op jit(solution)/shard_map/all_gather | solution.py:288
  51.7 1.0 shard_map.95
  52.6 2.0 %all-gather.9 = f32[128,512]{1,0:T(8,128)S(1)} all-gather(f32[64,512]{1,0:T(8,128)S(1)} %get-tuple-element.44), channel_id=11, replica_groups={{9,16},{8,0},{11,18},{10,2},{13,20},{12,4},{15,22},{14,6},{24,33},{25,1..., dimensions={0}, use_global_device_ids=true | all-gather | bytes 393216 | tf_op jit(solution)/shard_map/all_gather | solution.py:286
  54.6 2.0 %all-gather.10 = f32[128,512]{1,0:T(8,128)S(1)} all-gather(f32[64,512]{1,0:T(8,128)S(1)} %bitcast_add_fusion), channel_id=12, replica_groups=mesh['z'=16,'yhi'=2,'core'=2,'x'=4,'ylo'=2] {'core'}, dimensions={0}, use_global_device_ids=true | all-gather | bytes 393216 | tf_op jit(solution)/shard_map/all_gather | solution.py:288
  56.6 1.0 shard_map.96
  57.6 1.9 %all_gather.99 = f32[2,16,512]{2,1,0:T(8,128)S(1)} all-gather(f32[1,16,512]{2,1,0:T(8,128)S(1)} %dynamic-slice_bitcast_fusion), channel_id=1, replica_groups={{9,16},{8,0},{11,18},{10,2},{13,20},{12,4},{15,22},{14,6},{24,33},{25,1..., dimensions={0}, use_global_device_ids=true | all-gather | bytes 98304 | tf_op jit(solution)/shard_map/all_gather | solution.py:286
  59.5 1.8 %all_gather.100 = f32[2,16,512]{2,1,0:T(8,128)S(1)} all-gather(f32[1,16,512]{2,1,0:T(8,128)S(1)} %bitcast_add_fusion.5), channel_id=1, replica_groups=mesh['z'=16,'yhi'=2,'core'=2,'x'=4,'ylo'=2] {'core'}, dimensions={0}, use_global_device_ids=true | all-gather | bytes 98304 | tf_op jit(solution)/shard_map/all_gather | solution.py:288
  61.4 35.6 %all_gather.101 = f32[2,4,512]{2,1,0:T(4,128)S(1)} all-gather(f32[1,4,512]{2,1,0:T(4,128)S(1)} %constant_dynamic-slice_fusion), channel_id=1, replica_groups=mesh['z'=16,'yhi'=2,'core'=2,'x'=4,'ylo'=2] {'ylo'}, dimensions={0}, use_global_device_ids=true | all-gather | bytes 24576 | tf_op jit(solution)/shard_map/all_gather | solution.py:294
  97.0 0.6 select_bitcast_fusion
  (12 shorter events, 0.1 us)
Async XLA Ops:
  0.0 18.8 %copy-start = (f32[32,32]{1,0:T(8,128)S(1)}, f32[32,32]{1,0:T(8,128)}, u32[]{:S(2)}) copy-start(f32[32,32]{1,0:T(8,128)} %uptake_weight.1) | copy-start | bytes 12292
  0.0 18.9 %copy-start.1 = (f32[32,32]{1,0:T(8,128)S(1)}, f32[32,32]{1,0:T(8,128)}, u32[]{:S(2)}) copy-start(f32[32,32]{1,0:T(8,128)} %param.17) | copy-start | bytes 12292
  4.7 25.8 %collective-permute-start = (f32[512,512]{1,0:T(8,128)}, f32[512,512]{1,0:T(8,128)}, u32[]{:S(2)}, u32[]{:S(2)}) collective-permute-start(f32[512,512]{1,0:T(8,128)} %get-tuple-element.30), channel_id=1, source_target_pairs={{0,8},{8,0},{1,9},{9,1},{2,10},{10,2},{3,11},{11,3},{4,12},{12,4},... | collective-permute-start | bytes 3145736 | tf_op jit(solution)/shard_map/ppermute | solution.py:242
  15.3 12.3 %all-to-all-start = ((f32[8,7,4,512]{3,2,1,0:T(4,128)}), f32[8,7,4,512]{3,2,1,0:T(4,128)S(1)}, u32[]{:S(2)}, u32[]{:S(2)}) async-start(f32[8,7,4,512]{3,2,1,0:T(4,128)} %get-tuple-element.26), calls=%async_computation | async-start | bytes 917504 | tf_op jit(solution)/shard_map/all_to_all | solution.py:231

commit v9 on v7

--- a/solution.py
+++ b/solution.py
@@ -70,13 +70,15 @@
         copies[t] = buffer[...]
 
 
-def lend_kernel(facts, tiles, lent, buffer, arrival):
-    slots = tiles.shape[1]
-    distance = 2 - 4 * facts[CORE_AT]
-    fetch = pltpu.make_async_copy(tiles.at[0, slot_at(facts, slots, distance)], buffer, arrival)
+def lend_kernel(offsets_hbm, tiles, lent, offsets, buffer, arrival):
+    ask = pltpu.make_async_copy(offsets_hbm, offsets, arrival.at[0])
+    ask.start()
+    ask.wait()
+    distance = 2 - 4 * lax.axis_index("core")
+    fetch = pltpu.make_async_copy(tiles.at[0, slot_at(offsets.at[0], tiles.shape[1], distance)], buffer, arrival.at[1])
     fetch.start()
     fetch.wait()
-    lent[...] = jnp.where(slot_live(facts, slots, distance), buffer[...].astype(jnp.float32), 0.0)
+    lent[...] = buffer[...].astype(jnp.float32)
 
 
 def arrange_kernel(facts, wet, tiles, inverse, ordered, shared, upper, arrival):
@@ -96,6 +98,8 @@
         at = slice(c * levels, (c + 1) * levels)
         shared[0:levels, at] = jnp.where(lane < wet[c], inverse[c], 0.0)
         shared[levels : levels + 8, at] = jnp.where(row < wet[c], 1.0, 0.0)
+    lending = jnp.where(slot_live(facts, slots, -2 * direction), 1.0, 0.0)
+    shared[levels + 4 :, :] = jnp.full((4, shared.shape[1]), lending, jnp.float32)
     upper[...] = jnp.full(upper.shape, facts[CORE_AT], jnp.int32).astype(jnp.float32)
     for fetch in fetches:
         fetch.wait()
@@ -140,6 +144,7 @@
             blocks[0, side * spans + s] = jnp.where(same, full_high, jnp.zeros_like(full_high))
             blocks[1, side * spans + s] = jnp.where(same, full_low, jnp.zeros_like(full_low))
         wet[side : side + 1, :] = adjoint[side, tracers + levels : tracers + levels + 1, :]
+        wet[2 + side : 3 + side, :] = adjoint[side, tracers + levels + 4 : tracers + levels + 5, :]
 
 
 def step_kernel(adjoint, ordered, borrowed, upper, slopes, uptake_t, release_t, *rest, section, levels, first):
@@ -163,7 +168,7 @@
             settled[side, :, at] = dot_split(high[:, at], low[:, at], blocks[0, k], blocks[1, k])
     is_upper = upper[0:1, :] > 0.5
     own_high, own_low = halves(jnp.where(is_upper, settled[1], settled[0]))
-    other = jnp.where(is_upper, settled[0], settled[1]).astype(jnp.bfloat16)
+    other = jnp.where(is_upper, wet[2:3, :] * settled[0], wet[3:4, :] * settled[1]).astype(jnp.bfloat16)
     send[0:tracers, :] = dot(own_high, ordered[0]) + dot(other, borrowed[...])
     send[tracers:, :] = dot(own_high, ordered[1])
     release_high, release_low = halves(release_t[...])
@@ -222,13 +227,13 @@
     facts = jnp.concatenate([tile_offset.reshape(-1), tile_count, core])
     lent = pl.pallas_call(
         lend_kernel,
-        in_specs=[smem, hbm],
+        in_specs=[hbm] * 2,
         out_specs=vmem,
         out_shape=shape((boxes, boxes), f32),
-        scratch_shapes=[pltpu.VMEM((boxes, boxes), bf16), dma],
+        scratch_shapes=[pltpu.SMEM(tile_offset.shape, jnp.int32), pltpu.VMEM((boxes, boxes), bf16), dma((2,))],
         compiler_params=lean,
         name="lend",
-    )(facts, in_hbm(explicit_tiles))
+    )(in_hbm(tile_offset), in_hbm(explicit_tiles))
     borrowed = lax.ppermute(lent, "core", [(0, 1), (1, 0)])
     ordered, shared, upper = pl.pallas_call(
         arrange_kernel,
@@ -261,7 +266,7 @@
     )(gathered, shared, uptake_weight)
     adjoint = lax.all_gather(start, "core")
     uptake_t, release_t = uptake_weight.T, release_weight.T
-    kept_shapes = [shape((2, 2 * spans, SPAN, SPAN), bf16), shape((2, boxes), f32)]
+    kept_shapes = [shape((2, 2 * spans, SPAN, SPAN), bf16), shape((4, boxes), f32)]
     kept = []
     for section in range(sections - 1, -1, -1):
         first = section == sections - 1

time: 97.6 us -> 96.4 us (0.988)
  no operation moved by 1% of the time
where the time goes in v9:
time: 96.4 us; the launch traced here: 95.7 us
  blocking collectives  61.8 us (64%)
  Pallas kernels  14.3 us (15%)
  starting transfers between devices  12.2 us (13%)
  waiting for transfers between devices  5.6 us (6%)
    all_gather x1, blocking collectives, local(): lax.all_gather(passed, 'ylo')  35.7 us
    all_gather x6, blocking collectives, local(): arrived = lax.all_gather(send, EVERY, axis_index_groups=groups)  11.8 us
    all_gather x6, blocking collectives, local(): adjoint = lax.all_gather(keep, 'core')  11.8 us
    ppermute x1, starting transfers between devices, local(): borrowed = lax.ppermute(lent, 'core', [(0, 1), (1, 0)])  8.73 us
    pallas_call x6, Pallas kernels, local(): pl.pallas_call(step, in_specs=[vmem] * (7 + len(kept)), out_specs=[vmem]...  5.87 us
    all_to_all x1, waiting for transfers between devices, local(): lax.all_to_all(copies, TRACER, split_axis=0, concat_axis=0, tiled=True)  5.6 us
    all_to_all x1, starting transfers between devices, local(): lax.all_to_all(copies, TRACER, split_axis=0, concat_axis=0, tiled=True)  3.48 us
    pallas_call x1, Pallas kernels, local(): pl.pallas_call(lend_kernel, in_specs=[hbm] * 2, out_specs=vmem, out_shape...  2.91 us
  transfers between devices with their start and end apart: 2, of which 1 were waited for; matrix products, arithmetic and copies ran while one was open for 0% of the time, Pallas kernels for 4%

profile of v9, /device:TPU:1, one launch (start us, length us, event | category | flops | bytes accessed | tf_op | source)
XLA Modules:
  0.0 95.7 jit_solution(13298130459116737972)
XLA Ops:
  0.0 0.0 copy-start.4
  0.0 0.0 copy-start.3
  0.0 0.0 copy-start.1
  0.0 0.0 copy-start.2
  0.0 0.0 copy-start
  0.0 2.9 %lend.1 = f32[512,512]{1,0:T(8,128)} custom-call(s32[1,5]{1,0:T(1,128)} %offsets_hbm.1, bf16[1,5,512,512]{3,2,1,0:T(8,128)(2,1)} %tiles.3), custom_call_target="tpu_custom_call" | custom-call | tf_op jit(solution)/shard_map/lend/pallas_call | solution.py:228
  3.0 8.7 %collective-permute-start = (f32[512,512]{1,0:T(8,128)}, f32[512,512]{1,0:T(8,128)}, u32[]{:S(2)}, u32[]{:S(2)}) collective-permute-start(f32[512,512]{1,0:T(8,128)} %lend.1), channel_id=1, source_target_pairs={{0,8},{8,0},{1,9},{9,1},{2,10},{10,2},{3,11},{11,3},{4,12},{12,4},... | collective-permute-start | bytes 3145736 | tf_op jit(solution)/shard_map/ppermute | solution.py:237
  11.7 1.6 %pack.1 = f32[8,7,4,512]{3,2,1,0:T(4,128)} custom-call(f32[4,512]{1,0:T(4,128)} %cotangent.1, f32[6,4,512]{2,1,0:T(4,128)} %states.1), custom_call_target="tpu_custom_call" | custom-call | tf_op jit(solution)/shard_map/pack/pallas_call | solution.py:217
  13.3 3.5 %all-to-all-start = ((f32[8,7,4,512]{3,2,1,0:T(4,128)}), f32[8,7,4,512]{3,2,1,0:T(4,128)S(1)}, u32[]{:S(2)}, u32[]{:S(2)}) async-start(f32[8,7,4,512]{3,2,1,0:T(4,128)} %pack.1), calls=%async_computation | async-start | bytes 917504 | tf_op jit(solution)/shard_map/all_to_all | solution.py:226
  17.5 0.0 copy-done.3
  17.5 0.1 copy.13
  17.6 0.0 copy-done.1
  17.6 0.1 copy.12
  17.6 0.0 copy-done.4
  17.6 0.1 pad_add_fusion.facts
  17.7 0.0 copy-done.2
  17.7 0.0 copy-done
  17.7 2.3 %arrange.1 = (bf16[4,512,512]{2,1,0:T(8,128)(2,1)S(1)}, f32[40,512]{1,0:T(8,128)S(1)}, f32[8,512]{1,0:T(8,128)S(1)}) custom-call(s32[7]{0:T(128)S(1)} %pad_add_fusion.facts, s32[16]{0:T(128)S(1)} %copy-done.2, bf16[1,5,512,512]{3,2,1,0:T(8,128)(2,1)} %tiles.3, f32[16,32,32]{2,1,0:T(8,128)S(1)} %copy-done), custom_call_target="tpu_custom_call" | custom-call | tf_op jit(solution)/shard_map/arrange/pallas_call | solution.py:238
  20.0 5.6 %all-to-all-done.gathered = f32[8,7,4,512]{3,2,1,0:T(4,128)S(1)} async-done(((f32[8,7,4,512]{3,2,1,0:T(4,128)}), f32[8,7,4,512]{3,2,1,0:T(4,128)S(1)}, u32[]{:S(2)}, u32[]{:S(2)}) %all-to-all-start) | async-done | bytes 458784 | tf_op jit(solution)/shard_map/all_to_all | solution.py:226
  25.6 0.3 gathered.1
  25.9 2.5 %all-gather = f32[144,512]{1,0:T(8,128)S(1)} all-gather(f32[72,512]{1,0:T(8,128)S(1)} %get-tuple-element.25), channel_id=2, replica_groups=mesh['z'=16,'yhi'=2,'core'=2,'x'=4,'ylo'=2] {'core'}, dimensions={0}, use_global_device_ids=true | all-gather | bytes 442368 | tf_op jit(solution)/shard_map/all_gather | solution.py:267
  28.5 0.0 collective-permute-done.borrowed
  28.5 1.3 %round.1.refs_2_ = bf16[512,512]{1,0:T(8,128)(2,1)S(1)} custom-call(f32[512,512]{1,0:T(8,128)} %collective-permute-done.borrowed), custom_call_target="tpu_custom_call" | custom-call | tf_op jit(solution)/shard_map/round/pallas_call | solution.py:251
  29.7 1.0 %shard_map.91 = (f32[64,512]{1,0:T(8,128)S(1)}, f32[64,512]{1,0:T(8,128)S(1)}, bf16[2,4,256,256]{3,2,1,0:T(8,128)(2,1)S(1)}, f32[4,512]{1,0:T(4,128)S(1)}) custom-call(f32[2,72,512]{2,1,0:T(8,128)S(1)} %bitcast.34, bf16[4,512,512]{2,1,0:T(8,128)(2,1)S(1)} %get-tuple-element.26.refs_1_, bf16[512,512]{1,0:T(8,128)(2,1)S(1)} %round.1.refs_2_, ...), custom_call_target="tpu_custom_call" | custom-call | tf_op jit(solution)/shard_map/pallas_call | solution.py:278
  30.7 2.0 %all-gather.1 = f32[128,512]{1,0:T(8,128)S(1)} all-gather(f32[64,512]{1,0:T(8,128)S(1)} %get-tuple-element.31), channel_id=3, replica_groups={{9,16},{8,0},{11,18},{10,2},{13,20},{12,4},{15,22},{14,6},{24,33},{25,1..., dimensions={0}, use_global_device_ids=true | all-gather | bytes 393216 | tf_op jit(solution)/shard_map/all_gather | solution.py:294
  32.7 2.0 %all-gather.2 = f32[128,512]{1,0:T(8,128)S(1)} all-gather(f32[64,512]{1,0:T(8,128)S(1)} %bitcast_add_fusion.4), channel_id=4, replica_groups=mesh['z'=16,'yhi'=2,'core'=2,'x'=4,'ylo'=2] {'core'}, dimensions={0}, use_global_device_ids=true | all-gather | bytes 393216 | tf_op jit(solution)/shard_map/all_gather | solution.py:296
  34.8 1.0 %shard_map.92 = (f32[64,512]{1,0:T(8,128)S(1)}, f32[64,512]{1,0:T(8,128)S(1)}) custom-call(f32[2,64,512]{2,1,0:T(8,128)S(1)} %bitcast.36, bf16[4,512,512]{2,1,0:T(8,128)(2,1)S(1)} %get-tuple-element.26.refs_1_, bf16[512,512]{1,0:T(8,128)(2,1)S(1)} %round.1.refs_2_, f32[8,512]{1,0:T(8,128)S(1)} %get-tuple-element.27.refs_3_, ...), custom_call_target="tpu_custom_call" | custom-call | tf_op jit(solution)/shard_map/pallas_call | solution.py:278
  35.7 2.0 %all-gather.3 = f32[128,512]{1,0:T(8,128)S(1)} all-gather(f32[64,512]{1,0:T(8,128)S(1)} %get-tuple-element.34), channel_id=5, replica_groups={{9,16},{8,0},{11,18},{10,2},{13,20},{12,4},{15,22},{14,6},{24,33},{25,1..., dimensions={0}, use_global_device_ids=true | all-gather | bytes 393216 | tf_op jit(solution)/shard_map/all_gather | solution.py:294
  37.7 2.0 %all-gather.4 = f32[128,512]{1,0:T(8,128)S(1)} all-gather(f32[64,512]{1,0:T(8,128)S(1)} %bitcast_add_fusion.3), channel_id=6, replica_groups=mesh['z'=16,'yhi'=2,'core'=2,'x'=4,'ylo'=2] {'core'}, dimensions={0}, use_global_device_ids=true | all-gather | bytes 393216 | tf_op jit(solution)/shard_map/all_gather | solution.py:296
  39.7 1.0 %shard_map.93 = (f32[64,512]{1,0:T(8,128)S(1)}, f32[64,512]{1,0:T(8,128)S(1)}) custom-call(f32[2,64,512]{2,1,0:T(8,128)S(1)} %bitcast.37, bf16[4,512,512]{2,1,0:T(8,128)(2,1)S(1)} %get-tuple-element.26.refs_1_, bf16[512,512]{1,0:T(8,128)(2,1)S(1)} %round.1.refs_2_, f32[8,512]{1,0:T(8,128)S(1)} %get-tuple-element.27.refs_3_, ...), custom_call_target="tpu_custom_call" | custom-call | tf_op jit(solution)/shard_map/pallas_call | solution.py:278
  40.7 2.0 %all-gather.5 = f32[128,512]{1,0:T(8,128)S(1)} all-gather(f32[64,512]{1,0:T(8,128)S(1)} %get-tuple-element.36), channel_id=7, replica_groups={{9,16},{8,0},{11,18},{10,2},{13,20},{12,4},{15,22},{14,6},{24,33},{25,1..., dimensions={0}, use_global_device_ids=true | all-gather | bytes 393216 | tf_op jit(solution)/shard_map/all_gather | solution.py:294
  42.7 2.0 %all-gather.6 = f32[128,512]{1,0:T(8,128)S(1)} all-gather(f32[64,512]{1,0:T(8,128)S(1)} %bitcast_add_fusion.2), channel_id=8, replica_groups=mesh['z'=16,'yhi'=2,'core'=2,'x'=4,'ylo'=2] {'core'}, dimensions={0}, use_global_device_ids=true | all-gather | bytes 393216 | tf_op jit(solution)/shard_map/all_gather | solution.py:296
  44.7 1.0 %shard_map.94 = (f32[64,512]{1,0:T(8,128)S(1)}, f32[64,512]{1,0:T(8,128)S(1)}) custom-call(f32[2,64,512]{2,1,0:T(8,128)S(1)} %bitcast.38, bf16[4,512,512]{2,1,0:T(8,128)(2,1)S(1)} %get-tuple-element.26.refs_1_, bf16[512,512]{1,0:T(8,128)(2,1)S(1)} %round.1.refs_2_, f32[8,512]{1,0:T(8,128)S(1)} %get-tuple-element.27.refs_3_, ...), custom_call_target="tpu_custom_call" | custom-call | tf_op jit(solution)/shard_map/pallas_call | solution.py:278
  45.7 2.0 %all-gather.7 = f32[128,512]{1,0:T(8,128)S(1)} all-gather(f32[64,512]{1,0:T(8,128)S(1)} %get-tuple-element.38), channel_id=9, replica_groups={{9,16},{8,0},{11,18},{10,2},{13,20},{12,4},{15,22},{14,6},{24,33},{25,1..., dimensions={0}, use_global_device_ids=true | all-gather | bytes 393216 | tf_op jit(solution)/shard_map/all_gather | solution.py:294
  47.7 2.0 %all-gather.8 = f32[128,512]{1,0:T(8,128)S(1)} all-gather(f32[64,512]{1,0:T(8,128)S(1)} %bitcast_add_fusion.1), channel_id=10, replica_groups=mesh['z'=16,'yhi'=2,'core'=2,'x'=4,'ylo'=2] {'core'}, dimensions={0}, use_global_device_ids=true | all-gather | bytes 393216 | tf_op jit(solution)/shard_map/all_gather | solution.py:296
  49.7 1.0 %shard_map.95 = (f32[64,512]{1,0:T(8,128)S(1)}, f32[64,512]{1,0:T(8,128)S(1)}) custom-call(f32[2,64,512]{2,1,0:T(8,128)S(1)} %bitcast.39, bf16[4,512,512]{2,1,0:T(8,128)(2,1)S(1)} %get-tuple-element.26.refs_1_, bf16[512,512]{1,0:T(8,128)(2,1)S(1)} %round.1.refs_2_, f32[8,512]{1,0:T(8,128)S(1)} %get-tuple-element.27.refs_3_, ...), custom_call_target="tpu_custom_call" | custom-call | tf_op jit(solution)/shard_map/pallas_call | solution.py:278
  50.7 2.0 %all-gather.9 = f32[128,512]{1,0:T(8,128)S(1)} all-gather(f32[64,512]{1,0:T(8,128)S(1)} %get-tuple-element.40), channel_id=11, replica_groups={{9,16},{8,0},{11,18},{10,2},{13,20},{12,4},{15,22},{14,6},{24,33},{25,1..., dimensions={0}, use_global_device_ids=true | all-gather | bytes 393216 | tf_op jit(solution)/shard_map/all_gather | solution.py:294
  52.7 2.0 %all-gather.10 = f32[128,512]{1,0:T(8,128)S(1)} all-gather(f32[64,512]{1,0:T(8,128)S(1)} %bitcast_add_fusion), channel_id=12, replica_groups=mesh['z'=16,'yhi'=2,'core'=2,'x'=4,'ylo'=2] {'core'}, dimensions={0}, use_global_device_ids=true | all-gather | bytes 393216 | tf_op jit(solution)/shard_map/all_gather | solution.py:296
  54.7 1.0 %shard_map.96 = (f32[64,512]{1,0:T(8,128)S(1)}, f32[64,512]{1,0:T(8,128)S(1)}) custom-call(f32[2,64,512]{2,1,0:T(8,128)S(1)} %bitcast.35, bf16[4,512,512]{2,1,0:T(8,128)(2,1)S(1)} %get-tuple-element.26.refs_1_, bf16[512,512]{1,0:T(8,128)(2,1)S(1)} %round.1.refs_2_, f32[8,512]{1,0:T(8,128)S(1)} %get-tuple-element.27.refs_3_, ...), custom_call_target="tpu_custom_call" | custom-call | tf_op jit(solution)/shard_map/pallas_call | solution.py:278
  55.7 1.9 %all_gather.99 = f32[2,16,512]{2,1,0:T(8,128)S(1)} all-gather(f32[1,16,512]{2,1,0:T(8,128)S(1)} %dynamic-slice_bitcast_fusion), channel_id=1, replica_groups={{9,16},{8,0},{11,18},{10,2},{13,20},{12,4},{15,22},{14,6},{24,33},{25,1..., dimensions={0}, use_global_device_ids=true | all-gather | bytes 98304 | tf_op jit(solution)/shard_map/all_gather | solution.py:294
  57.6 1.8 %all_gather.100 = f32[2,16,512]{2,1,0:T(8,128)S(1)} all-gather(f32[1,16,512]{2,1,0:T(8,128)S(1)} %bitcast_add_fusion.5), channel_id=1, replica_groups=mesh['z'=16,'yhi'=2,'core'=2,'x'=4,'ylo'=2] {'core'}, dimensions={0}, use_global_device_ids=true | all-gather | bytes 98304 | tf_op jit(solution)/shard_map/all_gather | solution.py:296
  59.5 35.7 %all_gather.101 = f32[2,4,512]{2,1,0:T(4,128)S(1)} all-gather(f32[1,4,512]{2,1,0:T(4,128)S(1)} %constant_dynamic-slice_fusion), channel_id=1, replica_groups=mesh['z'=16,'yhi'=2,'core'=2,'x'=4,'ylo'=2] {'ylo'}, dimensions={0}, use_global_device_ids=true | all-gather | bytes 24576 | tf_op jit(solution)/shard_map/all_gather | solution.py:302
  95.1 0.6 select_bitcast_fusion
  (12 shorter events, 0.1 us)
Async XLA Ops:
  0.0 17.6 %copy-start.4 = (s32[1,5]{1,0:T(1,128)S(1)}, s32[1,5]{1,0:T(1,128)}, u32[]{:S(2)}) copy-start(s32[1,5]{1,0:T(1,128)} %offsets_hbm.1) | copy-start | bytes 64
  0.0 17.5 %copy-start.3 = (f32[32,32]{1,0:T(8,128)S(1)}, f32[32,32]{1,0:T(8,128)}, u32[]{:S(2)}) copy-start(f32[32,32]{1,0:T(8,128)} %param.17) | copy-start | bytes 12292
  0.0 17.6 %copy-start.1 = (f32[32,32]{1,0:T(8,128)S(1)}, f32[32,32]{1,0:T(8,128)}, u32[]{:S(2)}) copy-start(f32[32,32]{1,0:T(8,128)} %uptake_weight.1) | copy-start | bytes 12292
  0.0 17.7 %copy-start.2 = (s32[16]{0:T(128)S(1)}, s32[16]{0:T(128)}, u32[]{:S(2)}) copy-start(s32[16]{0:T(128)} %wet.1) | copy-start | bytes 196
  0.0 17.7 %copy-start = (f32[16,32,32]{2,1,0:T(8,128)S(1)}, f32[16,32,32]{2,1,0:T(8,128)}, u32[]{:S(2)}) copy-start(f32[16,32,32]{2,1,0:T(8,128)} %inverse.1) | copy-start | bytes 196612
  3.0 25.5 %collective-permute-start = (f32[512,512]{1,0:T(8,128)}, f32[512,512]{1,0:T(8,128)}, u32[]{:S(2)}, u32[]{:S(2)}) collective-permute-start(f32[512,512]{1,0:T(8,128)} %lend.1), channel_id=1, source_target_pairs={{0,8},{8,0},{1,9},{9,1},{2,10},{10,2},{3,11},{11,3},{4,12},{12,4},... | collective-permute-start | bytes 3145736 | tf_op jit(solution)/shard_map/ppermute | solution.py:237
  13.3 12.3 %all-to-all-start = ((f32[8,7,4,512]{3,2,1,0:T(4,128)}), f32[8,7,4,512]{3,2,1,0:T(4,128)S(1)}, u32[]{:S(2)}, u32[]{:S(2)}) async-start(f32[8,7,4,512]{3,2,1,0:T(4,128)} %pack.1), calls=%async_computation | async-start | bytes 917504 | tf_op jit(solution)/shard_map/all_to_all | solution.py:226

commit v10 on v9

--- a/solution.py
+++ b/solution.py
@@ -59,15 +59,15 @@
     return live > 0
 
 
-def pack_kernel(cotangent, states, copies, buffer, fetched):
-    first = pltpu.make_async_copy(cotangent, buffer.at[0], fetched.at[0])
-    rest = pltpu.make_async_copy(states, buffer.at[pl.ds(1, states.shape[0])], fetched.at[1])
-    first.start()
-    rest.start()
-    first.wait()
-    rest.wait()
-    for t in range(copies.shape[0]):
-        copies[t] = buffer[...]
+def pack_kernel(cotangent, states, copies, sent):
+    peers = copies.shape[0]
+    sends = [pltpu.make_async_copy(cotangent, copies.at[t, 0], sent.at[0, t]) for t in range(peers)] + [
+        pltpu.make_async_copy(states, copies.at[t, pl.ds(1, states.shape[0])], sent.at[1, t]) for t in range(peers)
+    ]
+    for send in sends:
+        send.start()
+    for send in sends:
+        send.wait()
 
 
 def lend_kernel(offsets_hbm, tiles, lent, offsets, buffer, arrival):
@@ -217,9 +217,9 @@
     copies = pl.pallas_call(
         pack_kernel,
         in_specs=[hbm] * 2,
-        out_specs=vmem,
+        out_specs=hbm,
         out_shape=shape((peers, 1 + sections, tracers_here, boxes), f32),
-        scratch_shapes=[pltpu.VMEM((1 + sections, tracers_here, boxes), f32), dma((2,))],
+        scratch_shapes=[dma((2, peers))],
         compiler_params=lean,
         name="pack",
     )(in_hbm(cotangent), in_hbm(states))

time: 96.4 us -> 110 us (1.14)
  Pallas kernels: 14.3 us -> 27.8 us
    pallas_call x1, Pallas kernels: 1.63 us -> 15.1 us  [local(): pl.pallas_call(pack_kernel, in_specs=[hbm] * 2, out_specs=hbm, out_shape=...]
  transfers between devices with their start and end apart: 2 -> 2, of which waited for: 1 -> 1; matrix products, arithmetic and copies ran while one was open for 0% -> 0% of each run, Pallas kernels for 4% -> 16%
where the time goes in v10:
time: 110 us; the launch traced here: 109 us
  blocking collectives  61.8 us (56%)
  Pallas kernels  27.8 us (25%)
  starting transfers between devices  12.2 us (11%)
  waiting for transfers between devices  5.6 us (5%)
    all_gather x1, blocking collectives, local(): lax.all_gather(passed, 'ylo')  35.7 us
    pallas_call x1, Pallas kernels, local(): pl.pallas_call(pack_kernel, in_specs=[hbm] * 2, out_specs=hbm, out_shape=...  15.1 us
    all_gather x6, blocking collectives, local(): arrived = lax.all_gather(send, EVERY, axis_index_groups=groups)  11.8 us
    all_gather x6, blocking collectives, local(): adjoint = lax.all_gather(keep, 'core')  11.8 us
    ppermute x1, starting transfers between devices, local(): borrowed = lax.ppermute(lent, 'core', [(0, 1), (1, 0)])  8.73 us
    pallas_call x6, Pallas kernels, local(): pl.pallas_call(step, in_specs=[vmem] * (7 + len(kept)), out_specs=[vmem]...  5.88 us
    all_to_all x1, waiting for transfers between devices, local(): lax.all_to_all(copies, TRACER, split_axis=0, concat_axis=0, tiled=True)  5.6 us
    all_to_all x1, starting transfers between devices, local(): lax.all_to_all(copies, TRACER, split_axis=0, concat_axis=0, tiled=True)  3.48 us
  transfers between devices with their start and end apart: 2, of which 1 were waited for; matrix products, arithmetic and copies ran while one was open for 0% of the time, Pallas kernels for 16%

profile of v10, /device:TPU:1, one launch (start us, length us, event | category | flops | bytes accessed | tf_op | source)
XLA Modules:
  0.0 109.2 jit_solution(16774941301996227472)
XLA Ops:
  0.0 0.0 copy-start.4
  0.0 0.0 copy-start.3
  0.0 0.0 copy-start.1
  0.0 0.0 copy-start.2
  0.0 0.0 copy-start
  0.0 2.9 %lend.1 = f32[512,512]{1,0:T(8,128)} custom-call(s32[1,5]{1,0:T(1,128)} %offsets_hbm.1, bf16[1,5,512,512]{3,2,1,0:T(8,128)(2,1)} %tiles.3), custom_call_target="tpu_custom_call" | custom-call | tf_op jit(solution)/shard_map/lend/pallas_call | solution.py:228
  3.0 8.7 %collective-permute-start = (f32[512,512]{1,0:T(8,128)}, f32[512,512]{1,0:T(8,128)}, u32[]{:S(2)}, u32[]{:S(2)}) collective-permute-start(f32[512,512]{1,0:T(8,128)} %lend.1), channel_id=1, source_target_pairs={{0,8},{8,0},{1,9},{9,1},{2,10},{10,2},{3,11},{11,3},{4,12},{12,4},... | collective-permute-start | bytes 3145736 | tf_op jit(solution)/shard_map/ppermute | solution.py:237
  11.7 15.1 %pack.1 = f32[8,7,4,512]{3,2,1,0:T(4,128)} custom-call(f32[4,512]{1,0:T(4,128)} %cotangent.1, f32[6,4,512]{2,1,0:T(4,128)} %states.1), custom_call_target="tpu_custom_call" | custom-call | tf_op jit(solution)/shard_map/pack/pallas_call | solution.py:217
  26.8 3.5 %all-to-all-start = ((f32[8,7,4,512]{3,2,1,0:T(4,128)}), f32[8,7,4,512]{3,2,1,0:T(4,128)S(1)}, u32[]{:S(2)}, u32[]{:S(2)}) async-start(f32[8,7,4,512]{3,2,1,0:T(4,128)} %pack.1), calls=%async_computation | async-start | bytes 917504 | tf_op jit(solution)/shard_map/all_to_all | solution.py:226
  31.0 0.0 copy-done.3
  31.0 0.1 copy.13
  31.1 0.0 copy-done.1
  31.1 0.1 copy.12
  31.2 0.0 copy-done.4
  31.2 0.1 pad_add_fusion.facts
  31.2 0.0 copy-done.2
  31.2 0.0 copy-done
  31.2 2.3 %arrange.1 = (bf16[4,512,512]{2,1,0:T(8,128)(2,1)S(1)}, f32[40,512]{1,0:T(8,128)S(1)}, f32[8,512]{1,0:T(8,128)S(1)}) custom-call(s32[7]{0:T(128)S(1)} %pad_add_fusion.facts, s32[16]{0:T(128)S(1)} %copy-done.2, bf16[1,5,512,512]{3,2,1,0:T(8,128)(2,1)} %tiles.3, f32[16,32,32]{2,1,0:T(8,128)S(1)} %copy-done), custom_call_target="tpu_custom_call" | custom-call | tf_op jit(solution)/shard_map/arrange/pallas_call | solution.py:238
  33.5 5.6 %all-to-all-done.gathered = f32[8,7,4,512]{3,2,1,0:T(4,128)S(1)} async-done(((f32[8,7,4,512]{3,2,1,0:T(4,128)}), f32[8,7,4,512]{3,2,1,0:T(4,128)S(1)}, u32[]{:S(2)}, u32[]{:S(2)}) %all-to-all-start) | async-done | bytes 458784 | tf_op jit(solution)/shard_map/all_to_all | solution.py:226
  39.1 0.3 gathered.1
  39.5 2.5 %all-gather = f32[144,512]{1,0:T(8,128)S(1)} all-gather(f32[72,512]{1,0:T(8,128)S(1)} %get-tuple-element.25), channel_id=2, replica_groups=mesh['z'=16,'yhi'=2,'core'=2,'x'=4,'ylo'=2] {'core'}, dimensions={0}, use_global_device_ids=true | all-gather | bytes 442368 | tf_op jit(solution)/shard_map/all_gather | solution.py:267
  42.0 0.0 collective-permute-done.borrowed
  42.0 1.3 %round.1.refs_2_ = bf16[512,512]{1,0:T(8,128)(2,1)S(1)} custom-call(f32[512,512]{1,0:T(8,128)} %collective-permute-done.borrowed), custom_call_target="tpu_custom_call" | custom-call | tf_op jit(solution)/shard_map/round/pallas_call | solution.py:251
  43.3 1.0 shard_map.91
  44.2 2.0 %all-gather.1 = f32[128,512]{1,0:T(8,128)S(1)} all-gather(f32[64,512]{1,0:T(8,128)S(1)} %get-tuple-element.31), channel_id=3, replica_groups={{9,16},{8,0},{11,18},{10,2},{13,20},{12,4},{15,22},{14,6},{24,33},{25,1..., dimensions={0}, use_global_device_ids=true | all-gather | bytes 393216 | tf_op jit(solution)/shard_map/all_gather | solution.py:294
  46.3 2.0 %all-gather.2 = f32[128,512]{1,0:T(8,128)S(1)} all-gather(f32[64,512]{1,0:T(8,128)S(1)} %bitcast_add_fusion.4), channel_id=4, replica_groups=mesh['z'=16,'yhi'=2,'core'=2,'x'=4,'ylo'=2] {'core'}, dimensions={0}, use_global_device_ids=true | all-gather | bytes 393216 | tf_op jit(solution)/shard_map/all_gather | solution.py:296
  48.3 1.0 shard_map.92
  49.2 2.0 %all-gather.3 = f32[128,512]{1,0:T(8,128)S(1)} all-gather(f32[64,512]{1,0:T(8,128)S(1)} %get-tuple-element.34), channel_id=5, replica_groups={{9,16},{8,0},{11,18},{10,2},{13,20},{12,4},{15,22},{14,6},{24,33},{25,1..., dimensions={0}, use_global_device_ids=true | all-gather | bytes 393216 | tf_op jit(solution)/shard_map/all_gather | solution.py:294
  51.3 2.0 %all-gather.4 = f32[128,512]{1,0:T(8,128)S(1)} all-gather(f32[64,512]{1,0:T(8,128)S(1)} %bitcast_add_fusion.3), channel_id=6, replica_groups=mesh['z'=16,'yhi'=2,'core'=2,'x'=4,'ylo'=2] {'core'}, dimensions={0}, use_global_device_ids=true | all-gather | bytes 393216 | tf_op jit(solution)/shard_map/all_gather | solution.py:296
  53.2 1.0 shard_map.93
  54.2 2.0 %all-gather.5 = f32[128,512]{1,0:T(8,128)S(1)} all-gather(f32[64,512]{1,0:T(8,128)S(1)} %get-tuple-element.36), channel_id=7, replica_groups={{9,16},{8,0},{11,18},{10,2},{13,20},{12,4},{15,22},{14,6},{24,33},{25,1..., dimensions={0}, use_global_device_ids=true | all-gather | bytes 393216 | tf_op jit(solution)/shard_map/all_gather | solution.py:294
  56.2 2.0 %all-gather.6 = f32[128,512]{1,0:T(8,128)S(1)} all-gather(f32[64,512]{1,0:T(8,128)S(1)} %bitcast_add_fusion.2), channel_id=8, replica_groups=mesh['z'=16,'yhi'=2,'core'=2,'x'=4,'ylo'=2] {'core'}, dimensions={0}, use_global_device_ids=true | all-gather | bytes 393216 | tf_op jit(solution)/shard_map/all_gather | solution.py:296
  58.2 1.0 shard_map.94
  59.2 2.0 %all-gather.7 = f32[128,512]{1,0:T(8,128)S(1)} all-gather(f32[64,512]{1,0:T(8,128)S(1)} %get-tuple-element.38), channel_id=9, replica_groups={{9,16},{8,0},{11,18},{10,2},{13,20},{12,4},{15,22},{14,6},{24,33},{25,1..., dimensions={0}, use_global_device_ids=true | all-gather | bytes 393216 | tf_op jit(solution)/shard_map/all_gather | solution.py:294
  61.2 2.0 %all-gather.8 = f32[128,512]{1,0:T(8,128)S(1)} all-gather(f32[64,512]{1,0:T(8,128)S(1)} %bitcast_add_fusion.1), channel_id=10, replica_groups=mesh['z'=16,'yhi'=2,'core'=2,'x'=4,'ylo'=2] {'core'}, dimensions={0}, use_global_device_ids=true | all-gather | bytes 393216 | tf_op jit(solution)/shard_map/all_gather | solution.py:296
  63.2 1.0 shard_map.95
  64.2 2.0 %all-gather.9 = f32[128,512]{1,0:T(8,128)S(1)} all-gather(f32[64,512]{1,0:T(8,128)S(1)} %get-tuple-element.40), channel_id=11, replica_groups={{9,16},{8,0},{11,18},{10,2},{13,20},{12,4},{15,22},{14,6},{24,33},{25,1..., dimensions={0}, use_global_device_ids=true | all-gather | bytes 393216 | tf_op jit(solution)/shard_map/all_gather | solution.py:294
  66.2 2.0 %all-gather.10 = f32[128,512]{1,0:T(8,128)S(1)} all-gather(f32[64,512]{1,0:T(8,128)S(1)} %bitcast_add_fusion), channel_id=12, replica_groups=mesh['z'=16,'yhi'=2,'core'=2,'x'=4,'ylo'=2] {'core'}, dimensions={0}, use_global_device_ids=true | all-gather | bytes 393216 | tf_op jit(solution)/shard_map/all_gather | solution.py:296
  68.2 1.0 shard_map.96
  69.2 1.9 %all_gather.99 = f32[2,16,512]{2,1,0:T(8,128)S(1)} all-gather(f32[1,16,512]{2,1,0:T(8,128)S(1)} %dynamic-slice_bitcast_fusion), channel_id=1, replica_groups={{9,16},{8,0},{11,18},{10,2},{13,20},{12,4},{15,22},{14,6},{24,33},{25,1..., dimensions={0}, use_global_device_ids=true | all-gather | bytes 98304 | tf_op jit(solution)/shard_map/all_gather | solution.py:294
  71.1 1.8 %all_gather.100 = f32[2,16,512]{2,1,0:T(8,128)S(1)} all-gather(f32[1,16,512]{2,1,0:T(8,128)S(1)} %bitcast_add_fusion.5), channel_id=1, replica_groups=mesh['z'=16,'yhi'=2,'core'=2,'x'=4,'ylo'=2] {'core'}, dimensions={0}, use_global_device_ids=true | all-gather | bytes 98304 | tf_op jit(solution)/shard_map/all_gather | solution.py:296
  73.0 35.7 %all_gather.101 = f32[2,4,512]{2,1,0:T(4,128)S(1)} all-gather(f32[1,4,512]{2,1,0:T(4,128)S(1)} %constant_dynamic-slice_fusion), channel_id=1, replica_groups=mesh['z'=16,'yhi'=2,'core'=2,'x'=4,'ylo'=2] {'ylo'}, dimensions={0}, use_global_device_ids=true | all-gather | bytes 24576 | tf_op jit(solution)/shard_map/all_gather | solution.py:302
  108.6 0.6 select_bitcast_fusion
  (12 shorter events, 0.1 us)
Async XLA Ops:
  0.0 31.2 %copy-start.4 = (s32[1,5]{1,0:T(1,128)S(1)}, s32[1,5]{1,0:T(1,128)}, u32[]{:S(2)}) copy-start(s32[1,5]{1,0:T(1,128)} %offsets_hbm.1) | copy-start | bytes 64
  0.0 31.0 %copy-start.3 = (f32[32,32]{1,0:T(8,128)S(1)}, f32[32,32]{1,0:T(8,128)}, u32[]{:S(2)}) copy-start(f32[32,32]{1,0:T(8,128)} %param.17) | copy-start | bytes 12292
  0.0 31.1 %copy-start.1 = (f32[32,32]{1,0:T(8,128)S(1)}, f32[32,32]{1,0:T(8,128)}, u32[]{:S(2)}) copy-start(f32[32,32]{1,0:T(8,128)} %uptake_weight.1) | copy-start | bytes 12292
  0.0 31.2 %copy-start.2 = (s32[16]{0:T(128)S(1)}, s32[16]{0:T(128)}, u32[]{:S(2)}) copy-start(s32[16]{0:T(128)} %wet.1) | copy-start | bytes 196
  0.0 31.2 %copy-start = (f32[16,32,32]{2,1,0:T(8,128)S(1)}, f32[16,32,32]{2,1,0:T(8,128)}, u32[]{:S(2)}) copy-start(f32[16,32,32]{2,1,0:T(8,128)} %inverse.1) | copy-start | bytes 196612
  3.0 39.0 %collective-permute-start = (f32[512,512]{1,0:T(8,128)}, f32[512,512]{1,0:T(8,128)}, u32[]{:S(2)}, u32[]{:S(2)}) collective-permute-start(f32[512,512]{1,0:T(8,128)} %lend.1), channel_id=1, source_target_pairs={{0,8},{8,0},{1,9},{9,1},{2,10},{10,2},{3,11},{11,3},{4,12},{12,4},... | collective-permute-start | bytes 3145736 | tf_op jit(solution)/shard_map/ppermute | solution.py:237
  26.8 12.3 %all-to-all-start = ((f32[8,7,4,512]{3,2,1,0:T(4,128)}), f32[8,7,4,512]{3,2,1,0:T(4,128)S(1)}, u32[]{:S(2)}, u32[]{:S(2)}) async-start(f32[8,7,4,512]{3,2,1,0:T(4,128)} %pack.1), calls=%async_computation | async-start | bytes 917504 | tf_op jit(solution)/shard_map/all_to_all | solution.py:226

commit v11 on v9

--- a/solution.py
+++ b/solution.py
@@ -110,10 +110,6 @@
             ordered[n] = jnp.zeros(ordered.shape[1:], ordered.dtype)
 
 
-def round_kernel(borrowed, tile_out):
-    tile_out[...] = borrowed[...].astype(jnp.bfloat16)
-
-
 def gathered_kernel(gathered, shared, uptake_weight, start, slopes):
     peers, _, few, _ = gathered.shape
     tracers = uptake_weight.shape[0]
@@ -150,11 +146,14 @@
 def step_kernel(adjoint, ordered, borrowed, upper, slopes, uptake_t, release_t, *rest, section, levels, first):
     tracers = uptake_t.shape[0]
     if first:
-        send, keep, blocks, wet, settled = rest
+        send, keep, blocks, wet, tile, settled, buffer, arrival = rest
+        fetch = pltpu.make_async_copy(borrowed, buffer, arrival)
+        fetch.start()
         lay_out_blocks(adjoint, tracers, levels, blocks, wet)
         pair = (adjoint[0, 0:tracers, :], adjoint[1, 0:tracers, :])
     else:
         blocks, wet, send, keep, settled = rest
+        tile = borrowed
         pair = (
             wet[0:1, :] * (adjoint[0, 0:tracers, :] + adjoint[1, tracers:, :]),
             wet[1:2, :] * (adjoint[1, 0:tracers, :] + adjoint[0, tracers:, :]),
@@ -169,7 +168,6 @@
     is_upper = upper[0:1, :] > 0.5
     own_high, own_low = halves(jnp.where(is_upper, settled[1], settled[0]))
     other = jnp.where(is_upper, wet[2:3, :] * settled[0], wet[3:4, :] * settled[1]).astype(jnp.bfloat16)
-    send[0:tracers, :] = dot(own_high, ordered[0]) + dot(other, borrowed[...])
     send[tracers:, :] = dot(own_high, ordered[1])
     release_high, release_low = halves(release_t[...])
     pushed = slopes[section] * dot_split(release_high, release_low, own_high, own_low)
@@ -177,6 +175,10 @@
     uptake_high, uptake_low = halves(uptake_t[...])
     keep[0:tracers, :] = dot(own_high, ordered[2]) + dot_split(uptake_high, uptake_low, pushed_high, pushed_low)
     keep[tracers:, :] = dot(own_high, ordered[3])
+    if first:
+        fetch.wait()
+        tile[...] = buffer[...].astype(jnp.bfloat16)
+    send[0:tracers, :] = dot(own_high, ordered[0]) + dot(other, tile[...])
 
 
 def local(
@@ -234,7 +236,7 @@
         compiler_params=lean,
         name="lend",
     )(in_hbm(tile_offset), in_hbm(explicit_tiles))
-    borrowed = lax.ppermute(lent, "core", [(0, 1), (1, 0)])
+    borrowed = in_hbm(lax.ppermute(lent, "core", [(0, 1), (1, 0)]))
     ordered, shared, upper = pl.pallas_call(
         arrange_kernel,
         in_specs=[smem] * 2 + [hbm, vmem],
@@ -248,14 +250,6 @@
         compiler_params=lean,
         name="arrange",
     )(facts, wet_levels, in_hbm(explicit_tiles), implicit_inverse)
-    borrowed = pl.pallas_call(
-        round_kernel,
-        in_specs=[vmem],
-        out_specs=vmem,
-        out_shape=shape((boxes, boxes), bf16),
-        compiler_params=lean,
-        name="round",
-    )(borrowed)
     start, slopes = pl.pallas_call(
         gathered_kernel,
         in_specs=[vmem] * 3,
@@ -274,16 +268,17 @@
         def step(*refs, section=section, first=first):
             step_kernel(*refs, section=section, levels=levels, first=first)
 
-        out_shape = [shape((2 * tracers, boxes), f32)] * 2 + kept_shapes * first
+        out_shape = [shape((2 * tracers, boxes), f32)] * 2 + (kept_shapes + [shape((boxes, boxes), bf16)]) * first
         send, keep, *made = pl.pallas_call(
             step,
-            in_specs=[vmem] * (7 + len(kept)),
+            in_specs=[vmem] * 2 + [hbm if first else vmem] + [vmem] * (4 + len(kept)),
             out_specs=[vmem] * len(out_shape),
             out_shape=out_shape,
-            scratch_shapes=[pltpu.VMEM((2, tracers, boxes), f32)],
+            scratch_shapes=[pltpu.VMEM((2, tracers, boxes), f32)] + [pltpu.VMEM((boxes, boxes), f32), dma] * first,
             compiler_params=lean,
         )(adjoint, ordered, borrowed, upper, slopes, uptake_t, release_t, *kept)
-        kept = made or kept
+        if first:
+            *kept, borrowed = made
         if section == 0:
             rows = ylo_size * tracers_here
             at = (0, lax.axis_index("x") * rows, 0)

time: 96.4 us -> 95.7 us (level)
    pallas_call x7 -> x6, Pallas kernels: 7.15 us -> 6.44 us  [local(): pl.pallas_call(step, in_specs=[vmem] * 2 + [hbm if first else vmem] + [vm...]
where the time goes in v11:
time: 95.7 us; the launch traced here: 95 us
  blocking collectives  61.8 us (65%)
  Pallas kernels  13.6 us (14%)
  starting transfers between devices  12.2 us (13%)
  waiting for transfers between devices  5.61 us (6%)
    all_gather x1, blocking collectives, local(): lax.all_gather(passed, 'ylo')  35.7 us
    all_gather x6, blocking collectives, local(): arrived = lax.all_gather(send, EVERY, axis_index_groups=groups)  11.8 us
    all_gather x6, blocking collectives, local(): adjoint = lax.all_gather(keep, 'core')  11.8 us
    ppermute x1, starting transfers between devices, local(): borrowed = in_hbm(lax.ppermute(lent, 'core', [(0, 1), (1, 0)]))  8.73 us
    pallas_call x6, Pallas kernels, local(): pl.pallas_call(step, in_specs=[vmem] * 2 + [hbm if first else vmem] + [vm...  6.44 us
    all_to_all x1, waiting for transfers between devices, local(): lax.all_to_all(copies, TRACER, split_axis=0, concat_axis=0, tiled=True)  5.6 us
    all_to_all x1, starting transfers between devices, local(): lax.all_to_all(copies, TRACER, split_axis=0, concat_axis=0, tiled=True)  3.48 us
    pallas_call x1, Pallas kernels, local(): pl.pallas_call(lend_kernel, in_specs=[hbm] * 2, out_specs=vmem, out_shape...  2.91 us
  transfers between devices with their start and end apart: 2, of which 1 were waited for; matrix products, arithmetic and copies ran while one was open for 0% of the time, Pallas kernels for 4%

profile of v11, /device:TPU:1, one launch (start us, length us, event | category | flops | bytes accessed | tf_op | source)
XLA Modules:
  0.0 95.0 jit_solution(3812266206805857634)
XLA Ops:
  0.0 0.0 copy-start.4
  0.0 0.0 copy-start.1
  0.0 0.0 copy-start.3
  0.0 0.0 copy-start
  0.0 0.0 copy-start.2
  0.0 2.9 %lend.1 = f32[512,512]{1,0:T(8,128)} custom-call(s32[1,5]{1,0:T(1,128)} %offsets_hbm.1, bf16[1,5,512,512]{3,2,1,0:T(8,128)(2,1)} %tiles.3), custom_call_target="tpu_custom_call" | custom-call | tf_op jit(solution)/shard_map/lend/pallas_call | solution.py:230
  3.0 8.7 %collective-permute-start = (f32[512,512]{1,0:T(8,128)}, f32[512,512]{1,0:T(8,128)}, u32[]{:S(2)}, u32[]{:S(2)}) collective-permute-start(f32[512,512]{1,0:T(8,128)} %lend.1), channel_id=1, source_target_pairs={{0,8},{8,0},{1,9},{9,1},{2,10},{10,2},{3,11},{11,3},{4,12},{12,4},... | collective-permute-start | bytes 3145736 | tf_op jit(solution)/shard_map/ppermute | solution.py:239
  11.7 1.6 %pack.1 = f32[8,7,4,512]{3,2,1,0:T(4,128)} custom-call(f32[4,512]{1,0:T(4,128)} %cotangent.1, f32[6,4,512]{2,1,0:T(4,128)} %states.1), custom_call_target="tpu_custom_call" | custom-call | tf_op jit(solution)/shard_map/pack/pallas_call | solution.py:219
  13.3 3.5 %all-to-all-start = ((f32[8,7,4,512]{3,2,1,0:T(4,128)}), f32[8,7,4,512]{3,2,1,0:T(4,128)S(1)}, u32[]{:S(2)}, u32[]{:S(2)}) async-start(f32[8,7,4,512]{3,2,1,0:T(4,128)} %pack.1), calls=%async_computation | async-start | bytes 917504 | tf_op jit(solution)/shard_map/all_to_all | solution.py:228
  17.5 0.0 copy-done.1
  17.5 0.1 copy.12
  17.6 0.0 copy-done.3
  17.6 0.1 copy.13
  17.6 0.0 copy-done.4
  17.6 0.1 pad_add_fusion.facts
  17.7 0.0 copy-done
  17.7 0.0 copy-done.2
  17.7 2.3 %arrange.1 = (bf16[4,512,512]{2,1,0:T(8,128)(2,1)S(1)}, f32[40,512]{1,0:T(8,128)S(1)}, f32[8,512]{1,0:T(8,128)S(1)}) custom-call(s32[7]{0:T(128)S(1)} %pad_add_fusion.facts, s32[16]{0:T(128)S(1)} %copy-done.2, bf16[1,5,512,512]{3,2,1,0:T(8,128)(2,1)} %tiles.3, f32[16,32,32]{2,1,0:T(8,128)S(1)} %copy-done), custom_call_target="tpu_custom_call" | custom-call | tf_op jit(solution)/shard_map/arrange/pallas_call | solution.py:240
  20.0 5.6 %all-to-all-done.gathered = f32[8,7,4,512]{3,2,1,0:T(4,128)S(1)} async-done(((f32[8,7,4,512]{3,2,1,0:T(4,128)}), f32[8,7,4,512]{3,2,1,0:T(4,128)S(1)}, u32[]{:S(2)}, u32[]{:S(2)}) %all-to-all-start) | async-done | bytes 458784 | tf_op jit(solution)/shard_map/all_to_all | solution.py:228
  25.6 0.3 gathered.1
  25.9 2.5 %all-gather = f32[144,512]{1,0:T(8,128)S(1)} all-gather(f32[72,512]{1,0:T(8,128)S(1)} %get-tuple-element.26), channel_id=2, replica_groups=mesh['z'=16,'yhi'=2,'core'=2,'x'=4,'ylo'=2] {'core'}, dimensions={0}, use_global_device_ids=true | all-gather | bytes 442368 | tf_op jit(solution)/shard_map/all_gather | solution.py:261
  28.5 0.0 collective-permute-done.refs_2_
  28.5 1.5 %shard_map.91 = (f32[64,512]{1,0:T(8,128)S(1)}, f32[64,512]{1,0:T(8,128)S(1)}, bf16[2,4,256,256]{3,2,1,0:T(8,128)(2,1)S(1)}, f32[4,512]{1,0:T(4,128)S(1)}, bf16[512,512]{1,0:T(8,128)(2,1)S(1)}) custom-call(f32[2,72,512]{2,1,0:T(8,128)S(1)} %bitcast.34, bf16[4,512,512]{2,1,0:T(8,128)(2,1)S(1)} %get-tuple-element.27.refs_1_, ...), custom_call_target="tpu_custom_call" | custom-call | tf_op jit(solution)/shard_map/pallas_call | solution.py:272
  30.0 2.0 %all-gather.1 = f32[128,512]{1,0:T(8,128)S(1)} all-gather(f32[64,512]{1,0:T(8,128)S(1)} %get-tuple-element.32), channel_id=3, replica_groups={{9,16},{8,0},{11,18},{10,2},{13,20},{12,4},{15,22},{14,6},{24,33},{25,1..., dimensions={0}, use_global_device_ids=true | all-gather | bytes 393216 | tf_op jit(solution)/shard_map/all_gather | solution.py:289
  32.0 2.0 %all-gather.2 = f32[128,512]{1,0:T(8,128)S(1)} all-gather(f32[64,512]{1,0:T(8,128)S(1)} %bitcast_add_fusion.4), channel_id=4, replica_groups=mesh['z'=16,'yhi'=2,'core'=2,'x'=4,'ylo'=2] {'core'}, dimensions={0}, use_global_device_ids=true | all-gather | bytes 393216 | tf_op jit(solution)/shard_map/all_gather | solution.py:291
  34.0 1.0 %shard_map.92 = (f32[64,512]{1,0:T(8,128)S(1)}, f32[64,512]{1,0:T(8,128)S(1)}) custom-call(f32[2,64,512]{2,1,0:T(8,128)S(1)} %bitcast.36, bf16[4,512,512]{2,1,0:T(8,128)(2,1)S(1)} %get-tuple-element.27.refs_1_, bf16[512,512]{1,0:T(8,128)(2,1)S(1)} %get-tuple-element.33.refs_2_, f32[8,512]{1,0:T(8,128)S(1)} %get-tuple-element.28.refs_3_, ...), custom_call_target="tpu_custom_call" | custom-call | tf_op jit(solution)/shard_map/pallas_call | solution.py:272
  35.0 2.0 %all-gather.3 = f32[128,512]{1,0:T(8,128)S(1)} all-gather(f32[64,512]{1,0:T(8,128)S(1)} %get-tuple-element.36), channel_id=5, replica_groups={{9,16},{8,0},{11,18},{10,2},{13,20},{12,4},{15,22},{14,6},{24,33},{25,1..., dimensions={0}, use_global_device_ids=true | all-gather | bytes 393216 | tf_op jit(solution)/shard_map/all_gather | solution.py:289
  37.0 2.0 %all-gather.4 = f32[128,512]{1,0:T(8,128)S(1)} all-gather(f32[64,512]{1,0:T(8,128)S(1)} %bitcast_add_fusion.3), channel_id=6, replica_groups=mesh['z'=16,'yhi'=2,'core'=2,'x'=4,'ylo'=2] {'core'}, dimensions={0}, use_global_device_ids=true | all-gather | bytes 393216 | tf_op jit(solution)/shard_map/all_gather | solution.py:291
  39.0 1.0 %shard_map.93 = (f32[64,512]{1,0:T(8,128)S(1)}, f32[64,512]{1,0:T(8,128)S(1)}) custom-call(f32[2,64,512]{2,1,0:T(8,128)S(1)} %bitcast.37, bf16[4,512,512]{2,1,0:T(8,128)(2,1)S(1)} %get-tuple-element.27.refs_1_, bf16[512,512]{1,0:T(8,128)(2,1)S(1)} %get-tuple-element.33.refs_2_, f32[8,512]{1,0:T(8,128)S(1)} %get-tuple-element.28.refs_3_, ...), custom_call_target="tpu_custom_call" | custom-call | tf_op jit(solution)/shard_map/pallas_call | solution.py:272
  40.0 2.0 %all-gather.5 = f32[128,512]{1,0:T(8,128)S(1)} all-gather(f32[64,512]{1,0:T(8,128)S(1)} %get-tuple-element.38), channel_id=7, replica_groups={{9,16},{8,0},{11,18},{10,2},{13,20},{12,4},{15,22},{14,6},{24,33},{25,1..., dimensions={0}, use_global_device_ids=true | all-gather | bytes 393216 | tf_op jit(solution)/shard_map/all_gather | solution.py:289
  42.0 2.0 %all-gather.6 = f32[128,512]{1,0:T(8,128)S(1)} all-gather(f32[64,512]{1,0:T(8,128)S(1)} %bitcast_add_fusion.2), channel_id=8, replica_groups=mesh['z'=16,'yhi'=2,'core'=2,'x'=4,'ylo'=2] {'core'}, dimensions={0}, use_global_device_ids=true | all-gather | bytes 393216 | tf_op jit(solution)/shard_map/all_gather | solution.py:291
  44.0 1.0 %shard_map.94 = (f32[64,512]{1,0:T(8,128)S(1)}, f32[64,512]{1,0:T(8,128)S(1)}) custom-call(f32[2,64,512]{2,1,0:T(8,128)S(1)} %bitcast.38, bf16[4,512,512]{2,1,0:T(8,128)(2,1)S(1)} %get-tuple-element.27.refs_1_, bf16[512,512]{1,0:T(8,128)(2,1)S(1)} %get-tuple-element.33.refs_2_, f32[8,512]{1,0:T(8,128)S(1)} %get-tuple-element.28.refs_3_, ...), custom_call_target="tpu_custom_call" | custom-call | tf_op jit(solution)/shard_map/pallas_call | solution.py:272
  45.0 2.0 %all-gather.7 = f32[128,512]{1,0:T(8,128)S(1)} all-gather(f32[64,512]{1,0:T(8,128)S(1)} %get-tuple-element.40), channel_id=9, replica_groups={{9,16},{8,0},{11,18},{10,2},{13,20},{12,4},{15,22},{14,6},{24,33},{25,1..., dimensions={0}, use_global_device_ids=true | all-gather | bytes 393216 | tf_op jit(solution)/shard_map/all_gather | solution.py:289
  47.0 2.0 %all-gather.8 = f32[128,512]{1,0:T(8,128)S(1)} all-gather(f32[64,512]{1,0:T(8,128)S(1)} %bitcast_add_fusion.1), channel_id=10, replica_groups=mesh['z'=16,'yhi'=2,'core'=2,'x'=4,'ylo'=2] {'core'}, dimensions={0}, use_global_device_ids=true | all-gather | bytes 393216 | tf_op jit(solution)/shard_map/all_gather | solution.py:291
  49.0 1.0 %shard_map.95 = (f32[64,512]{1,0:T(8,128)S(1)}, f32[64,512]{1,0:T(8,128)S(1)}) custom-call(f32[2,64,512]{2,1,0:T(8,128)S(1)} %bitcast.39, bf16[4,512,512]{2,1,0:T(8,128)(2,1)S(1)} %get-tuple-element.27.refs_1_, bf16[512,512]{1,0:T(8,128)(2,1)S(1)} %get-tuple-element.33.refs_2_, f32[8,512]{1,0:T(8,128)S(1)} %get-tuple-element.28.refs_3_, ...), custom_call_target="tpu_custom_call" | custom-call | tf_op jit(solution)/shard_map/pallas_call | solution.py:272
  50.0 2.0 %all-gather.9 = f32[128,512]{1,0:T(8,128)S(1)} all-gather(f32[64,512]{1,0:T(8,128)S(1)} %get-tuple-element.42), channel_id=11, replica_groups={{9,16},{8,0},{11,18},{10,2},{13,20},{12,4},{15,22},{14,6},{24,33},{25,1..., dimensions={0}, use_global_device_ids=true | all-gather | bytes 393216 | tf_op jit(solution)/shard_map/all_gather | solution.py:289
  52.0 2.0 %all-gather.10 = f32[128,512]{1,0:T(8,128)S(1)} all-gather(f32[64,512]{1,0:T(8,128)S(1)} %bitcast_add_fusion), channel_id=12, replica_groups=mesh['z'=16,'yhi'=2,'core'=2,'x'=4,'ylo'=2] {'core'}, dimensions={0}, use_global_device_ids=true | all-gather | bytes 393216 | tf_op jit(solution)/shard_map/all_gather | solution.py:291
  54.0 1.0 %shard_map.96 = (f32[64,512]{1,0:T(8,128)S(1)}, f32[64,512]{1,0:T(8,128)S(1)}) custom-call(f32[2,64,512]{2,1,0:T(8,128)S(1)} %bitcast.35, bf16[4,512,512]{2,1,0:T(8,128)(2,1)S(1)} %get-tuple-element.27.refs_1_, bf16[512,512]{1,0:T(8,128)(2,1)S(1)} %get-tuple-element.33.refs_2_, f32[8,512]{1,0:T(8,128)S(1)} %get-tuple-element.28.refs_3_, ...), custom_call_target="tpu_custom_call" | custom-call | tf_op jit(solution)/shard_map/pallas_call | solution.py:272
  55.0 1.9 %all_gather.99 = f32[2,16,512]{2,1,0:T(8,128)S(1)} all-gather(f32[1,16,512]{2,1,0:T(8,128)S(1)} %dynamic-slice_bitcast_fusion), channel_id=1, replica_groups={{9,16},{8,0},{11,18},{10,2},{13,20},{12,4},{15,22},{14,6},{24,33},{25,1..., dimensions={0}, use_global_device_ids=true | all-gather | bytes 98304 | tf_op jit(solution)/shard_map/all_gather | solution.py:289
  56.8 1.8 %all_gather.100 = f32[2,16,512]{2,1,0:T(8,128)S(1)} all-gather(f32[1,16,512]{2,1,0:T(8,128)S(1)} %bitcast_add_fusion.5), channel_id=1, replica_groups=mesh['z'=16,'yhi'=2,'core'=2,'x'=4,'ylo'=2] {'core'}, dimensions={0}, use_global_device_ids=true | all-gather | bytes 98304 | tf_op jit(solution)/shard_map/all_gather | solution.py:291
  58.8 35.7 %all_gather.101 = f32[2,4,512]{2,1,0:T(4,128)S(1)} all-gather(f32[1,4,512]{2,1,0:T(4,128)S(1)} %constant_dynamic-slice_fusion), channel_id=1, replica_groups=mesh['z'=16,'yhi'=2,'core'=2,'x'=4,'ylo'=2] {'ylo'}, dimensions={0}, use_global_device_ids=true | all-gather | bytes 24576 | tf_op jit(solution)/shard_map/all_gather | solution.py:297
  94.4 0.6 select_bitcast_fusion
  (12 shorter events, 0.1 us)
Async XLA Ops:
  0.0 17.6 %copy-start.4 = (s32[1,5]{1,0:T(1,128)S(1)}, s32[1,5]{1,0:T(1,128)}, u32[]{:S(2)}) copy-start(s32[1,5]{1,0:T(1,128)} %offsets_hbm.1) | copy-start | bytes 64
  0.0 17.5 %copy-start.1 = (f32[32,32]{1,0:T(8,128)S(1)}, f32[32,32]{1,0:T(8,128)}, u32[]{:S(2)}) copy-start(f32[32,32]{1,0:T(8,128)} %uptake_weight.1) | copy-start | bytes 12292
  0.0 17.6 %copy-start.3 = (f32[32,32]{1,0:T(8,128)S(1)}, f32[32,32]{1,0:T(8,128)}, u32[]{:S(2)}) copy-start(f32[32,32]{1,0:T(8,128)} %param.17) | copy-start | bytes 12292
  0.0 17.7 %copy-start = (f32[16,32,32]{2,1,0:T(8,128)S(1)}, f32[16,32,32]{2,1,0:T(8,128)}, u32[]{:S(2)}) copy-start(f32[16,32,32]{2,1,0:T(8,128)} %inverse.1) | copy-start | bytes 196612
  0.0 17.7 %copy-start.2 = (s32[16]{0:T(128)S(1)}, s32[16]{0:T(128)}, u32[]{:S(2)}) copy-start(s32[16]{0:T(128)} %wet.1) | copy-start | bytes 196
  3.0 25.5 %collective-permute-start = (f32[512,512]{1,0:T(8,128)}, f32[512,512]{1,0:T(8,128)}, u32[]{:S(2)}, u32[]{:S(2)}) collective-permute-start(f32[512,512]{1,0:T(8,128)} %lend.1), channel_id=1, source_target_pairs={{0,8},{8,0},{1,9},{9,1},{2,10},{10,2},{3,11},{11,3},{4,12},{12,4},... | collective-permute-start | bytes 3145736 | tf_op jit(solution)/shard_map/ppermute | solution.py:239
  13.3 12.3 %all-to-all-start = ((f32[8,7,4,512]{3,2,1,0:T(4,128)}), f32[8,7,4,512]{3,2,1,0:T(4,128)S(1)}, u32[]{:S(2)}, u32[]{:S(2)}) async-start(f32[8,7,4,512]{3,2,1,0:T(4,128)} %pack.1), calls=%async_computation | async-start | bytes 917504 | tf_op jit(solution)/shard_map/all_to_all | solution.py:228
